TPU v7x, 32 devices: a whole 2x2x4 slice. The times are simulated.
32 devices in a mesh: groups: 2 (over y), rows: 4 (over z), cols: 2 (over core), futures: 2 (over x).
Axes of the slice: x: 2, y: 2, z: 4, core: 2. Of those that a mesh axis runs over, the one named last changes fastest.
Arguments:
- features: bfloat16 [256, 64, 256], P('futures', ('groups', 'rows'), 'cols'), parts along dimension 1, may hold values from -6 to 6
- trunk_weights: bfloat16 [2, 9, 256, 256], P(None, None, 'futures'), may hold values from -0.125 to 0.125
- head_weights: bfloat16 [8, 3, 256], replicated, may hold values from -0.375 to 0.375
- flow_target: float32 [2, 64, 256], P(None, ('groups', 'rows'), 'cols'), parts along dimension 1, may hold values from -6 to 6
- labels: int32 [64, 256], P(('groups', 'rows'), 'cols'), parts along dimension 0, may hold values 0 or 1
- winner: int32 [8, 32], P(('groups', 'rows'), 'cols'), parts along dimension 0, may hold values from 0 to 7
Outputs:
- loss: float32 [2], P('groups'), parts along dimension 0
- trunk_grad: float32 [4, 9, 256, 256], P('groups', None, 'futures'), parts along dimension 0
- head_grad: float32 [8, 6, 256], P('futures', 'groups'), parts along dimension 1
There are 2 independent parts, one for each index of `groups`. A program takes and returns all parts, laid end to end along the dimension named above; an argument that names none is the same for every part. Nothing has to cross between parts.
Inputs may be any that keep to these rules, and one draw needn't show every extreme that they name: `winner`: the winning future of each block of 8 x 8 cells.
All inputs are finite; a program needn't handle non-finite values. No bound on the sum of `labels` on one device may be relied on, other than what follows from the above.
Results may differ from a plain program's by a relative error of at most 0.0045.
Values may be sent and summed in bfloat16 or wider, within the bound.
No kernel may reach another device: no remote copies, remote signals or barrier semaphores. Data moves between devices by JAX's collectives and lax.ppermute only.
A program may use at most 64 MiB of HBM per device.

v0:
```python
import math

import jax
import jax.numpy as jnp
from jax import lax
from jax.sharding import PartitionSpec as P

BLK = 8


def extended(block, sides, width):
    for axis, dim in sides:
        count = lax.axis_size(axis)
        forward = [(i, i + 1) for i in range(count - 1)]
        backward = [(target, source) for source, target in forward]
        low = lax.ppermute(
            lax.slice_in_dim(block, block.shape[dim] - width, None, axis=dim), axis, forward
        )
        high = lax.ppermute(lax.slice_in_dim(block, 0, width, axis=dim), axis, backward)
        block = jnp.concatenate([low, block, high], axis=dim)
    return block


def column_views(padded, width):
    views = []
    for col_off in range(3):
        shifted = padded[:, :, col_off : col_off + width]
        views.append(shifted.reshape(padded.shape[0], padded.shape[1] * width))
    return views


def conv_forward(padded, taps, height, width):
    views = column_views(padded, width)
    total = jnp.zeros((taps.shape[1], height * width), jnp.float32)
    for col_off in range(3):
        for row_off in range(3):
            window = lax.slice_in_dim(
                views[col_off], row_off * width, (row_off + height) * width, axis=1
            )
            total = total + jnp.dot(
                taps[3 * row_off + col_off], window, preferred_element_type=jnp.float32
            )
    return total.reshape(taps.shape[1], height, width)


def conv_backward(padded_grad, taps, height, width):
    views = column_views(padded_grad, width)
    total = jnp.zeros((taps.shape[2], height * width), jnp.float32)
    for col_off in range(3):
        for row_off in range(3):
            window = lax.slice_in_dim(
                views[col_off], row_off * width, (row_off + height) * width, axis=1
            )
            offset = 3 * (2 - row_off) + (2 - col_off)
            total = total + lax.dot_general(
                taps[offset], window, (((0,), (0,)), ((), ())), preferred_element_type=jnp.float32
            )
    return total.reshape(taps.shape[2], height, width)


def weight_grad(grad, padded, height, width):
    flat = grad.reshape(grad.shape[0], height * width)
    views = column_views(padded, width)
    pieces = [None] * 9
    for col_off in range(3):
        for row_off in range(3):
            window = lax.slice_in_dim(
                views[col_off], row_off * width, (row_off + height) * width, axis=1
            )
            pieces[3 * row_off + col_off] = lax.dot_general(
                flat, window, (((1,), (1,)), ((), ())), preferred_element_type=jnp.float32
            )
    return jnp.stack(pieces)


def silu_slope(pre):
    sigma = jax.nn.sigmoid(pre)
    return sigma * (1.0 + pre * (1.0 - sigma))


def losses_and_grads(heads, labels, flow_target, mask, scale):
    logit = heads[:, 0]
    target = labels.astype(jnp.float32)[None]
    first = heads[:, 1] - flow_target[0][None]
    second = heads[:, 2] - flow_target[1][None]
    cell = jax.nn.softplus(logit) - target * logit + 0.5 * (first * first + second * second)
    total = jnp.sum(mask * cell)
    d_logit = mask * (jax.nn.sigmoid(logit) - target) * scale
    d_first = mask * first * scale
    d_second = mask * second * scale
    grads = jnp.stack([d_logit, d_first, d_second], axis=1).astype(jnp.bfloat16)
    return (total, grads)


def local(features, trunk_weights, head_weights, flow_target, labels, winner):
    chan_here = features.shape[0]
    rows_here = features.shape[1]
    cols_here = features.shape[2]
    channels = trunk_weights.shape[3]
    layer_count = trunk_weights.shape[0]
    fut_total = head_weights.shape[0]
    fut_here = fut_total // lax.axis_size("futures")
    fut_index = lax.axis_index("futures")
    cell_count = rows_here * cols_here * lax.axis_size("rows") * lax.axis_size("cols")
    scale = 1.0 / math.sqrt(cell_count)
    active = features
    saved_pads = []
    saved_pre = []
    for layer in range(layer_count):
        whole = lax.all_gather(active, "futures", axis=0, tiled=True)
        padded = extended(whole, (("rows", 1), ("cols", 2)), 1)
        pre = conv_forward(padded, trunk_weights[layer], rows_here, cols_here)
        active = jax.nn.silu(pre).astype(jnp.bfloat16)
        saved_pads.append(padded)
        saved_pre.append(pre)
    whole_out = lax.all_gather(active, "futures", axis=0, tiled=True)
    flat_out = whole_out.reshape(channels, rows_here * cols_here)
    mine = lax.dynamic_slice_in_dim(head_weights, fut_index * fut_here, fut_here, 0)
    heads = jnp.dot(
        mine.reshape(fut_here * 3, channels), flat_out, preferred_element_type=jnp.float32
    ).reshape(fut_here, 3, rows_here, cols_here)
    block_ids = jnp.repeat(jnp.repeat(winner, BLK, axis=0), BLK, axis=1)
    owned = fut_index * fut_here + jnp.arange(fut_here, dtype=jnp.int32)
    mask = (block_ids[None] == owned[:, None, None]).astype(jnp.float32)
    total, head_grads = losses_and_grads(heads, labels, flow_target, mask, scale)
    loss_sum = lax.psum(total, ("rows", "cols", "futures"))
    flat_grads = head_grads.reshape(fut_here * 3, rows_here * cols_here)
    head_local = lax.dot_general(
        flat_grads, flat_out, (((1,), (1,)), ((), ())), preferred_element_type=jnp.float32
    )
    all_heads = lax.all_gather(head_grads, "futures", axis=0, tiled=True)
    columns = lax.dynamic_slice_in_dim(head_weights, fut_index * chan_here, chan_here, 2)
    upstream = lax.dot_general(
        columns.reshape(fut_total * 3, chan_here),
        all_heads.reshape(fut_total * 3, rows_here * cols_here),
        (((0,), (0,)), ((), ())),
        preferred_element_type=jnp.float32,
    ).reshape(chan_here, rows_here, cols_here)
    trunk_parts = [None] * layer_count
    for layer in reversed(range(layer_count)):
        slope_grad = (upstream * silu_slope(saved_pre[layer])).astype(jnp.bfloat16)
        trunk_parts[layer] = weight_grad(slope_grad, saved_pads[layer], rows_here, cols_here)
        if layer > 0:
            grad_pad = extended(slope_grad, (("rows", 1), ("cols", 2)), 1)
            kernel = trunk_weights[layer]
            upstream = lax.psum_scatter(
                conv_backward(grad_pad, kernel, rows_here, cols_here),
                "futures",
                scatter_dimension=0,
                tiled=True,
            )
    stacked = jnp.stack(trunk_parts)
    trunk_grad, head_sum = lax.psum((stacked, head_local), ("rows", "cols"))
    loss = (loss_sum / cell_count).reshape(1)
    return (loss, trunk_grad, head_sum.reshape(fut_here, 3, channels))


def solution(mesh):
    placed = (
        P("futures", ("groups", "rows"), "cols"),
        P(None, None, "futures", None),
        P(),
        P(None, ("groups", "rows"), "cols"),
        P(("groups", "rows"), "cols"),
        P(("groups", "rows"), "cols"),
    )
    return jax.shard_map(
        local,
        mesh=mesh,
        in_specs=placed,
        out_specs=(P("groups"), P("groups", None, "futures", None), P("futures", "groups", None)),
        check_vma=False,
    )
```

profile of v0, /device:TPU:0, one launch (start us, length us, event | category | flops | bytes accessed | tf_op | source)
XLA Modules:
  0.0 198.5 jit_solution(13538310453566543887)
XLA Ops:
  7.3 1.2 copy.17
  8.4 10.1 %all_gather.12 = bf16[256,8,128]{0,2,1:T(8,128)(2,1)S(1)} all-gather(bf16[128,8,128]{0,2,1:T(8,128)(2,1)S(1)} %copy.17), channel_id=1, replica_groups=mesh['groups'=2,'rows'=4,'cols'=2,'futures'=2] {'futures'}, dimensions={0}, use_global_device_ids=true | all-gather | bytes 786432 | tf_op jit(solution)/shard_map/all_gather | solution.py:110
  18.5 1.3 collective-permute-start.1
  19.8 4.5 %collective-permute-start = (bf16[256,1,128]{0,2,1:T(8,128)(2,1)S(1)}, bf16[256,1,128]{0,2,1:T(8,128)(2,1)S(1)}, u32[]{:S(2)}, u32[]{:S(2)}) collective-permute-start(bf16[256,1,128]{0,2,1:T(8,128)(2,1)S(1)} %get-tuple-element.20), channel_id=1, source_target_pairs={{0,4},{4,8},{8,12},{1,5},{5,9},{9,13},{2,6},{6,10},{10,14},{3,7},{... | collective-permute-start | bytes 196616 | tf_op jit(solution)/shard_map/ppermute | solution.py:16
  24.5 0.6 reshape.153
  25.3 1.0 collective-permute-done
  26.4 1.3 collective-permute-start.2
  27.7 1.3 collective-permute-start.3
  29.3 0.3 fusion.60
  29.6 1.2 collective-permute-done.3
  30.7 0.4 pad_maximum_fusion.4
  31.4 0.3 fusion.67
  31.7 0.3 convolution_add_fusion.17
  32.0 0.3 convolution_add_fusion.16
  32.3 0.4 fusion.5
  32.7 0.3 convolution_add_fusion.14
  33.0 0.3 convolution_add_fusion.13
  33.5 9.2 %all_gather.13 = bf16[256,8,128]{0,2,1:T(8,128)(2,1)S(1)} all-gather(bf16[128,8,128]{0,2,1:T(8,128)(2,1)S(1)} %multiply_convert_fusion.2), channel_id=1, replica_groups=mesh['groups'=2,'rows'=4,'cols'=2,'futures'=2] {'futures'}, dimensions={0}, use_global_device_ids=true | all-gather | bytes 786432 | tf_op jit(solution)/shard_map/all_gather | solution.py:110
  42.7 4.3 %collective-permute-start.4 = (bf16[256,1,128]{0,2,1:T(8,128)(2,1)S(1)}, bf16[256,1,128]{0,2,1:T(8,128)(2,1)S(1)}, u32[]{:S(2)}, u32[]{:S(2)}) collective-permute-start(bf16[256,1,128]{0,2,1:T(8,128)(2,1)S(1)} %get-tuple-element.18), channel_id=1, source_target_pairs={{0,4},{4,8},{8,12},{1,5},{5,9},{9,13},{2,6},{6,10},{10,14},{3,7},{... | collective-permute-start | bytes 196616 | tf_op jit(solution)/shard_map/ppermute | solution.py:16
  47.0 1.3 collective-permute-start.5
  48.3 0.6 collective-permute-done.4
  48.9 4.2 %collective-permute-done.5 = bf16[256,1,128]{0,2,1:T(8,128)(2,1)S(1)} collective-permute-done((bf16[256,1,128]{0,2,1:T(8,128)(2,1)S(1)}, bf16[256,1,128]{0,2,1:T(8,128)(2,1)S(1)}, u32[]{:S(2)}, u32[]{:S(2)}) %collective-permute-start.5) | collective-permute-done | bytes 65568 | tf_op jit(solution)/shard_map/ppermute | solution.py:19
  53.2 1.3 collective-permute-start.6
  54.5 1.3 collective-permute-start.7
  56.1 0.3 fusion.38
  56.4 1.2 collective-permute-done.7
  57.5 0.4 pad_maximum_fusion.2
  57.9 0.3 fusion.32
  58.2 0.3 fusion.45
  58.5 0.3 convolution_add_fusion.12
  58.8 0.3 convolution_add_fusion.11
  59.1 0.4 fusion.2
  59.5 0.3 convolution_add_fusion.9
  59.8 0.3 convolution_add_fusion.8
  60.2 9.1 %all_gather.14 = bf16[256,8,128]{0,2,1:T(8,128)(2,1)S(1)} all-gather(bf16[128,8,128]{0,2,1:T(8,128)(2,1)S(1)} %multiply_convert_fusion.1), channel_id=1, replica_groups=mesh['groups'=2,'rows'=4,'cols'=2,'futures'=2] {'futures'}, dimensions={0}, use_global_device_ids=true | all-gather | bytes 786432 | tf_op jit(solution)/shard_map/all_gather | solution.py:116
  69.8 4.5 %all_gather.15 = bf16[8,3,8,128]{3,2,1,0:T(8,128)(2,1)S(1)} all-gather(bf16[4,3,8,128]{3,2,1,0:T(8,128)(2,1)S(1)} %copy.19), channel_id=1, replica_groups=mesh['groups'=2,'rows'=4,'cols'=2,'futures'=2] {'futures'}, dimensions={0}, use_global_device_ids=true | all-gather | bytes 73728 | tf_op jit(solution)/shard_map/all_gather | solution.py:131
  74.3 0.3 fusion.6
  74.7 3.7 %collective-permute-start.8 = (bf16[128,1,128]{0,2,1:T(8,128)(2,1)S(1)}, bf16[128,1,128]{0,2,1:T(8,128)(2,1)S(1)}, u32[]{:S(2)}, u32[]{:S(2)}) collective-permute-start(bf16[128,1,128]{0,2,1:T(8,128)(2,1)S(1)} %get-tuple-element.25), channel_id=1, source_target_pairs={{0,4},{4,8},{8,12},{1,5},{5,9},{9,13},{2,6},{6,10},{10,14},{3,7},{... | collective-permute-start | bytes 98312 | tf_op jit(solution)/shard_map/ppermute | solution.py:16
  78.4 1.3 collective-permute-start.9
  79.9 4.2 %collective-permute-done.9 = bf16[128,1,128]{0,2,1:T(8,128)(2,1)S(1)} collective-permute-done((bf16[128,1,128]{0,2,1:T(8,128)(2,1)S(1)}, bf16[128,1,128]{0,2,1:T(8,128)(2,1)S(1)}, u32[]{:S(2)}, u32[]{:S(2)}) %collective-permute-start.9) | collective-permute-done | bytes 32800 | tf_op jit(solution)/shard_map/ppermute | solution.py:19
  84.2 1.3 collective-permute-start.11
  85.5 3.0 %collective-permute-start.10 = (bf16[128,10,1]{0,2,1:T(2,128)(2,1)S(1)}, bf16[128,10,1]{0,2,1:T(2,128)(2,1)S(1)}, u32[]{:S(2)}, u32[]{:S(2)}) collective-permute-start(bf16[128,10,1]{0,2,1:T(2,128)(2,1)S(1)} %get-tuple-element.24), channel_id=1, source_target_pairs={{0,2},{1,3},{4,6},{5,7},{8,10},{9,11},{12,14},{13,15},{16,18},{17,... | collective-permute-start | bytes 7688 | tf_op jit(solution)/shard_map/ppermute | solution.py:16
  88.6 0.8 collective-permute-done.10
  89.9 0.3 convolution_add_fusion.7
  91.9 1.2 convolution_add_fusion
  93.2 2.0 %fusion.15 = f32[9,128,256]{2,1,0:T(8,128)} fusion(bf16[128,1024]{0,1:T(8,128)(2,1)S(1)} %bitcast.266, bf16[256,1280]{0,1:T(8,128)(2,1)} %bitcast.317), kind=kOutput, calls=%fused_computation.44 | convolution fusion | flops 67108864 | bytes 917504 | tf_op jit(solution)/shard_map/dot_general | solution.py:70
  95.2 0.9 fusion.14
  96.1 0.9 fusion.13
  97.1 0.9 fusion.12
  98.0 0.9 fusion.11
  98.9 0.9 fusion.10
  99.9 0.9 fusion.9
  100.8 0.9 fusion.8
  101.7 0.9 fusion.7
  102.6 10.2 %reduce-scatter.2.cloned.1.call-done = f32[128,8,128]{0,2,1:T(8,128)} async-done(((f32[256,8,128]{0,2,1:T(8,128)}), f32[128,8,128]{0,2,1:T(8,128)}) %reduce-scatter.2.cloned.1.call-update) | async-done | bytes 524304 | tf_op jit(solution)/shard_map/reduce_scatter | solution.py:146
  112.9 1.4 multiply_convert_fusion
  116.9 3.0 %pad_maximum_fusion = f32[2,9,128,256]{3,2,1,0:T(8,128)} fusion(f32[1,9,128,256]{3,2,1,0:T(8,128)} %bitcast.70, f32[1,9,128,256]{3,2,1,0:T(8,128)S(1)} %bitcast.335), kind=kLoop, calls=%fused_computation | loop fusion | flops 589824 | bytes 4718592 | tf_op jit(solution)/shard_map/stack | solution.py:152
  119.9 0.7 copy-done.9
  120.6 0.7 fusion.154
  121.3 33.5 %psum.21 = f32[]{:T(128)} all-reduce(f32[]{:T(128)} %fusion.154), channel_id=1, replica_groups=mesh['groups'=2,'rows'=4,'cols'=2,'futures'=2] {'rows','cols','futures'}, use_global_device_ids=true, to_apply=%region_1.2 | all-reduce | flops 1 | bytes 8 | tf_op jit(solution)/shard_map/psum | solution.py:126
  155.1 26.6 %psum.23 = f32[4,3,256]{2,1,0:T(4,128)S(1)} all-reduce(f32[4,3,256]{2,1,0:T(4,128)S(1)} %reshape.150), channel_id=1, replica_groups=mesh['groups'=2,'rows'=4,'cols'=2,'futures'=2] {'rows','cols'}, use_global_device_ids=true, to_apply=%region_4.5 | all-reduce | flops 3072 | bytes 24576 | tf_op jit(solution)/shard_map/psum | solution.py:153
  181.7 0.6 copy.22
  183.0 4.3 %all-reduce.2.cloned.1.call-done = f32[2,9,128,256]{3,2,1,0:T(8,128)} async-done(((f32[2,9,128,256]{3,2,1,0:T(8,128)}), f32[2,9,128,256]{3,2,1,0:T(8,128)}) %all-reduce.2.cloned.1.call-update) | async-done | bytes 2359312 | tf_op jit(solution)/shard_map/psum | solution.py:153
  187.3 3.3 %copy.55 = f32[2,9,128,256]{3,2,1,0:T(8,128)} copy(f32[2,9,128,256]{3,2,1,0:T(8,128)} %all-reduce.2.cloned.1.call-done) | data formatting | bytes 4718592
  (106 shorter events, 7.3 us)
Async XLA Ops:
  7.2 17.3 %copy-start = (bf16[8,3,256]{2,0,1:T(8,128)(2,1)S(1)}, bf16[8,3,256]{2,0,1:T(8,128)(2,1)}, u32[]{:S(2)}) copy-start(bf16[8,3,256]{2,0,1:T(8,128)(2,1)} %param.8) | copy-start | bytes 36868
  7.2 17.2 %copy-start.20 = (s32[8,128]{1,0:T(8,128)S(1)}, s32[8,128]{1,0:T(8,128)}, u32[]{:S(2)}) copy-start(s32[8,128]{1,0:T(8,128)} %param.10) | copy-start | bytes 12292
  7.2 17.2 %copy-start.16 = (f32[2,8,128]{2,1,0:T(8,128)S(1)}, f32[2,8,128]{2,1,0:T(8,128)}, u32[]{:S(2)}) copy-start(f32[2,8,128]{2,1,0:T(8,128)} %param.9) | copy-start | bytes 24580
  7.2 17.9 %copy-start.23 = (s32[1,16]{1,0:T(1,128)S(1)}, s32[1,16]{1,0:T(1,128)}, u32[]{:S(2)}) copy-start(s32[1,16]{1,0:T(1,128)} %param.11) | copy-start | bytes 196
  7.2 105.7 %reduce-scatter.2.cloned.1.call-start = ((), (), s32[]{:S(2)}) async-start(), calls=%async_computation.1 | async-start | bytes 1572864 | tf_op jit(solution)/shard_map/reduce_scatter | solution.py:146
  8.4 20.6 %copy-start.6 = (bf16[2,9,128,256]{3,2,1,0:T(8,128)(2,1)S(1)}, bf16[2,9,128,256]{3,2,1,0:T(8,128)(2,1)}, u32[]{:S(2)}) copy-start(bf16[2,9,128,256]{3,2,1,0:T(8,128)(2,1)} %param.7) | copy-start | bytes 3538948
  18.5 7.8 %collective-permute-start.1 = (bf16[256,1,128]{0,2,1:T(8,128)(2,1)S(1)}, bf16[256,1,128]{0,2,1:T(8,128)(2,1)S(1)}, u32[]{:S(2)}, u32[]{:S(2)}) collective-permute-start(bf16[256,1,128]{0,2,1:T(8,128)(2,1)S(1)} %get-tuple-element.19), channel_id=1, source_target_pairs={{4,0},{8,4},{12,8},{5,1},{9,5},{13,9},{6,2},{10,6},{14,10},{7,3},{... | collective-permute-start | bytes 196616 | tf_op jit(solution)/shard_map/ppermute | solution.py:19
  19.8 6.4 %collective-permute-start = (bf16[256,1,128]{0,2,1:T(8,128)(2,1)S(1)}, bf16[256,1,128]{0,2,1:T(8,128)(2,1)S(1)}, u32[]{:S(2)}, u32[]{:S(2)}) collective-permute-start(bf16[256,1,128]{0,2,1:T(8,128)(2,1)S(1)} %get-tuple-element.20), channel_id=1, source_target_pairs={{0,4},{4,8},{8,12},{1,5},{5,9},{9,13},{2,6},{6,10},{10,14},{3,7},{... | collective-permute-start | bytes 196616 | tf_op jit(solution)/shard_map/ppermute | solution.py:16
  24.4 45.1 %copy-start.12 = (f32[8,128]{1,0:T(8,128)}, f32[8,128]{1,0:T(8,128)S(1)}, u32[]{:S(2)}) copy-start(f32[8,128]{1,0:T(8,128)S(1)} %get-tuple-element.30) | copy-start | bytes 12292
  24.4 45.1 %copy-start.14 = (f32[8,128]{1,0:T(8,128)}, f32[8,128]{1,0:T(8,128)S(1)}, u32[]{:S(2)}) copy-start(f32[8,128]{1,0:T(8,128)S(1)} %get-tuple-element.31) | copy-start | bytes 12292
  25.3 44.3 %copy-start.18 = (s32[128]{0:T(128)}, s32[128]{0:T(128)S(1)}, u32[]{:S(2)}) copy-start(s32[128]{0:T(128)S(1)} %broadcast_in_dim.9) | copy-start | bytes 1540
  26.4 3.2 %collective-permute-start.2 = (bf16[256,10,1]{0,2,1:T(2,128)(2,1)S(1)}, bf16[256,10,1]{0,2,1:T(2,128)(2,1)S(1)}, u32[]{:S(2)}, u32[]{:S(2)}) collective-permute-start(bf16[256,10,1]{0,2,1:T(2,128)(2,1)S(1)} %get-tuple-element.15), channel_id=1, source_target_pairs={{0,2},{1,3},{4,6},{5,7},{8,10},{9,11},{12,14},{13,15},{16,18},{17,... | collective-permute-start | bytes 15368 | tf_op jit(solution)/shard_map/ppermute | solution.py:16
  27.7 3.1 %collective-permute-start.3 = (bf16[256,10,1]{0,2,1:T(2,128)(2,1)S(1)}, bf16[256,10,1]{0,2,1:T(2,128)(2,1)S(1)}, u32[]{:S(2)}, u32[]{:S(2)}) collective-permute-start(bf16[256,10,1]{0,2,1:T(2,128)(2,1)S(1)} %get-tuple-element.16), channel_id=1, source_target_pairs={{2,0},{3,1},{6,4},{7,5},{10,8},{11,9},{14,12},{15,13},{18,16},{19,... | collective-permute-start | bytes 15368 | tf_op jit(solution)/shard_map/ppermute | solution.py:19
  33.3 15.6 %copy-start.3 = (f32[1024,128]{1,0:T(8,128)}, f32[1024,128]{1,0:T(8,128)S(1)}, u32[]{:S(2)}) copy-start(f32[1024,128]{1,0:T(8,128)S(1)} %convolution_add_fusion.13) | copy-start | bytes 1572868
  33.4 22.3 %copy-start.7 = (bf16[2,9,128,256]{3,2,1,0:T(8,128)(2,1)S(1)}, bf16[2,9,128,256]{3,2,1,0:T(8,128)(2,1)}, u32[]{:S(2)}) copy-start(bf16[2,9,128,256]{3,2,1,0:T(8,128)(2,1)} %param.7) | copy-start | bytes 3538948
  42.7 6.2 %collective-permute-start.4 = (bf16[256,1,128]{0,2,1:T(8,128)(2,1)S(1)}, bf16[256,1,128]{0,2,1:T(8,128)(2,1)S(1)}, u32[]{:S(2)}, u32[]{:S(2)}) collective-permute-start(bf16[256,1,128]{0,2,1:T(8,128)(2,1)S(1)} %get-tuple-element.18), channel_id=1, source_target_pairs={{0,4},{4,8},{8,12},{1,5},{5,9},{9,13},{2,6},{6,10},{10,14},{3,7},{... | collective-permute-start | bytes 196616 | tf_op jit(solution)/shard_map/ppermute | solution.py:16
  47.0 22.7 %copy-start.21 = (s32[4]{0:T(128)}, s32[4]{0:T(128)S(1)}, u32[]{:S(2)}) copy-start(s32[4]{0:T(128)S(1)} %iota_add_fusion) | copy-start | bytes 52
  47.0 6.2 %collective-permute-start.5 = (bf16[256,1,128]{0,2,1:T(8,128)(2,1)S(1)}, bf16[256,1,128]{0,2,1:T(8,128)(2,1)S(1)}, u32[]{:S(2)}, u32[]{:S(2)}) collective-permute-start(bf16[256,1,128]{0,2,1:T(8,128)(2,1)S(1)} %get-tuple-element.17), channel_id=1, source_target_pairs={{4,0},{8,4},{12,8},{5,1},{9,5},{13,9},{6,2},{10,6},{14,10},{7,3},{... | collective-permute-start | bytes 196616 | tf_op jit(solution)/shard_map/ppermute | solution.py:19
  53.2 3.2 %collective-permute-start.6 = (bf16[256,10,1]{0,2,1:T(2,128)(2,1)S(1)}, bf16[256,10,1]{0,2,1:T(2,128)(2,1)S(1)}, u32[]{:S(2)}, u32[]{:S(2)}) collective-permute-start(bf16[256,10,1]{0,2,1:T(2,128)(2,1)S(1)} %get-tuple-element.11), channel_id=1, source_target_pairs={{0,2},{1,3},{4,6},{5,7},{8,10},{9,11},{12,14},{13,15},{16,18},{17,... | collective-permute-start | bytes 15368 | tf_op jit(solution)/shard_map/ppermute | solution.py:16
  54.5 3.1 %collective-permute-start.7 = (bf16[256,10,1]{0,2,1:T(2,128)(2,1)S(1)}, bf16[256,10,1]{0,2,1:T(2,128)(2,1)S(1)}, u32[]{:S(2)}, u32[]{:S(2)}) collective-permute-start(bf16[256,10,1]{0,2,1:T(2,128)(2,1)S(1)} %get-tuple-element.12), channel_id=1, source_target_pairs={{2,0},{3,1},{6,4},{7,5},{10,8},{11,9},{14,12},{15,13},{18,16},{19,... | collective-permute-start | bytes 15368 | tf_op jit(solution)/shard_map/ppermute | solution.py:19
  57.9 0.9 copy-start.1
  60.1 14.2 %copy-start.17 = (bf16[24,128,1]{1,0,2:T(8,128)(2,1)S(1)}, bf16[24,128,1]{1,0,2:T(8,128)(2,1)}, u32[]{:S(2)}) copy-start(bf16[24,128,1]{1,0,2:T(8,128)(2,1)} %reshape.153) | copy-start | bytes 18436
  69.3 5.3 %copy-start.4 = (bf16[256,8,128]{0,2,1:T(8,128)(2,1)}, bf16[256,8,128]{0,2,1:T(8,128)(2,1)S(1)}, u32[]{:S(2)}) copy-start(bf16[256,8,128]{0,2,1:T(8,128)(2,1)S(1)} %all_gather.14) | copy-start | bytes 1572868
  69.6 5.1 %copy-start.8 = (f32[4,3,8,128]{3,0,2,1:T(4,128)}, f32[4,3,8,128]{3,0,2,1:T(4,128)S(1)}, u32[]{:S(2)}) copy-start(f32[4,3,8,128]{3,0,2,1:T(4,128)S(1)} %fusion.25) | copy-start | bytes 147460
  69.8 4.9 %copy-start.10 = (bf16[4,3,8,128]{3,2,1,0:T(8,128)(2,1)}, bf16[4,3,8,128]{3,2,1,0:T(8,128)(2,1)S(1)}, u32[]{:S(2)}) copy-start(bf16[4,3,8,128]{3,2,1,0:T(8,128)(2,1)S(1)} %copy.19) | copy-start | bytes 73732
  74.7 5.3 %collective-permute-start.8 = (bf16[128,1,128]{0,2,1:T(8,128)(2,1)S(1)}, bf16[128,1,128]{0,2,1:T(8,128)(2,1)S(1)}, u32[]{:S(2)}, u32[]{:S(2)}) collective-permute-start(bf16[128,1,128]{0,2,1:T(8,128)(2,1)S(1)} %get-tuple-element.25), channel_id=1, source_target_pairs={{0,4},{4,8},{8,12},{1,5},{5,9},{9,13},{2,6},{6,10},{10,14},{3,7},{... | collective-permute-start | bytes 98312 | tf_op jit(solution)/shard_map/ppermute | solution.py:16
  78.4 5.8 %collective-permute-start.9 = (bf16[128,1,128]{0,2,1:T(8,128)(2,1)S(1)}, bf16[128,1,128]{0,2,1:T(8,128)(2,1)S(1)}, u32[]{:S(2)}, u32[]{:S(2)}) collective-permute-start(bf16[128,1,128]{0,2,1:T(8,128)(2,1)S(1)} %get-tuple-element.26), channel_id=1, source_target_pairs={{4,0},{8,4},{12,8},{5,1},{9,5},{13,9},{6,2},{10,6},{14,10},{7,3},{... | collective-permute-start | bytes 98312 | tf_op jit(solution)/shard_map/ppermute | solution.py:19
  84.2 4.3 %collective-permute-start.11 = (bf16[128,10,1]{0,2,1:T(2,128)(2,1)S(1)}, bf16[128,10,1]{0,2,1:T(2,128)(2,1)S(1)}, u32[]{:S(2)}, u32[]{:S(2)}) collective-permute-start(bf16[128,10,1]{0,2,1:T(2,128)(2,1)S(1)} %get-tuple-element.23), channel_id=1, source_target_pairs={{2,0},{3,1},{6,4},{7,5},{10,8},{11,9},{14,12},{15,13},{18,16},{19,... | collective-permute-start | bytes 7688 | tf_op jit(solution)/shard_map/ppermute | solution.py:19
  85.5 3.8 %collective-permute-start.10 = (bf16[128,10,1]{0,2,1:T(2,128)(2,1)S(1)}, bf16[128,10,1]{0,2,1:T(2,128)(2,1)S(1)}, u32[]{:S(2)}, u32[]{:S(2)}) collective-permute-start(bf16[128,10,1]{0,2,1:T(2,128)(2,1)S(1)} %get-tuple-element.24), channel_id=1, source_target_pairs={{0,2},{1,3},{4,6},{5,7},{8,10},{9,11},{12,14},{13,15},{16,18},{17,... | collective-permute-start | bytes 7688 | tf_op jit(solution)/shard_map/ppermute | solution.py:16
  93.1 94.1 %all-reduce.2.cloned.1.call-start = ((), (), s32[]{:S(2)}) async-start(), calls=%async_computation.2 | async-start | bytes 4718592 | tf_op jit(solution)/shard_map/psum | solution.py:153
  93.2 3.9 %copy-start.2 = (bf16[256,10,128]{0,2,1:T(8,128)(2,1)S(1)}, bf16[256,10,128]{0,2,1:T(8,128)(2,1)}, u32[]{:S(2)}) copy-start(bf16[256,10,128]{0,2,1:T(8,128)(2,1)} %copy-done.1) | copy-start | bytes 1966084
  119.8 0.8 copy-start.9
  119.8 0.8 copy-start.13
  119.8 0.8 copy-start.15
  119.8 0.8 copy-start.19
  119.8 0.8 copy-start.22
  119.8 35.0 %copy-start.11 = (bf16[4,3,8,128]{3,2,1,0:T(8,128)(2,1)S(1)}, bf16[4,3,8,128]{3,2,1,0:T(8,128)(2,1)}, u32[]{:S(2)}) copy-start(bf16[4,3,8,128]{3,2,1,0:T(8,128)(2,1)} %copy-done.10) | copy-start | bytes 73732
  119.8 35.0 %copy-start.5 = (bf16[256,8,128]{0,2,1:T(8,128)(2,1)S(1)}, bf16[256,8,128]{0,2,1:T(8,128)(2,1)}, u32[]{:S(2)}) copy-start(bf16[256,8,128]{0,2,1:T(8,128)(2,1)} %copy-done.4) | copy-start | bytes 1572868
Sparse Core Ops, SparseCore 0:
  93.3 19.5 reduce-scatter.1
  120.0 67.2 all-reduce.1
where the time goes:
time: 199 us
  blocking collectives  93.1 us (47%)
  waiting for transfers between devices  28 us (14%)
  starting transfers between devices  25.9 us (13%)
  matrix products  21.6 us (11%)
  between operations  16.6 us (8%)
  local copies, waits for them, and re-layouts  6.89 us (3%)
  other arithmetic  6.43 us (3%)
    psum x1, blocking collectives, local(): loss_sum = lax.psum(total, ('rows', 'cols', 'futures'))  33.5 us
    psum x1, blocking collectives, local(): trunk_grad, head_sum = lax.psum((stacked, head_local), ('rows', 'cols'))  26.6 us
    all_gather x2, blocking collectives, local(): whole = lax.all_gather(active, 'futures', axis=0, tiled=True)  19.3 us
    ppermute x6, starting transfers between devices, extended(): lax.ppermute(lax.slice_in_dim(block, block.shape[dim] - width, None, axis...  18.1 us
    dot_general x18, matrix products, weight_grad(): lax.dot_general(flat, window, (((1,), (1,)), ((), ())), preferred_element...  11.9 us
    ppermute x6, waiting for transfers between devices, extended(): lax.ppermute(lax.slice_in_dim(block, 0, width, axis=dim), axis, backward)  10.8 us
    reduce_scatter x1, waiting for transfers between devices, local(): lax.psum_scatter(conv_backward(grad_pad, kernel, rows_here, cols_here), '...  10.2 us
    all_gather x1, blocking collectives, local(): whole_out = lax.all_gather(active, 'futures', axis=0, tiled=True)  9.09 us
  transfers between devices with their start and end apart: 14, of which 10 were waited for; matrix products, arithmetic and copies ran while one was open for 7% of the time, Pallas kernels for 0%

commit v1 on v0

v1 whole, which is shorter than its diff:
```python
import functools
import math

import jax
import jax.numpy as jnp
from jax import lax
from jax.experimental import pallas as pl
from jax.experimental.pallas import tpu as pltpu
from jax.sharding import PartitionSpec as P

BLK = 8
SLOT = 16
F32 = jnp.float32
BF16 = jnp.bfloat16
VMEM = pl.BlockSpec(memory_space=pltpu.VMEM)
SMEM = pl.BlockSpec(memory_space=pltpu.SMEM)
PARAMS = pltpu.CompilerParams(vmem_limit_bytes=48 * 1024 * 1024)


def swap(block, axis, distance=1):
    count = lax.axis_size(axis)
    return lax.ppermute(block, axis, [(i, i ^ distance) for i in range(count)])


def shift(block, axis, step):
    count = lax.axis_size(axis)
    pairs = [(i, i + step) for i in range(count) if 0 <= i + step < count]
    return lax.ppermute(block, axis, pairs)


def ordered(flag, first, second, axis):
    return jnp.concatenate(
        [jnp.where(flag, second, first), jnp.where(flag, first, second)], axis=axis
    )


def pieces(total, step):
    return [(lo, min(step, total - lo)) for lo in range(0, total, step)]


def forward_taps(taps_ref, mat_ref):
    channels = taps_ref.shape[1]
    for tap in range(9):
        row, col = tap // 3, tap % 3
        mat_ref[
            row * channels : (row + 1) * channels, col * channels : (col + 1) * channels
        ] = taps_ref[tap].T


def clear_ends(low_ref, high_ref, count):
    blank = jnp.zeros((8, low_ref.shape[1]), F32)
    low_ref[:8, :] = blank
    high_ref[8 + count : 16 + count, :] = blank


def convolve(src_ref, mat_ref, low_ref, mid_ref, high_ref, count, stride):
    channels = src_ref.shape[1]
    clear_ends(low_ref, high_ref, count)
    for lo, size in pieces(count, 448):
        rows = jnp.concatenate(
            [src_ref[lo + row * stride : lo + row * stride + size, :] for row in range(3)], axis=1
        )
        for col, ref in enumerate((low_ref, mid_ref, high_ref)):
            ref[8 + lo : 8 + lo + size, :] = jnp.dot(
                rows,
                mat_ref[:, col * channels : (col + 1) * channels],
                preferred_element_type=F32,
            )


def combined(low_ref, mid_ref, high_ref, lo, size):
    return (
        low_ref[7 + lo : 7 + lo + size, :]
        + mid_ref[8 + lo : 8 + lo + size, :]
        + high_ref[9 + lo : 9 + lo + size, :]
    )


def own_part(value, index, count):
    width = value.shape[1] // count
    result = value[:, :width]
    for part in range(1, count):
        result = jnp.where(index == part, value[:, part * width : (part + 1) * width], result)
    return result


def kernel_grads(grad_ref, src_ref, base, stride, out_ref):
    own = grad_ref.shape[1]
    cells = grad_ref.shape[0]
    turned = grad_ref[...].T
    moved = jnp.concatenate(
        [
            pltpu.roll(turned, cells - 1, 1).astype(BF16),
            turned.astype(BF16),
            pltpu.roll(turned, 1, 1).astype(BF16),
        ],
        axis=0,
    )
    for row in range(3):
        start = base + row * stride
        part = jnp.dot(moved, src_ref[start : start + cells, :], preferred_element_type=F32)
        for col in range(3):
            tap = 3 * row + col
            out_ref[tap * own : (tap + 1) * own, :] = part[col * own : (col + 1) * own, :]


def first_layer(geom, scal, mid, top, bottom, tiles, taps, padded, active, slope, mat, low, cen, high):
    height, width, futs, layers = geom
    stride = width + SLOT
    halo = layers + 1
    col = scal[1]
    row_at = scal[2]
    row_count = scal[3]
    slots = height + 2 * halo
    lane = lax.broadcasted_iota(jnp.int32, tiles.shape[1:], 0)
    near = (lane < SLOT // 2).astype(jnp.int32) != col
    blank = jnp.zeros(tiles.shape[1:], BF16)
    padded[:SLOT, :] = jnp.where(near & (col == 1), tiles[0], blank)
    for row in range(slots):
        at = SLOT + row * stride
        if row < halo:
            source = top[row]
        elif row < halo + height:
            source = mid[row - halo]
        else:
            source = bottom[row - halo - height]
        padded[at : at + width, :] = source
        after = tiles[row + 1] if row + 1 < slots else blank
        padded[at + width : at + stride, :] = jnp.where(
            near, jnp.where(col == 1, after, tiles[row]), blank
        )
    forward_taps(taps, mat)
    count = active.shape[0]
    convolve(padded, mat, low, cen, high, count, stride)
    spot = lax.broadcasted_iota(jnp.int32, (stride, active.shape[1]), 0)
    inside = (spot < width) | ((col == 0) & (spot < width + SLOT // 2)) | (
        (col == 1) & (spot >= width + SLOT // 2)
    )

    bump = ((spot >= width) & (col == 1)).astype(jnp.int32)

    def finish(at, size, keep):
        pre = combined(low, cen, high, at, size)
        sigma = jax.nn.sigmoid(pre)
        active[at : at + size, :] = jnp.where(keep, pre * sigma, 0.0).astype(BF16)
        return pre, sigma

    edge = halo - 1
    finish(0, SLOT, (col == 1) & (row_at * height - edge >= 0))
    for row in range(height + 2 * edge):
        at = SLOT + row * stride
        place = row_at * height + row - edge
        keep = inside & (bump + place >= 0) & (bump + place < row_count * height)
        pre, sigma = finish(at, stride, keep)
        if edge <= row < edge + height:
            mine = (row - edge) * width
            own_pre = own_part(pre[:width], scal[0], futs)
            own_sig = own_part(sigma[:width], scal[0], futs)
            slope[mine : mine + width, :] = own_sig * (1.0 + own_pre * (1.0 - own_sig))


def last_layer(
    geom, scale, scal, active, taps, heads_w, aux, grad, taps_grad, head_grad, loss,
    mat, low, cen, high, out, pre_s, own_grad
):
    height, width, futs, layers = geom
    stride = width + SLOT
    count = grad.shape[0]
    forward_taps(taps, mat)
    convolve(active, mat, low, cen, high, count, stride)
    for lo, size in pieces(count, 208):
        pre = combined(low, cen, high, lo, size)
        pre_s[lo : lo + size, :] = pre
        out[lo : lo + size, :] = (pre * jax.nn.sigmoid(pre)).astype(BF16)
    nfut = heads_w.shape[0] // 3
    heads = lax.dot_general(
        heads_w[...], out[...], (((1,), (1,)), ((), ())), preferred_element_type=F32
    )
    logit = heads[:nfut]
    target = aux[0:1, :]
    first = heads[nfut : 2 * nfut] - aux[1:2, :]
    second = heads[2 * nfut :] - aux[2:3, :]
    future = lax.broadcasted_iota(jnp.int32, logit.shape, 0).astype(F32)
    mask = jnp.where(aux[3:4, :] == future, aux[4:5, :], 0.0)
    cell = (
        jnp.maximum(logit, 0.0)
        + jnp.log1p(jnp.exp(-jnp.abs(logit)))
        - target * logit
        + 0.5 * (first * first + second * second)
    )
    own = aux[5:6, :]
    loss[...] = jnp.broadcast_to(
        jnp.sum(jnp.where(mask * own > 0.0, cell, 0.0)), loss.shape
    )
    picked = mask > 0.0
    grads = jnp.concatenate(
        [
            jnp.where(picked, (jax.nn.sigmoid(logit) - target) * scale, 0.0),
            jnp.where(picked, first * scale, 0.0),
            jnp.where(picked, second * scale, 0.0),
        ],
        axis=0,
    )
    mine = jnp.where(own > 0.0, grads, 0.0).astype(BF16)
    grads = grads.astype(BF16)
    head_grad[...] = jnp.dot(mine, out[...], preferred_element_type=F32)
    up = lax.dot_general(
        grads, heads_w[...], (((0,), (0,)), ((), ())), preferred_element_type=F32
    )
    low[: count, :] = up
    own_grad[...] = jnp.zeros_like(own_grad)

    def back(lo, size):
        pre = pre_s[lo : lo + size, :]
        sigma = jax.nn.sigmoid(pre)
        value = (low[lo : lo + size, :] * (sigma * (1.0 + pre * (1.0 - sigma)))).astype(BF16)
        grad[lo : lo + size, :] = value
        return value

    back(0, SLOT)
    for row in range(height + 2):
        at = SLOT + row * stride
        value = back(at, stride)
        if 1 <= row <= height:
            mine_at = SLOT + (row - 1) * stride
            own_grad[mine_at : mine_at + width, :] = own_part(
                value[:width].astype(F32), scal[0], futs
            )
    kernel_grads(own_grad, active, stride, stride, taps_grad)


def back_layer(
    geom, scal, grad, taps, slope, padded, taps_grad, mat, low, cen, high, own_grad
):
    height, width, futs, layers = geom
    stride = width + SLOT
    channels = taps.shape[2]
    own = channels // futs
    count = SLOT + height * stride
    for tap in range(9):
        row, col = tap // 3, tap % 3
        mat[
            (2 - row) * channels : (3 - row) * channels, (2 - col) * own : (3 - col) * own
        ] = own_part(taps[tap], scal[0], futs)
    clear_ends(low, high, count)
    for lo, size in pieces(count, 400):
        rows = jnp.concatenate(
            [grad[lo + row * stride : lo + row * stride + size, :] for row in range(3)], axis=1
        )
        part = jnp.dot(rows, mat[...], preferred_element_type=F32)
        for col, ref in enumerate((low, cen, high)):
            ref[8 + lo : 8 + lo + size, :] = part[:, col * own : (col + 1) * own]
    own_grad[...] = jnp.zeros_like(own_grad)
    for row in range(height):
        at = SLOT + row * stride
        up = combined(low, cen, high, at, width)
        value = (up * slope[row * width : (row + 1) * width, :]).astype(BF16)
        own_grad[at : at + width, :] = value.astype(F32)
    kernel_grads(own_grad, padded, layers * stride, stride, taps_grad)


def other_taps(taps, core):
    half = taps.shape[1] // 2
    send = jnp.where(core == 0, taps[:, :half], taps[:, half:])
    got = swap(send, "futures")
    mate = swap(got, "cols")
    return ordered(core == 1, got, mate, 1)


def whole_taps(taps, fut, core):
    if lax.axis_size("futures") != 2:
        return lax.all_gather(taps, "futures", axis=1, tiled=True)
    return ordered(fut == 1, taps, other_taps(taps, core), 1)


def whole_channels(block, fut):
    if lax.axis_size("futures") != 2:
        return lax.all_gather(block, "futures", axis=block.ndim - 1, tiled=True)
    return ordered(fut == 1, block, swap(block, "futures"), block.ndim - 1)


def halves(block, flag):
    half = block.shape[0] // 2
    low, high = block[:half], block[half:]
    return jnp.where(flag, high, low), jnp.where(flag, low, high)


def tile_sum(block, core, row_at):
    kept, sent = halves(block, core == 1)
    kept = kept + swap(sent, "cols")
    bit = row_at & 1
    pair, sent = halves(kept, bit == 1)
    pair = pair + swap(rounded(sent).astype(BF16), "rows").astype(F32)
    pair = rounded(pair)
    done = (pair + swap(pair.astype(BF16), "rows", 2).astype(F32)).astype(BF16)
    done = ordered(bit == 1, done, swap(done, "rows"), 0)
    return ordered(core == 1, done, swap(done, "cols"), 0).astype(F32)


def small_sum(block):
    block = block + swap(block, "cols")
    block = block + swap(block, "rows")
    return block + swap(block, "rows", 2)


def rounded(value):
    return lax.reduce_precision(value, 8, 7)


def split3(value):
    high = rounded(value)
    rest = value - high
    mid = rounded(rest)
    return [high.astype(BF16), mid.astype(BF16), rounded(rest - mid).astype(BF16)]


def cell_data(labels, flow_target, winner, core, row_at, rows_total):
    height, width = labels.shape
    blocks = jnp.repeat(jnp.repeat(winner, BLK, axis=0), BLK, axis=1)
    planes = jnp.stack(
        [labels.astype(BF16), blocks.astype(BF16)]
        + split3(flow_target[0])
        + split3(flow_target[1])
    )
    above = shift(planes[:, -1], "rows", 1)[:, None]
    below = shift(planes[:, 0], "rows", -1)[:, None]
    planes = jnp.concatenate([above, planes, below], axis=1)
    edge = jnp.where(core == 0, planes[:, :, -SLOT:], planes[:, :, :SLOT])
    tile = swap(edge, "cols")
    count = height + 2
    blank = jnp.zeros_like(tile[:, :1])
    slots = jnp.where(
        core == 0,
        jnp.concatenate([blank, tile], axis=1),
        jnp.concatenate([tile, blank], axis=1),
    )
    rows = jnp.concatenate([planes, jnp.zeros_like(planes[:, :1])], axis=1)
    flat = jnp.concatenate([slots, rows], axis=2).astype(F32)
    flat = flat.reshape(flat.shape[0], -1)
    stride = width + SLOT
    total = SLOT + count * stride
    flat = flat[:, :total]
    line = jnp.arange(count + 1, dtype=jnp.int32)[:, None] - 1
    spot = jnp.arange(stride, dtype=jnp.int32)[None] - SLOT
    main = spot >= 0
    right = (core == 0) & (spot == -SLOT)
    left = (core == 1) & (spot == -1)
    line = jnp.where(right, line - 1, line)
    at = row_at * height + line
    real = (at >= 0) & (at < rows_total * height) & (line >= -1) & (line <= height)
    valid = (real & (main | right | left)).astype(F32).reshape(-1)[:total]
    own = (main & (line >= 0) & (line < height)).astype(F32).reshape(-1)[:total]
    return jnp.stack(
        [
            flat[0],
            flat[2] + flat[3] + flat[4],
            flat[5] + flat[6] + flat[7],
            flat[1],
            valid,
            own,
            jnp.zeros_like(own),
            jnp.zeros_like(own),
        ]
    )


def local(features, trunk_weights, head_weights, flow_target, labels, winner):
    own, height, width = features.shape
    layers, _, _, channels = trunk_weights.shape
    fut_total = head_weights.shape[0]
    futs = lax.axis_size("futures")
    fut_here = fut_total // futs
    rows_total = lax.axis_size("rows")
    fut = lax.axis_index("futures")
    core = lax.axis_index("cols")
    row_at = lax.axis_index("rows")
    cell_count = height * width * rows_total * lax.axis_size("cols")
    scale = 1.0 / math.sqrt(cell_count)
    halo = layers + 1
    stride = width + SLOT
    geom = (height, width, futs, layers)
    scal = jnp.stack([fut, core, row_at, jnp.int32(rows_total)]).astype(jnp.int32)

    mine = jnp.transpose(features, (1, 2, 0))
    mid = whole_channels(mine, fut)
    taps = [whole_taps(trunk_weights[layer], fut, core) for layer in range(layers)]
    top = shift(mid[-halo:], "rows", 1)
    bottom = shift(mid[:halo], "rows", -1)
    edge_of = lambda block: jnp.where(core == 0, block[:, -SLOT:], block[:, :SLOT])
    tiles = swap(
        jnp.concatenate([edge_of(top), edge_of(mid), edge_of(bottom)], axis=0), "cols"
    )
    aux = cell_data(labels, flow_target, winner, core, row_at, rows_total)
    heads_w = jnp.transpose(head_weights, (1, 0, 2)).reshape(3 * fut_total, channels)

    def cells(rows):
        return SLOT + rows * stride

    first_cells = cells(height + 4)
    last_cells = cells(height + 2)
    own_cells = -(-cells(height) // 128) * 128
    shape = jax.ShapeDtypeStruct
    padded, active, slope = pl.pallas_call(
        functools.partial(first_layer, geom),
        out_shape=(
            shape((cells(height + 6), channels), BF16),
            shape((first_cells, channels), BF16),
            shape((height * width, own), F32),
        ),
        in_specs=[SMEM] + [VMEM] * 5,
        out_specs=(VMEM,) * 3,
        scratch_shapes=[pltpu.VMEM((3 * channels, 3 * channels), BF16)]
        + [pltpu.VMEM((first_cells + 16, channels), F32)] * 3,
        compiler_params=PARAMS,
        name="first_layer",
    )(scal, mid, top, bottom, tiles, taps[0])

    grad, last_grads, head_grads, loss = pl.pallas_call(
        functools.partial(last_layer, geom, scale),
        out_shape=(
            shape((last_cells, channels), BF16),
            shape((9 * own, channels), F32),
            shape((3 * fut_total, channels), F32),
            shape((8, channels), F32),
        ),
        in_specs=[SMEM] + [VMEM] * 4,
        out_specs=(VMEM,) * 4,
        scratch_shapes=[pltpu.VMEM((3 * channels, 3 * channels), BF16)]
        + [pltpu.VMEM((last_cells + 16, channels), F32)] * 3
        + [
            pltpu.VMEM((last_cells, channels), BF16),
            pltpu.VMEM((last_cells, channels), F32),
            pltpu.VMEM((own_cells, own), F32),
        ],
        compiler_params=PARAMS,
        name="last_layer",
    )(scal, active, taps[1], heads_w, aux)

    first_grads = pl.pallas_call(
        functools.partial(back_layer, geom),
        out_shape=shape((9 * own, channels), F32),
        in_specs=[SMEM] + [VMEM] * 4,
        out_specs=VMEM,
        scratch_shapes=[pltpu.VMEM((3 * channels, 3 * own), BF16)]
        + [pltpu.VMEM((cells(height) + 16, own), F32)] * 3
        + [pltpu.VMEM((own_cells, own), F32)],
        compiler_params=PARAMS,
        name="back_layer",
    )(scal, grad, taps[1], slope, padded)

    by_fut = head_grads.reshape(3, fut_total, channels)
    by_fut = lax.dynamic_slice_in_dim(by_fut, fut * fut_here, fut_here, 1)
    small = jnp.concatenate([by_fut.reshape(3 * fut_here, channels), loss[:1]], axis=0)
    if rows_total == 4:
        sums = [tile_sum(block, core, row_at) for block in (last_grads, first_grads)][::-1]
        small = small_sum(small)
    else:
        sums = [lax.psum(block, ("rows", "cols")) for block in (first_grads, last_grads)]
        small = lax.psum(small, ("rows", "cols"))
    trunk_grad = jnp.stack(sums).reshape(layers, 9, own, channels)
    head_grad = jnp.transpose(small[:-1].reshape(3, fut_here, channels), (1, 0, 2))
    total = small[-1, :1] / cell_count
    return (total, trunk_grad, head_grad)


def solution(mesh):
    placed = (
        P("futures", ("groups", "rows"), "cols"),
        P(None, None, "futures", None),
        P(),
        P(None, ("groups", "rows"), "cols"),
        P(("groups", "rows"), "cols"),
        P(("groups", "rows"), "cols"),
    )
    return jax.shard_map(
        local,
        mesh=mesh,
        in_specs=placed,
        out_specs=(P("groups"), P("groups", None, "futures", None), P("futures", "groups", None)),
        check_vma=False,
    )
```

time: 199 us -> 89.6 us (0.45)
  blocking collectives: 93.1 us -> 0 us
  matrix products: 21.6 us -> 0 us
  between operations: 16.6 us -> 3.05 us
  Pallas kernels: 0 us -> 10.9 us
  starting transfers between devices: 25.9 us -> 30.8 us
    psum x2 -> x0, blocking collectives: 60.2 us -> none  [the longest x1 33.5 us: local(): loss_sum = lax.psum(total, ('rows', 'cols', 'futures'))]
    all_gather x4 -> x0, blocking collectives: 32.9 us -> none  [the longest x2 19.3 us: local(): whole = lax.all_gather(active, 'futures', axis=0, tiled=True)]
    dot_general x48 -> x0, matrix products: 21.6 us -> none  [the longest x18 11.9 us: weight_grad(): lax.dot_general(flat, window, (((1,), (1,)), ((), ())), preferred_element...]
    ppermute x12 -> x24, waiting for transfers between devices: 13.4 us -> 28.9 us  [the longest x20 21.4 us: swap(): return lax.ppermute(block, axis, [(i, i ^ distance) for i in range(count)])]
    pallas_call x0 -> x3, Pallas kernels: none -> 10.9 us  [the longest x1 4.7 us: local(): pl.pallas_call(functools.partial(last_layer, geom, scale), out_shape=(sha...]
    reduce_scatter x1 -> x0, waiting for transfers between devices: 10.2 us -> none  [local(): lax.psum_scatter(conv_backward(grad_pad, kernel, rows_here, cols_here), '...]
    ppermute x12 -> x24, starting transfers between devices: 25.9 us -> 30.8 us  [the longest x20 19.4 us: swap(): return lax.ppermute(block, axis, [(i, i ^ distance) for i in range(count)])]
    psum x1 -> x0, waiting for transfers between devices: 4.3 us -> none  [local(): trunk_grad, head_sum = lax.psum((stacked, head_local), ('rows', 'cols'))]
  transfers between devices with their start and end apart: 14 -> 24, of which waited for: 10 -> 13; matrix products, arithmetic and copies ran while one was open for 7% -> 8% of each run, Pallas kernels for 0% -> 3%
where the time goes in v1:
time: 89.6 us; the launch traced here: 89.2 us
  starting transfers between devices  30.8 us (34%)
  waiting for transfers between devices  28.9 us (32%)
  Pallas kernels  10.9 us (12%)
  local copies, waits for them, and re-layouts  8.45 us (9%)
  other arithmetic  7.06 us (8%)
  between operations  3.05 us (3%)
    ppermute x20, waiting for transfers between devices, swap(): return lax.ppermute(block, axis, [(i, i ^ distance) for i in range(count)])  21.4 us
    ppermute x20, starting transfers between devices, swap(): return lax.ppermute(block, axis, [(i, i ^ distance) for i in range(count)])  19.4 us
    ppermute x4, starting transfers between devices, shift(): return lax.ppermute(block, axis, pairs)  11.3 us
    ppermute x4, waiting for transfers between devices, shift(): return lax.ppermute(block, axis, pairs)  7.51 us
    unnamed x30, local copies, waits for them, and re-layouts  5.34 us
    pallas_call x1, Pallas kernels, local(): pl.pallas_call(functools.partial(last_layer, geom, scale), out_shape=(sha...  4.7 us
    pallas_call x1, Pallas kernels, local(): pl.pallas_call(functools.partial(first_layer, geom), out_shape=(shape((ce...  3.14 us
    pallas_call x1, Pallas kernels, local(): pl.pallas_call(functools.partial(back_layer, geom), out_shape=shape((9 *...  3.1 us
  transfers between devices with their start and end apart: 24, of which 13 were waited for; matrix products, arithmetic and copies ran while one was open for 8% of the time, Pallas kernels for 3%

profile of v1, /device:TPU:0, one launch (start us, length us, event | category | flops | bytes accessed | tf_op | source)
XLA Modules:
  0.0 89.2 jit_solution(18282879113110385660)
XLA Ops:
  0.6 1.2 %copy.21 = bf16[128,8,128]{0,2,1:T(8,128)(2,1)S(1)} copy(bf16[128,8,128]{2,1,0:T(8,128)(2,1)} %param.6) | data formatting | bytes 524288 | tf_op args[0]
  1.8 3.0 %collective-permute-start = (bf16[8,128,128]{2,1,0:T(8,128)(2,1)S(1)}, bf16[8,128,128]{2,1,0:T(8,128)(2,1)S(1)}, u32[]{:S(2)}, u32[]{:S(2)}) collective-permute-start(bf16[8,128,128]{2,1,0:T(8,128)(2,1)S(1)} %bitcast.51), channel_id=1, source_target_pairs={{0,1},{1,0},{2,3},{3,2},{4,5},{5,4},{6,7},{7,6},{8,9},{9,8},{10,11... | collective-permute-start | bytes 786440 | tf_op jit(solution)/shard_map/ppermute | solution.py:22
  4.8 1.3 %slice_bitcast_fusion = (bf16[9,128,256]{2,1,0:T(8,128)(2,1)S(1)}, bf16[9,128,256]{2,1,0:T(8,128)(2,1)S(1)}) fusion(bf16[2,9,128,256]{3,2,1,0:T(8,128)(2,1)} %param.7), kind=kLoop, calls=%fused_computation.18 | loop fusion | bytes 2359296 | tf_op jit(solution)/shard_map/squeeze | solution.py:386
  6.2 0.1 collective-permute-start.6
  6.3 2.1 %collective-permute-start.4 = (bf16[9,64,256]{2,1,0:T(8,128)(2,1)S(1)}, bf16[9,64,256]{2,1,0:T(8,128)(2,1)S(1)}, u32[]{:S(2)}, u32[]{:S(2)}) collective-permute-start(bf16[9,64,256]{2,1,0:T(8,128)(2,1)S(1)} %slice_select_fusion.3), channel_id=1, source_target_pairs={{0,1},{1,0},{2,3},{3,2},{4,5},{5,4},{6,7},{7,6},{8,9},{9,8},{10,11... | collective-permute-start | bytes 884744 | tf_op jit(solution)/shard_map/ppermute | solution.py:22
  8.4 0.1 broadcast_in_dim.42
  8.5 0.1 convert_element_type.107
  8.7 1.3 %collective-permute-start.9 = (bf16[8,128]{1,0:T(8,128)(2,1)S(1)}, bf16[8,128]{1,0:T(8,128)(2,1)S(1)}, u32[]{:S(2)}, u32[]{:S(2)}) collective-permute-start(bf16[8,128]{1,0:T(8,128)(2,1)S(1)} %bitcast.54), channel_id=1, source_target_pairs={{4,0},{8,4},{12,8},{5,1},{9,5},{13,9},{6,2},{10,6},{14,10},{7,3},{... | collective-permute-start | bytes 6152 | tf_op jit(solution)/shard_map/ppermute | solution.py:28
  10.0 4.5 %collective-permute-start.8 = (bf16[8,128]{1,0:T(8,128)(2,1)S(1)}, bf16[8,128]{1,0:T(8,128)(2,1)S(1)}, u32[]{:S(2)}, u32[]{:S(2)}) collective-permute-start(bf16[8,128]{1,0:T(8,128)(2,1)S(1)} %bitcast.56), channel_id=1, source_target_pairs={{0,4},{4,8},{8,12},{1,5},{5,9},{9,13},{2,6},{6,10},{10,14},{3,7},{... | collective-permute-start | bytes 6152 | tf_op jit(solution)/shard_map/ppermute | solution.py:28
  14.6 0.1 fusion.12
  14.7 0.1 reshape.129
  14.8 0.1 and.89
  15.0 0.9 %collective-permute-done.8 = bf16[8,128]{1,0:T(8,128)(2,1)S(1)} collective-permute-done((bf16[8,128]{1,0:T(8,128)(2,1)S(1)}, bf16[8,128]{1,0:T(8,128)(2,1)S(1)}, u32[]{:S(2)}, u32[]{:S(2)}) %collective-permute-start.8) | collective-permute-done | bytes 2080 | tf_op jit(solution)/shard_map/ppermute | solution.py:28
  15.9 0.1 slice_select_fusion.4
  16.0 0.1 collective-permute-start.10
  16.1 0.1 pad_add_fusion.scal
  16.2 0.1 pad.18.clone
  16.2 1.0 %collective-permute-done.10 = bf16[8,10,16]{2,1,0:T(8,128)(2,1)S(1)} collective-permute-done((bf16[8,10,16]{2,1,0:T(8,128)(2,1)S(1)}, bf16[8,10,16]{2,1,0:T(8,128)(2,1)S(1)}, u32[]{:S(2)}, u32[]{:S(2)}) %collective-permute-start.10) | collective-permute-done | bytes 2592 | tf_op jit(solution)/shard_map/ppermute | solution.py:22
  17.3 0.1 maximum_convert_fusion.1
  17.4 0.1 reshape.124
  17.6 0.1 stack.63.aux
  17.8 4.2 %collective-permute-start.1 = (bf16[3,128,256]{2,1,0:T(8,128)(2,1)S(1)}, bf16[3,128,256]{2,1,0:T(8,128)(2,1)S(1)}, u32[]{:S(2)}, u32[]{:S(2)}) collective-permute-start(bf16[3,128,256]{2,1,0:T(8,128)(2,1)S(1)} %get-tuple-element.34), channel_id=1, source_target_pairs={{0,4},{4,8},{8,12},{1,5},{5,9},{9,13},{2,6},{6,10},{10,14},{3,7},{... | collective-permute-start | bytes 589832 | tf_op jit(solution)/shard_map/ppermute | solution.py:28
  22.0 1.3 %collective-permute-start.2 = (bf16[3,128,256]{2,1,0:T(8,128)(2,1)S(1)}, bf16[3,128,256]{2,1,0:T(8,128)(2,1)S(1)}, u32[]{:S(2)}, u32[]{:S(2)}) collective-permute-start(bf16[3,128,256]{2,1,0:T(8,128)(2,1)S(1)} %get-tuple-element.33), channel_id=1, source_target_pairs={{4,0},{8,4},{12,8},{5,1},{9,5},{13,9},{6,2},{10,6},{14,10},{7,3},{... | collective-permute-start | bytes 589832 | tf_op jit(solution)/shard_map/ppermute | solution.py:28
  23.5 0.3 collective-permute-done.4
  23.7 0.2 collective-permute-start.5
  24.0 6.6 %collective-permute-done.2.bottom = bf16[3,128,256]{2,1,0:T(8,128)(2,1)S(1)} collective-permute-done((bf16[3,128,256]{2,1,0:T(8,128)(2,1)S(1)}, bf16[3,128,256]{2,1,0:T(8,128)(2,1)S(1)}, u32[]{:S(2)}, u32[]{:S(2)}) %collective-permute-start.2) | collective-permute-done | bytes 196640 | tf_op jit(solution)/shard_map/ppermute | solution.py:28
  30.6 0.1 collective-permute-start.3
  30.8 1.1 %copy-done.7 = bf16[2,9,128,256]{3,2,1,0:T(8,128)(2,1)S(1)} copy-done((bf16[2,9,128,256]{3,2,1,0:T(8,128)(2,1)S(1)}, bf16[2,9,128,256]{3,2,1,0:T(8,128)(2,1)}, u32[]{:S(2)}) %copy-start.7) | copy-done | bytes 1179672
  31.9 0.5 broadcast_select_fusion.1
  32.4 0.2 pad_maximum_fusion
  32.6 3.1 %first_layer.1 = (bf16[2032,256]{1,0:T(8,128)(2,1)S(1)}, bf16[1744,256]{1,0:T(8,128)(2,1)S(1)}, f32[1024,128]{1,0:T(8,128)S(1)}) custom-call(s32[4]{0:T(128)S(1)} %pad_add_fusion.scal, bf16[8,128,256]{2,1,0:T(8,128)(2,1)S(1)} %pad_maximum_fusion.2.mid, bf16[3,128,256]{2,1,0:T(8,128)(2,1)S(1)} %collective-permute-done.1.top, ...), custom_call_target="tpu_custom_call" | custom-call | tf_op jit(solution)/shard_map/first_layer/pallas_call | solution.py:403
  35.8 1.0 %copy-done = bf16[2032,256]{1,0:T(8,128)(2,1)} copy-done((bf16[2032,256]{1,0:T(8,128)(2,1)}, bf16[2032,256]{1,0:T(8,128)(2,1)S(1)}, u32[]{:S(2)}) %copy-start) | copy-done | bytes 1040408
  36.8 4.7 %last_layer.1 = (bf16[1456,256]{1,0:T(8,128)(2,1)S(1)}, f32[1152,256]{1,0:T(8,128)S(1)}, f32[24,256]{1,0:T(8,128)S(1)}, f32[8,256]{1,0:T(8,128)S(1)}) custom-call(s32[4]{0:T(128)S(1)} %pad_add_fusion.scal, bf16[1744,256]{1,0:T(8,128)(2,1)S(1)} %get-tuple-element.10.active, bf16[9,256,256]{2,1,0:T(8,128)(2,1)S(1)} %get-tuple-element.52.taps, ...), custom_call_target="tpu_custom_call" | custom-call | tf_op jit(solution)/shard_map/last_layer/pallas_call | solution.py:418
  41.5 0.9 copy-done.2
  42.4 0.9 %slice_select_fusion.1 = f32[576,256]{1,0:T(8,128)} fusion(f32[1152,256]{1,0:T(8,128)S(1)} %get-tuple-element.16, pred[]{:T(512)S(6)} %eq.55), kind=kLoop, calls=%fused_computation.25 | loop fusion | flops 147456 | bytes 1769473 | tf_op jit(solution)/shard_map/jit(_where)/select_n | solution.py:285
  43.3 0.5 collective-permute-start.11
  43.9 1.2 %copy-done.1 = bf16[2032,256]{1,0:T(8,128)(2,1)S(1)} copy-done((bf16[2032,256]{1,0:T(8,128)(2,1)S(1)}, bf16[2032,256]{1,0:T(8,128)(2,1)}, u32[]{:S(2)}) %copy-start.1) | copy-done | bytes 1040408
  45.1 3.1 %back_layer.1 = f32[1152,256]{1,0:T(8,128)S(1)} custom-call(s32[4]{0:T(128)S(1)} %pad_add_fusion.scal, bf16[1456,256]{1,0:T(8,128)(2,1)S(1)} %copy-done.3, bf16[9,256,256]{2,1,0:T(8,128)(2,1)S(1)} %get-tuple-element.52.taps, f32[1024,128]{1,0:T(8,128)S(1)} %copy-done.5, bf16[2032,256]{1,0:T(8,128)(2,1)S(1)} %copy-done.1), custom_call_target="tpu_custom_call" | custom-call | tf_op jit(solution)/shard_map/back_layer/pallas_call | solution.py:439
  48.2 0.9 slice_select_fusion
  49.2 1.6 %collective-permute-start.12 = (f32[13,256]{1,0:T(8,128)S(1)}, f32[13,256]{1,0:T(8,128)S(1)}, u32[]{:S(2)}, u32[]{:S(2)}) collective-permute-start(f32[13,256]{1,0:T(8,128)S(1)} %fusion.22), channel_id=1, source_target_pairs={{0,4},{4,0},{8,12},{12,8},{1,5},{5,1},{9,13},{13,9},{2,6},{6,2},{1... | collective-permute-start | bytes 39944 | tf_op jit(solution)/shard_map/ppermute | solution.py:22
  50.8 2.2 %collective-permute-done.12 = f32[13,256]{1,0:T(8,128)S(1)} collective-permute-done((f32[13,256]{1,0:T(8,128)S(1)}, f32[13,256]{1,0:T(8,128)S(1)}, u32[]{:S(2)}, u32[]{:S(2)}) %collective-permute-start.12) | collective-permute-done | bytes 13344 | tf_op jit(solution)/shard_map/ppermute | solution.py:22
  53.0 2.6 %collective-permute-start.13 = (f32[13,256]{1,0:T(8,128)S(1)}, f32[13,256]{1,0:T(8,128)S(1)}, u32[]{:S(2)}, u32[]{:S(2)}) collective-permute-start(f32[13,256]{1,0:T(8,128)S(1)} %add.93), channel_id=1, source_target_pairs={{0,8},{4,12},{8,0},{12,4},{1,9},{5,13},{9,1},{13,5},{2,10},{6,14},... | collective-permute-start | bytes 39944 | tf_op jit(solution)/shard_map/ppermute | solution.py:22
  55.5 2.1 %collective-permute-done.13 = f32[13,256]{1,0:T(8,128)S(1)} collective-permute-done((f32[13,256]{1,0:T(8,128)S(1)}, f32[13,256]{1,0:T(8,128)S(1)}, u32[]{:S(2)}, u32[]{:S(2)}) %collective-permute-start.13) | collective-permute-done | bytes 13344 | tf_op jit(solution)/shard_map/ppermute | solution.py:22
  57.6 0.5 slice.205
  58.1 0.6 reshape.123
  59.4 1.2 %select_add_fusion = f32[576,256]{1,0:T(8,128)S(1)} fusion(f32[576,256]{1,0:T(8,128)} %collective-permute-done.19, f32[1152,256]{1,0:T(8,128)S(1)} %get-tuple-element.16, pred[]{:T(512)S(6)} %eq.55), kind=kLoop, calls=%fused_computation.16 | loop fusion | flops 294912 | bytes 2359297 | tf_op jit(solution)/shard_map/add | solution.py:290
  60.6 1.6 %collective-permute-start.20 = (bf16[288,256]{1,0:T(8,128)(2,1)S(1)}, bf16[288,256]{1,0:T(8,128)(2,1)S(1)}, u32[]{:S(2)}, u32[]{:S(2)}) collective-permute-start(bf16[288,256]{1,0:T(8,128)(2,1)S(1)} %reduce-precision_convert_fusion), channel_id=1, source_target_pairs={{0,4},{4,0},{8,12},{12,8},{1,5},{5,1},{9,13},{13,9},{2,6},{6,2},{1... | collective-permute-start | bytes 442376 | tf_op jit(solution)/shard_map/ppermute | solution.py:22
  62.3 0.1 select_add_fusion.1
  62.4 0.5 collective-permute-start.15
  63.0 3.2 %collective-permute-done.20 = bf16[288,256]{1,0:T(8,128)(2,1)S(1)} collective-permute-done((bf16[288,256]{1,0:T(8,128)(2,1)S(1)}, bf16[288,256]{1,0:T(8,128)(2,1)S(1)}, u32[]{:S(2)}, u32[]{:S(2)}) %collective-permute-start.20) | collective-permute-done | bytes 147488 | tf_op jit(solution)/shard_map/ppermute | solution.py:22
  66.3 3.3 %collective-permute-start.21 = (bf16[288,256]{1,0:T(8,128)(2,1)S(1)}, bf16[288,256]{1,0:T(8,128)(2,1)S(1)}, u32[]{:S(2)}, u32[]{:S(2)}) collective-permute-start(bf16[288,256]{1,0:T(8,128)(2,1)S(1)} %fusion.19), channel_id=1, source_target_pairs={{0,8},{4,12},{8,0},{12,4},{1,9},{5,13},{9,1},{13,5},{2,10},{6,14},... | collective-permute-start | bytes 442376 | tf_op jit(solution)/shard_map/ppermute | solution.py:22
  69.6 0.2 collective-permute-done.15
  69.9 2.9 %collective-permute-start.16 = (bf16[288,256]{1,0:T(8,128)(2,1)S(1)}, bf16[288,256]{1,0:T(8,128)(2,1)S(1)}, u32[]{:S(2)}, u32[]{:S(2)}) collective-permute-start(bf16[288,256]{1,0:T(8,128)(2,1)S(1)} %fusion.18), channel_id=1, source_target_pairs={{0,8},{4,12},{8,0},{12,4},{1,9},{5,13},{9,1},{13,5},{2,10},{6,14},... | collective-permute-start | bytes 442376 | tf_op jit(solution)/shard_map/ppermute | solution.py:22
  72.8 4.3 %collective-permute-done.21 = bf16[288,256]{1,0:T(8,128)(2,1)S(1)} collective-permute-done((bf16[288,256]{1,0:T(8,128)(2,1)S(1)}, bf16[288,256]{1,0:T(8,128)(2,1)S(1)}, u32[]{:S(2)}, u32[]{:S(2)}) %collective-permute-start.21) | collective-permute-done | bytes 147488 | tf_op jit(solution)/shard_map/ppermute | solution.py:22
  77.1 0.5 collective-permute-start.22
  77.6 1.8 %collective-permute-done.16 = bf16[288,256]{1,0:T(8,128)(2,1)S(1)} collective-permute-done((bf16[288,256]{1,0:T(8,128)(2,1)S(1)}, bf16[288,256]{1,0:T(8,128)(2,1)S(1)}, u32[]{:S(2)}, u32[]{:S(2)}) %collective-permute-start.16) | collective-permute-done | bytes 147488 | tf_op jit(solution)/shard_map/ppermute | solution.py:22
  79.4 0.1 add_convert_fusion.1
  79.4 0.1 collective-permute-start.17
  79.5 2.8 %collective-permute-done.22 = bf16[288,256]{1,0:T(8,128)(2,1)S(1)} collective-permute-done((bf16[288,256]{1,0:T(8,128)(2,1)S(1)}, bf16[288,256]{1,0:T(8,128)(2,1)S(1)}, u32[]{:S(2)}, u32[]{:S(2)}) %collective-permute-start.22) | collective-permute-done | bytes 147488 | tf_op jit(solution)/shard_map/ppermute | solution.py:22
  82.4 2.2 %collective-permute-done.17 = bf16[288,256]{1,0:T(8,128)(2,1)S(1)} collective-permute-done((bf16[288,256]{1,0:T(8,128)(2,1)S(1)}, bf16[288,256]{1,0:T(8,128)(2,1)S(1)}, u32[]{:S(2)}, u32[]{:S(2)}) %collective-permute-start.17) | collective-permute-done | bytes 147488 | tf_op jit(solution)/shard_map/ppermute | solution.py:22
  84.8 0.1 select_bitcast_fusion.1
  85.0 1.4 %collective-permute-done.18 = bf16[576,256]{1,0:T(8,128)(2,1)S(1)} collective-permute-done((bf16[576,256]{1,0:T(8,128)(2,1)S(1)}, bf16[576,256]{1,0:T(8,128)(2,1)S(1)}, u32[]{:S(2)}, u32[]{:S(2)}) %collective-permute-start.18) | collective-permute-done | bytes 294944 | tf_op jit(solution)/shard_map/ppermute | solution.py:22
  86.4 0.1 select_bitcast_fusion.3
  86.5 1.6 %maximum_convert_fusion = f32[2,9,128,256]{3,2,1,0:T(8,128)} fusion(bf16[1,9,128,256]{3,2,1,0:T(8,128)(2,1)S(1)} %bitcast.49, bf16[1,9,128,256]{3,2,1,0:T(8,128)(2,1)S(1)} %bitcast.50), kind=kLoop, calls=%fused_computation.2 | loop fusion | flops 1179648 | bytes 3538944 | tf_op jit(solution)/shard_map/stack | solution.py:460
  (93 shorter events, 1.5 us)
Async XLA Ops:
  1.8 15.9 %collective-permute-start = (bf16[8,128,128]{2,1,0:T(8,128)(2,1)S(1)}, bf16[8,128,128]{2,1,0:T(8,128)(2,1)S(1)}, u32[]{:S(2)}, u32[]{:S(2)}) collective-permute-start(bf16[8,128,128]{2,1,0:T(8,128)(2,1)S(1)} %bitcast.51), channel_id=1, source_target_pairs={{0,1},{1,0},{2,3},{3,2},{4,5},{5,4},{6,7},{7,6},{8,9},{9,8},{10,11... | collective-permute-start | bytes 786440 | tf_op jit(solution)/shard_map/ppermute | solution.py:22
  6.1 2.3 %copy-start.11 = (s32[8,128]{1,0:T(8,128)S(1)}, s32[8,128]{1,0:T(8,128)}, u32[]{:S(2)}) copy-start(s32[8,128]{1,0:T(8,128)} %param.10) | copy-start | bytes 12292
  6.1 2.3 %copy-start.12 = (s32[1,16]{1,0:T(1,128)S(1)}, s32[1,16]{1,0:T(1,128)}, u32[]{:S(2)}) copy-start(s32[1,16]{1,0:T(1,128)} %param.11) | copy-start | bytes 196
  6.1 2.5 %copy-start.10 = (f32[2,8,128]{2,1,0:T(8,128)S(1)}, f32[2,8,128]{2,1,0:T(8,128)}, u32[]{:S(2)}) copy-start(f32[2,8,128]{2,1,0:T(8,128)} %param.9) | copy-start | bytes 24580
  6.2 17.2 %collective-permute-start.6 = (bf16[9,64,256]{2,1,0:T(8,128)(2,1)S(1)}, bf16[9,64,256]{2,1,0:T(8,128)(2,1)S(1)}, u32[]{:S(2)}, u32[]{:S(2)}) collective-permute-start(bf16[9,64,256]{2,1,0:T(8,128)(2,1)S(1)} %slice_select_fusion.2), channel_id=1, source_target_pairs={{0,1},{1,0},{2,3},{3,2},{4,5},{5,4},{6,7},{7,6},{8,9},{9,8},{10,11... | collective-permute-start | bytes 884744 | tf_op jit(solution)/shard_map/ppermute | solution.py:22
  6.3 17.4 %collective-permute-start.4 = (bf16[9,64,256]{2,1,0:T(8,128)(2,1)S(1)}, bf16[9,64,256]{2,1,0:T(8,128)(2,1)S(1)}, u32[]{:S(2)}, u32[]{:S(2)}) collective-permute-start(bf16[9,64,256]{2,1,0:T(8,128)(2,1)S(1)} %slice_select_fusion.3), channel_id=1, source_target_pairs={{0,1},{1,0},{2,3},{3,2},{4,5},{5,4},{6,7},{7,6},{8,9},{9,8},{10,11... | collective-permute-start | bytes 884744 | tf_op jit(solution)/shard_map/ppermute | solution.py:22
  8.7 6.2 %collective-permute-start.9 = (bf16[8,128]{1,0:T(8,128)(2,1)S(1)}, bf16[8,128]{1,0:T(8,128)(2,1)S(1)}, u32[]{:S(2)}, u32[]{:S(2)}) collective-permute-start(bf16[8,128]{1,0:T(8,128)(2,1)S(1)} %bitcast.54), channel_id=1, source_target_pairs={{4,0},{8,4},{12,8},{5,1},{9,5},{13,9},{6,2},{10,6},{14,10},{7,3},{... | collective-permute-start | bytes 6152 | tf_op jit(solution)/shard_map/ppermute | solution.py:28
  10.0 5.8 %collective-permute-start.8 = (bf16[8,128]{1,0:T(8,128)(2,1)S(1)}, bf16[8,128]{1,0:T(8,128)(2,1)S(1)}, u32[]{:S(2)}, u32[]{:S(2)}) collective-permute-start(bf16[8,128]{1,0:T(8,128)(2,1)S(1)} %bitcast.56), channel_id=1, source_target_pairs={{0,4},{4,8},{8,12},{1,5},{5,9},{9,13},{2,6},{6,10},{10,14},{3,7},{... | collective-permute-start | bytes 6152 | tf_op jit(solution)/shard_map/ppermute | solution.py:28
  16.0 1.3 %collective-permute-start.10 = (bf16[8,10,16]{2,1,0:T(8,128)(2,1)S(1)}, bf16[8,10,16]{2,1,0:T(8,128)(2,1)S(1)}, u32[]{:S(2)}, u32[]{:S(2)}) collective-permute-start(bf16[8,10,16]{2,1,0:T(8,128)(2,1)S(1)} %slice_select_fusion.4), channel_id=1, source_target_pairs={{0,2},{2,0},{1,3},{3,1},{4,6},{6,4},{5,7},{7,5},{8,10},{10,8},{9,1... | collective-permute-start | bytes 7688 | tf_op jit(solution)/shard_map/ppermute | solution.py:22
  17.8 12.8 %collective-permute-start.1 = (bf16[3,128,256]{2,1,0:T(8,128)(2,1)S(1)}, bf16[3,128,256]{2,1,0:T(8,128)(2,1)S(1)}, u32[]{:S(2)}, u32[]{:S(2)}) collective-permute-start(bf16[3,128,256]{2,1,0:T(8,128)(2,1)S(1)} %get-tuple-element.34), channel_id=1, source_target_pairs={{0,4},{4,8},{8,12},{1,5},{5,9},{9,13},{2,6},{6,10},{10,14},{3,7},{... | collective-permute-start | bytes 589832 | tf_op jit(solution)/shard_map/ppermute | solution.py:28
  22.0 8.6 %collective-permute-start.2 = (bf16[3,128,256]{2,1,0:T(8,128)(2,1)S(1)}, bf16[3,128,256]{2,1,0:T(8,128)(2,1)S(1)}, u32[]{:S(2)}, u32[]{:S(2)}) collective-permute-start(bf16[3,128,256]{2,1,0:T(8,128)(2,1)S(1)} %get-tuple-element.33), channel_id=1, source_target_pairs={{4,0},{8,4},{12,8},{5,1},{9,5},{13,9},{6,2},{10,6},{14,10},{7,3},{... | collective-permute-start | bytes 589832 | tf_op jit(solution)/shard_map/ppermute | solution.py:28
  23.4 7.3 %collective-permute-start.7 = (bf16[9,64,256]{2,1,0:T(8,128)(2,1)S(1)}, bf16[9,64,256]{2,1,0:T(8,128)(2,1)S(1)}, u32[]{:S(2)}, u32[]{:S(2)}) collective-permute-start(bf16[9,64,256]{2,1,0:T(8,128)(2,1)S(1)} %collective-permute-done.6), channel_id=1, source_target_pairs={{0,2},{2,0},{1,3},{3,1},{4,6},{6,4},{5,7},{7,5},{8,10},{10,8},{9,1... | collective-permute-start | bytes 884744 | tf_op jit(solution)/shard_map/ppermute | solution.py:22
  23.7 7.0 %collective-permute-start.5 = (bf16[9,64,256]{2,1,0:T(8,128)(2,1)S(1)}, bf16[9,64,256]{2,1,0:T(8,128)(2,1)S(1)}, u32[]{:S(2)}, u32[]{:S(2)}) collective-permute-start(bf16[9,64,256]{2,1,0:T(8,128)(2,1)S(1)} %collective-permute-done.4), channel_id=1, source_target_pairs={{0,2},{2,0},{1,3},{3,1},{4,6},{6,4},{5,7},{7,5},{8,10},{10,8},{9,1... | collective-permute-start | bytes 884744 | tf_op jit(solution)/shard_map/ppermute | solution.py:22
  30.6 1.3 %copy-start.7 = (bf16[2,9,128,256]{3,2,1,0:T(8,128)(2,1)S(1)}, bf16[2,9,128,256]{3,2,1,0:T(8,128)(2,1)}, u32[]{:S(2)}) copy-start(bf16[2,9,128,256]{3,2,1,0:T(8,128)(2,1)} %param.7) | copy-start | bytes 3538948
  30.6 2.0 %collective-permute-start.3 = (bf16[14,16,256]{2,1,0:T(8,128)(2,1)S(1)}, bf16[14,16,256]{2,1,0:T(8,128)(2,1)S(1)}, u32[]{:S(2)}, u32[]{:S(2)}) collective-permute-start(bf16[14,16,256]{2,1,0:T(8,128)(2,1)S(1)} %pad_maximum_fusion.9), channel_id=1, source_target_pairs={{0,2},{2,0},{1,3},{3,1},{4,6},{6,4},{5,7},{7,5},{8,10},{10,8},{9,1... | collective-permute-start | bytes 344072 | tf_op jit(solution)/shard_map/ppermute | solution.py:22
  32.6 4.1 %copy-start.6 = (bf16[8,3,256]{2,0,1:T(8,128)(2,1)S(1)}, bf16[8,3,256]{2,0,1:T(8,128)(2,1)}, u32[]{:S(2)}) copy-start(bf16[8,3,256]{2,0,1:T(8,128)(2,1)} %param.8) | copy-start | bytes 36868
  35.8 1.0 %copy-start = (bf16[2032,256]{1,0:T(8,128)(2,1)}, bf16[2032,256]{1,0:T(8,128)(2,1)S(1)}, u32[]{:S(2)}) copy-start(bf16[2032,256]{1,0:T(8,128)(2,1)S(1)} %get-tuple-element.15.padded) | copy-start | bytes 3121156
  36.8 4.7 %copy-start.4 = (f32[1024,128]{1,0:T(8,128)}, f32[1024,128]{1,0:T(8,128)S(1)}, u32[]{:S(2)}) copy-start(f32[1024,128]{1,0:T(8,128)S(1)} %get-tuple-element.14.slope) | copy-start | bytes 1572868
  41.5 0.9 copy-start.2
  42.4 1.5 %copy-start.8 = (f32[12,256]{1,0:T(8,128)}, f32[12,256]{1,0:T(8,128)S(1)}, u32[]{:S(2)}) copy-start(f32[12,256]{1,0:T(8,128)S(1)} %reshape.122) | copy-start | bytes 36868
  42.4 1.5 %copy-start.3 = (bf16[1456,256]{1,0:T(8,128)(2,1)S(1)}, bf16[1456,256]{1,0:T(8,128)(2,1)}, u32[]{:S(2)}) copy-start(bf16[1456,256]{1,0:T(8,128)(2,1)} %copy-done.2) | copy-start | bytes 2236420
  42.4 1.5 %copy-start.5 = (f32[1024,128]{1,0:T(8,128)S(1)}, f32[1024,128]{1,0:T(8,128)}, u32[]{:S(2)}) copy-start(f32[1024,128]{1,0:T(8,128)} %copy-done.4) | copy-start | bytes 1572868
  43.3 16.1 %collective-permute-start.19 = (f32[576,256]{1,0:T(8,128)}, f32[576,256]{1,0:T(8,128)}, u32[]{:S(2)}, u32[]{:S(2)}) collective-permute-start(f32[576,256]{1,0:T(8,128)} %slice_select_fusion.1), channel_id=1, source_target_pairs={{0,2},{2,0},{1,3},{3,1},{4,6},{6,4},{5,7},{7,5},{8,10},{10,8},{9,1... | collective-permute-start | bytes 1769480 | tf_op jit(solution)/shard_map/ppermute | solution.py:22
  43.3 5.8 %collective-permute-start.11 = (f32[13,256]{1,0:T(8,128)S(1)}, f32[13,256]{1,0:T(8,128)S(1)}, u32[]{:S(2)}, u32[]{:S(2)}) collective-permute-start(f32[13,256]{1,0:T(8,128)S(1)} %pad_maximum_fusion.11), channel_id=1, source_target_pairs={{0,2},{2,0},{1,3},{3,1},{4,6},{6,4},{5,7},{7,5},{8,10},{10,8},{9,1... | collective-permute-start | bytes 39944 | tf_op jit(solution)/shard_map/ppermute | solution.py:22
  43.9 1.2 %copy-start.1 = (bf16[2032,256]{1,0:T(8,128)(2,1)S(1)}, bf16[2032,256]{1,0:T(8,128)(2,1)}, u32[]{:S(2)}) copy-start(bf16[2032,256]{1,0:T(8,128)(2,1)} %copy-done) | copy-start | bytes 3121156
  48.2 1.0 %copy-start.9 = (f32[12,256]{1,0:T(8,128)S(1)}, f32[12,256]{1,0:T(8,128)}, u32[]{:S(2)}) copy-start(f32[12,256]{1,0:T(8,128)} %copy-done.8) | copy-start | bytes 36868
  49.1 13.2 %collective-permute-start.14 = (f32[576,256]{1,0:T(8,128)}, f32[576,256]{1,0:T(8,128)S(1)}, u32[]{:S(2)}, u32[]{:S(2)}) collective-permute-start(f32[576,256]{1,0:T(8,128)} %slice_select_fusion), channel_id=1, source_target_pairs={{0,2},{2,0},{1,3},{3,1},{4,6},{6,4},{5,7},{7,5},{8,10},{10,8},{9,1... | collective-permute-start | bytes 1769480 | tf_op jit(solution)/shard_map/ppermute | solution.py:22
  49.2 3.8 %collective-permute-start.12 = (f32[13,256]{1,0:T(8,128)S(1)}, f32[13,256]{1,0:T(8,128)S(1)}, u32[]{:S(2)}, u32[]{:S(2)}) collective-permute-start(f32[13,256]{1,0:T(8,128)S(1)} %fusion.22), channel_id=1, source_target_pairs={{0,4},{4,0},{8,12},{12,8},{1,5},{5,1},{9,13},{13,9},{2,6},{6,2},{1... | collective-permute-start | bytes 39944 | tf_op jit(solution)/shard_map/ppermute | solution.py:22
  53.0 4.6 %collective-permute-start.13 = (f32[13,256]{1,0:T(8,128)S(1)}, f32[13,256]{1,0:T(8,128)S(1)}, u32[]{:S(2)}, u32[]{:S(2)}) collective-permute-start(f32[13,256]{1,0:T(8,128)S(1)} %add.93), channel_id=1, source_target_pairs={{0,8},{4,12},{8,0},{12,4},{1,9},{5,13},{9,1},{13,5},{2,10},{6,14},... | collective-permute-start | bytes 39944 | tf_op jit(solution)/shard_map/ppermute | solution.py:22
  60.6 5.6 %collective-permute-start.20 = (bf16[288,256]{1,0:T(8,128)(2,1)S(1)}, bf16[288,256]{1,0:T(8,128)(2,1)S(1)}, u32[]{:S(2)}, u32[]{:S(2)}) collective-permute-start(bf16[288,256]{1,0:T(8,128)(2,1)S(1)} %reduce-precision_convert_fusion), channel_id=1, source_target_pairs={{0,4},{4,0},{8,12},{12,8},{1,5},{5,1},{9,13},{13,9},{2,6},{6,2},{1... | collective-permute-start | bytes 442376 | tf_op jit(solution)/shard_map/ppermute | solution.py:22
  62.4 7.4 %collective-permute-start.15 = (bf16[288,256]{1,0:T(8,128)(2,1)S(1)}, bf16[288,256]{1,0:T(8,128)(2,1)S(1)}, u32[]{:S(2)}, u32[]{:S(2)}) collective-permute-start(bf16[288,256]{1,0:T(8,128)(2,1)S(1)} %reduce-precision_convert_fusion.1), channel_id=1, source_target_pairs={{0,4},{4,0},{8,12},{12,8},{1,5},{5,1},{9,13},{13,9},{2,6},{6,2},{1... | collective-permute-start | bytes 442376 | tf_op jit(solution)/shard_map/ppermute | solution.py:22
  66.3 10.8 %collective-permute-start.21 = (bf16[288,256]{1,0:T(8,128)(2,1)S(1)}, bf16[288,256]{1,0:T(8,128)(2,1)S(1)}, u32[]{:S(2)}, u32[]{:S(2)}) collective-permute-start(bf16[288,256]{1,0:T(8,128)(2,1)S(1)} %fusion.19), channel_id=1, source_target_pairs={{0,8},{4,12},{8,0},{12,4},{1,9},{5,13},{9,1},{13,5},{2,10},{6,14},... | collective-permute-start | bytes 442376 | tf_op jit(solution)/shard_map/ppermute | solution.py:22
  69.9 9.5 %collective-permute-start.16 = (bf16[288,256]{1,0:T(8,128)(2,1)S(1)}, bf16[288,256]{1,0:T(8,128)(2,1)S(1)}, u32[]{:S(2)}, u32[]{:S(2)}) collective-permute-start(bf16[288,256]{1,0:T(8,128)(2,1)S(1)} %fusion.18), channel_id=1, source_target_pairs={{0,8},{4,12},{8,0},{12,4},{1,9},{5,13},{9,1},{13,5},{2,10},{6,14},... | collective-permute-start | bytes 442376 | tf_op jit(solution)/shard_map/ppermute | solution.py:22
  77.1 5.2 %collective-permute-start.22 = (bf16[288,256]{1,0:T(8,128)(2,1)S(1)}, bf16[288,256]{1,0:T(8,128)(2,1)S(1)}, u32[]{:S(2)}, u32[]{:S(2)}) collective-permute-start(bf16[288,256]{1,0:T(8,128)(2,1)S(1)} %add_convert_fusion), channel_id=1, source_target_pairs={{0,4},{4,0},{8,12},{12,8},{1,5},{5,1},{9,13},{13,9},{2,6},{6,2},{1... | collective-permute-start | bytes 442376 | tf_op jit(solution)/shard_map/ppermute | solution.py:22
  79.4 5.2 %collective-permute-start.17 = (bf16[288,256]{1,0:T(8,128)(2,1)S(1)}, bf16[288,256]{1,0:T(8,128)(2,1)S(1)}, u32[]{:S(2)}, u32[]{:S(2)}) collective-permute-start(bf16[288,256]{1,0:T(8,128)(2,1)S(1)} %add_convert_fusion.1), channel_id=1, source_target_pairs={{0,4},{4,0},{8,12},{12,8},{1,5},{5,1},{9,13},{13,9},{2,6},{6,2},{1... | collective-permute-start | bytes 442376 | tf_op jit(solution)/shard_map/ppermute | solution.py:22
  82.4 2.4 %collective-permute-start.23 = (bf16[576,256]{1,0:T(8,128)(2,1)S(1)}, bf16[576,256]{1,0:T(8,128)(2,1)S(1)}, u32[]{:S(2)}, u32[]{:S(2)}) collective-permute-start(bf16[576,256]{1,0:T(8,128)(2,1)S(1)} %pad_maximum_fusion.8), channel_id=1, source_target_pairs={{0,2},{2,0},{1,3},{3,1},{4,6},{6,4},{5,7},{7,5},{8,10},{10,8},{9,1... | collective-permute-start | bytes 884744 | tf_op jit(solution)/shard_map/ppermute | solution.py:22
  84.7 1.6 %collective-permute-start.18 = (bf16[576,256]{1,0:T(8,128)(2,1)S(1)}, bf16[576,256]{1,0:T(8,128)(2,1)S(1)}, u32[]{:S(2)}, u32[]{:S(2)}) collective-permute-start(bf16[576,256]{1,0:T(8,128)(2,1)S(1)} %pad_maximum_fusion.7), channel_id=1, source_target_pairs={{0,2},{2,0},{1,3},{3,1},{4,6},{6,4},{5,7},{7,5},{8,10},{10,8},{9,1... | collective-permute-start | bytes 884744 | tf_op jit(solution)/shard_map/ppermute | solution.py:22

commit v2 on v1

v2 whole, which is shorter than its diff:
```python
import functools
import math

import jax
import jax.numpy as jnp
from jax import lax
from jax.experimental import pallas as pl
from jax.experimental.pallas import tpu as pltpu
from jax.sharding import PartitionSpec as P

BLK = 8
SLOT = 16
F32 = jnp.float32
BF16 = jnp.bfloat16
VMEM = pl.BlockSpec(memory_space=pltpu.VMEM)
SMEM = pl.BlockSpec(memory_space=pltpu.SMEM)
PARAMS = pltpu.CompilerParams(vmem_limit_bytes=14 * 1024 * 1024)


def swap(block, axis, distance=1):
    count = lax.axis_size(axis)
    return lax.ppermute(block, axis, [(i, i ^ distance) for i in range(count)])


def shift(block, axis, step):
    count = lax.axis_size(axis)
    pairs = [(i, i + step) for i in range(count) if 0 <= i + step < count]
    return lax.ppermute(block, axis, pairs)


def ordered(flag, first, second, axis):
    return jnp.concatenate(
        [jnp.where(flag, second, first), jnp.where(flag, first, second)], axis=axis
    )


def pieces(total, step):
    return [(lo, min(step, total - lo)) for lo in range(0, total, step)]


def whole_tap(layer, tap, scal, refs):
    if len(refs) == 1:
        return refs[0][tap]
    own_ref, got_ref, mate_ref = refs
    mine, got, mate = own_ref[layer, tap], got_ref[tap], mate_ref[tap]
    theirs = ordered(scal[1] == 1, got, mate, 0)
    return ordered(scal[0] == 1, mine, theirs, 0)


def forward_taps(layer, scal, refs, mat_ref):
    for tap in range(9):
        row, col = tap // 3, tap % 3
        block = whole_tap(layer, tap, scal, refs).T
        channels = block.shape[0]
        mat_ref[
            row * channels : (row + 1) * channels, col * channels : (col + 1) * channels
        ] = block


def clear_ends(low_ref, high_ref, count):
    blank = jnp.zeros((8, low_ref.shape[1]), F32)
    low_ref[:8, :] = blank
    high_ref[8 + count : 16 + count, :] = blank


def convolve(src_ref, mat_ref, low_ref, mid_ref, high_ref, count, stride):
    channels = src_ref.shape[1]
    clear_ends(low_ref, high_ref, count)
    for lo, size in pieces(count, 448):
        rows = jnp.concatenate(
            [src_ref[lo + row * stride : lo + row * stride + size, :] for row in range(3)], axis=1
        )
        for col, ref in enumerate((low_ref, mid_ref, high_ref)):
            ref[8 + lo : 8 + lo + size, :] = jnp.dot(
                rows,
                mat_ref[:, col * channels : (col + 1) * channels],
                preferred_element_type=F32,
            )


def combined(low_ref, mid_ref, high_ref, lo, size):
    return (
        low_ref[7 + lo : 7 + lo + size, :]
        + mid_ref[8 + lo : 8 + lo + size, :]
        + high_ref[9 + lo : 9 + lo + size, :]
    )


def own_part(value, index, count):
    width = value.shape[1] // count
    result = value[:, :width]
    for part in range(1, count):
        result = jnp.where(index == part, value[:, part * width : (part + 1) * width], result)
    return result


def kernel_grads(core, grad_ref, src_ref, base, stride, kept_ref, sent_ref):
    own = grad_ref.shape[1]
    cells = grad_ref.shape[0]
    turned = grad_ref[...].T
    moved = jnp.concatenate(
        [
            pltpu.roll(turned, cells - 1, 1).astype(BF16),
            turned.astype(BF16),
            pltpu.roll(turned, 1, 1).astype(BF16),
        ],
        axis=0,
    )
    for row in range(3):
        start = base + row * stride
        part = jnp.dot(moved, src_ref[start : start + cells, :], preferred_element_type=F32)
        for col in range(3):
            tap = 3 * row + col
            half = own // 2
            low = part[col * own : col * own + half, :]
            high = part[col * own + half : (col + 1) * own, :]
            kept_ref[tap] = jnp.where(core == 1, high, low)
            sent_ref[tap] = jnp.where(core == 1, low, high)


def prepare(scal, labels, flow, winner, taps, lines, *refs):
    layers = taps.shape[0]
    sends, sems = refs[:-1], refs[-1]
    copies = []
    for layer, send in enumerate(sends):
        half = send.shape[1]
        part = taps.at[layer, :, pl.ds(pl.multiple_of(scal[1] * half, half), half), :]
        copies.append(pltpu.make_async_copy(part, send, sems.at[layer]))
        copies[-1].start()
    height, width = labels.shape
    blocks = winner.shape[1]
    at = lax.broadcasted_iota(jnp.int32, (blocks, width), 1)
    block = lax.broadcasted_iota(jnp.int32, (blocks, width), 0)
    spread = ((at >= block * BLK) & (at < block * BLK + BLK)).astype(BF16)
    fields = [labels[...].astype(F32)]
    ids = [
        jnp.dot(winner[row : row + 1, :].astype(F32).astype(BF16), spread, preferred_element_type=F32)
        for row in range(height // BLK)
    ]
    fields.append(jnp.concatenate([jnp.broadcast_to(part, (BLK, width)) for part in ids], axis=0))
    for index in range(2):
        rest = flow[index]
        for _ in range(3):
            piece = rest.astype(BF16).astype(F32)
            fields.append(piece)
            rest = rest - piece
    for row in range(height):
        lines[row] = jnp.concatenate([field[row : row + 1] for field in fields], axis=0).astype(BF16)
    for copy in copies:
        copy.wait()


def first_layer(geom, scal, mid, top, bottom, tiles, *refs):
    taps = refs[:-7]
    padded, active, slope, mat, low, cen, high = refs[-7:]
    height, width, futs, layers = geom
    stride = width + SLOT
    halo = layers + 1
    col = scal[1]
    row_at = scal[2]
    row_count = scal[3]
    slots = height + 2 * halo
    lane = lax.broadcasted_iota(jnp.int32, tiles.shape[1:], 0)
    near = (lane < SLOT // 2).astype(jnp.int32) != col
    blank = jnp.zeros(tiles.shape[1:], BF16)
    padded[:SLOT, :] = jnp.where(near & (col == 1), tiles[0], blank)
    for row in range(slots):
        at = SLOT + row * stride
        if row < halo:
            source = top[row]
        elif row < halo + height:
            source = mid[row - halo]
        else:
            source = bottom[row - halo - height]
        padded[at : at + width, :] = source
        after = tiles[row + 1] if row + 1 < slots else blank
        padded[at + width : at + stride, :] = jnp.where(
            near, jnp.where(col == 1, after, tiles[row]), blank
        )
    forward_taps(0, scal, taps, mat)
    count = active.shape[0]
    convolve(padded, mat, low, cen, high, count, stride)
    spot = lax.broadcasted_iota(jnp.int32, (stride, active.shape[1]), 0)
    inside = (spot < width) | ((col == 0) & (spot < width + SLOT // 2)) | (
        (col == 1) & (spot >= width + SLOT // 2)
    )

    bump = ((spot >= width) & (col == 1)).astype(jnp.int32)

    def finish(at, size, keep):
        pre = combined(low, cen, high, at, size)
        sigma = jax.nn.sigmoid(pre)
        active[at : at + size, :] = jnp.where(keep, pre * sigma, 0.0).astype(BF16)
        return pre, sigma

    edge = halo - 1
    finish(0, SLOT, (col == 1) & (row_at * height - edge >= 0))
    for row in range(height + 2 * edge):
        at = SLOT + row * stride
        place = row_at * height + row - edge
        keep = inside & (bump + place >= 0) & (bump + place < row_count * height)
        pre, sigma = finish(at, stride, keep)
        if edge <= row < edge + height:
            mine = (row - edge) * width
            own_pre = own_part(pre[:width], scal[0], futs)
            own_sig = own_part(sigma[:width], scal[0], futs)
            slope[mine : mine + width, :] = own_sig * (1.0 + own_pre * (1.0 - own_sig))


def cell_data(scal, lines, above, below, tile, height, width):
    stride = width + SLOT
    count = height + 2
    core, row_at, row_count = scal[1], scal[2], scal[3]
    rows = [above[...]] + [lines[row] for row in range(height)] + [below[...]]
    blank = jnp.zeros(tile.shape[1:], F32)
    tiles = [blank] + [tile[row].astype(F32) for row in range(count)] + [blank]
    parts = []
    for row in range(count + 1):
        parts.append(jnp.where(core == 1, tiles[row + 1], tiles[row]))
        if row < count:
            parts.append(rows[row].astype(F32))
    flat = jnp.concatenate(parts, axis=1)
    place = lax.broadcasted_iota(jnp.int32, (8, flat.shape[1]), 1)
    line = jnp.full_like(place, -2)
    spot = place
    for row in range(count + 1):
        begin = row * stride
        line = jnp.where(place >= begin, row - 1, line)
        spot = jnp.where(place >= begin, place - (begin + SLOT), spot)
    main = spot >= 0
    right = (spot == -SLOT) & (core == 0)
    left = (spot == -1) & (core == 1)
    own = main & (line >= 0) & (line < height)
    line = line - right.astype(jnp.int32)
    at = row_at * height + line
    real = (at >= 0) & (at < row_count * height) & (line >= -1) & (line <= height)
    valid = real & (main | right | left)
    return (
        flat[0:1],
        flat[2:3] + flat[3:4] + flat[4:5],
        flat[5:6] + flat[6:7] + flat[7:8],
        flat[1:2],
        jnp.where(valid, 1.0, 0.0)[:1],
        jnp.where(own, 1.0, 0.0)[:1],
    )


def last_layer(
    geom, scale, scal, active, slope, padded, heads_w, lines, above, below, tile, *refs
):
    taps = refs[:-14]
    kept, sent, first_kept, first_sent, small = refs[-14:-9]
    mat, low, cen, high, out, pre_s, grad, own_grad, back_mat = refs[-9:]
    height, width, futs, layers = geom
    stride = width + SLOT
    count = grad.shape[0]
    forward_taps(layers - 1, scal, taps, mat)
    convolve(active, mat, low, cen, high, count, stride)
    for lo, size in pieces(count, 208):
        pre = combined(low, cen, high, lo, size)
        pre_s[lo : lo + size, :] = pre
        out[lo : lo + size, :] = (pre * jax.nn.sigmoid(pre)).astype(BF16)
    nfut = heads_w.shape[0] // 3
    heads = lax.dot_general(
        heads_w[...], out[...], (((1,), (1,)), ((), ())), preferred_element_type=F32
    )
    logit = heads[:nfut]
    target, flow_one, flow_two, picks, valid, own = cell_data(
        scal, lines, above, below, tile, height, width
    )
    first = heads[nfut : 2 * nfut] - flow_one
    second = heads[2 * nfut :] - flow_two
    future = lax.broadcasted_iota(jnp.int32, logit.shape, 0).astype(F32)
    mask = jnp.where(picks == future, valid, 0.0)
    cell = (
        jnp.maximum(logit, 0.0)
        + jnp.log1p(jnp.exp(-jnp.abs(logit)))
        - target * logit
        + 0.5 * (first * first + second * second)
    )
    loss = jnp.sum(jnp.where(mask * own > 0.0, cell, 0.0))
    picked = mask > 0.0
    grads = jnp.concatenate(
        [
            jnp.where(picked, (jax.nn.sigmoid(logit) - target) * scale, 0.0),
            jnp.where(picked, first * scale, 0.0),
            jnp.where(picked, second * scale, 0.0),
        ],
        axis=0,
    )
    mine = jnp.where(own > 0.0, grads, 0.0).astype(BF16)
    grads = grads.astype(BF16)
    by_head = jnp.dot(mine, out[...], preferred_element_type=F32)
    fut_here = nfut // futs
    lines = []
    for index in range(fut_here):
        for kind in range(3):
            at = kind * nfut + index
            line = by_head[at : at + 1, :]
            for part in range(1, futs):
                other = at + part * fut_here
                line = jnp.where(scal[0] == part, by_head[other : other + 1, :], line)
            lines.append(line)
    lines.append(jnp.broadcast_to(loss, (small.shape[0] - len(lines), small.shape[1])))
    small[...] = jnp.concatenate(lines, axis=0)
    up = lax.dot_general(
        grads, heads_w[...], (((0,), (0,)), ((), ())), preferred_element_type=F32
    )
    low[: count, :] = up
    own_grad[...] = jnp.zeros_like(own_grad)

    def back(lo, size):
        pre = pre_s[lo : lo + size, :]
        sigma = jax.nn.sigmoid(pre)
        value = (low[lo : lo + size, :] * (sigma * (1.0 + pre * (1.0 - sigma)))).astype(BF16)
        grad[lo : lo + size, :] = value
        return value

    back(0, SLOT)
    for row in range(height + 2):
        at = SLOT + row * stride
        value = back(at, stride)
        if 1 <= row <= height:
            mine_at = SLOT + (row - 1) * stride
            own_grad[mine_at : mine_at + width, :] = own_part(
                value[:width].astype(F32), scal[0], futs
            )
    kernel_grads(scal[1], own_grad, active, stride, stride, kept, sent)
    back_layer(
        geom, scal, grad, taps, slope, padded, first_kept, first_sent, back_mat, low, cen, high,
        own_grad,
    )


def back_layer(
    geom, scal, grad, taps, slope, padded, kept, sent, mat, low, cen, high, own_grad
):
    height, width, futs, layers = geom
    stride = width + SLOT
    channels = grad.shape[1]
    own = channels // futs
    count = SLOT + height * stride
    for tap in range(9):
        row, col = tap // 3, tap % 3
        mat[
            (2 - row) * channels : (3 - row) * channels, (2 - col) * own : (3 - col) * own
        ] = own_part(whole_tap(layers - 1, tap, scal, taps), scal[0], futs)
    low[:8, :own] = jnp.zeros((8, own), F32)
    high[8 + count : 16 + count, :own] = jnp.zeros((8, own), F32)
    for lo, size in pieces(count, 400):
        rows = jnp.concatenate(
            [grad[lo + row * stride : lo + row * stride + size, :] for row in range(3)], axis=1
        )
        part = jnp.dot(rows, mat[...], preferred_element_type=F32)
        for col, ref in enumerate((low, cen, high)):
            ref[8 + lo : 8 + lo + size, :own] = part[:, col * own : (col + 1) * own]
    own_grad[...] = jnp.zeros_like(own_grad)
    for row in range(height):
        at = SLOT + row * stride
        up = (
            low[7 + at : 7 + at + width, :own]
            + cen[8 + at : 8 + at + width, :own]
            + high[9 + at : 9 + at + width, :own]
        )
        value = (up * slope[row * width : (row + 1) * width, :]).astype(BF16)
        own_grad[at : at + width, :] = value.astype(F32)
    kernel_grads(scal[1], own_grad, padded, layers * stride, stride, kept, sent)


def tap_parts(taps, layer, send):
    if lax.axis_size("futures") != 2:
        return (lax.all_gather(taps[layer], "futures", axis=1, tiled=True),)
    got = swap(send, "futures")
    return (taps, got, swap(got, "cols"))


def tied(*blocks):
    return lax.optimization_barrier(blocks)


def tile_sums(last, first, small, core, row_at):
    bit = row_at & 1

    def over_cols(block, extra):
        kept, sent = block
        if extra is None:
            return kept + swap(sent, "cols"), None
        sent, extra = tied(sent, extra)
        got, more = tied(swap(sent, "cols"), swap(extra, "cols"))
        return kept + got, extra + more

    def over_pairs(block, extra):
        half = block.shape[1] // 2
        low, high = block[:, :half], block[:, half:]
        kept, sent = jnp.where(bit == 1, high, low), jnp.where(bit == 1, low, high)
        sent = rounded(sent).astype(BF16)
        if extra is None:
            return rounded(kept + swap(sent, "rows").astype(F32)), None
        sent, extra = tied(sent, extra)
        got, more = tied(swap(sent, "rows"), swap(extra, "rows"))
        return rounded(kept + got.astype(F32)), extra + more

    def over_ends(block, extra):
        sent = block.astype(BF16)
        if extra is None:
            return (block + swap(sent, "rows", 2).astype(F32)).astype(BF16), None
        sent, extra = tied(sent, extra)
        got, more = tied(swap(sent, "rows", 2), swap(extra, "rows", 2))
        return (block + got.astype(F32)).astype(BF16), extra + more

    for step in (over_cols, over_pairs, over_ends):
        last, small = step(last, small)
        first, _ = step(first, None)
    last, first = [ordered(bit == 1, block, swap(block, "rows"), 1) for block in (last, first)]
    last, first = [ordered(core == 1, block, swap(block, "cols"), 1) for block in (last, first)]
    return last.astype(F32), first.astype(F32), small


def rounded(value):
    return lax.reduce_precision(value, 8, 7)


def local(features, trunk_weights, head_weights, flow_target, labels, winner):
    own, height, width = features.shape
    layers, _, _, channels = trunk_weights.shape
    fut_total = head_weights.shape[0]
    futs = lax.axis_size("futures")
    fut_here = fut_total // futs
    rows_total = lax.axis_size("rows")
    fut = lax.axis_index("futures")
    core = lax.axis_index("cols")
    row_at = lax.axis_index("rows")
    cell_count = height * width * rows_total * lax.axis_size("cols")
    scale = 1.0 / math.sqrt(cell_count)
    halo = layers + 1
    stride = width + SLOT
    geom = (height, width, futs, layers)
    scal = jnp.stack([fut, core, row_at, jnp.int32(rows_total)]).astype(jnp.int32)

    shape = jax.ShapeDtypeStruct
    mine = jnp.transpose(features, (1, 2, 0))
    if futs == 2:
        theirs = swap(mine, "futures")
        mid = ordered(fut == 1, mine, theirs, 2)
    else:
        mid = lax.all_gather(mine, "futures", axis=2, tiled=True)
    lines, *sends = pl.pallas_call(
        prepare,
        out_shape=(shape((height, 8, width), BF16),)
        + (shape((9, own // 2, channels), BF16),) * layers,
        in_specs=[SMEM] + [VMEM] * 3 + [pl.BlockSpec(memory_space=pl.ANY)],
        out_specs=(VMEM,) * (1 + layers),
        scratch_shapes=[pltpu.SemaphoreType.DMA((layers,))],
        compiler_params=PARAMS,
        name="prepare",
    )(scal, labels, flow_target, winner, trunk_weights)
    taps = [tap_parts(trunk_weights, layer, sends[layer]) for layer in range(layers)]

    def with_line(block, line):
        line = jnp.pad(line, ((0, 0), (0, channels - width)))
        return jnp.concatenate([block.reshape(-1, channels), line], axis=0)

    top = shift(with_line(mid[-halo:], lines[-1]), "rows", 1)
    bottom = shift(with_line(mid[:halo], lines[0]), "rows", -1)
    rows = halo * width
    above, below = top[rows:, :width], bottom[rows:, :width]
    top = top[:rows].reshape(halo, width, channels)
    bottom = bottom[:rows].reshape(halo, width, channels)

    def edge_of(block):
        return jnp.where(core == 0, block[..., -SLOT:, :], block[..., :SLOT, :])

    tiles = swap(
        jnp.concatenate([edge_of(top), edge_of(mid), edge_of(bottom)], axis=0), "cols"
    )
    line_rows = jnp.concatenate([above[None], lines, below[None]], axis=0)
    tile = swap(
        jnp.where(core == 0, line_rows[:, :, -SLOT:], line_rows[:, :, :SLOT]), "cols"
    )
    heads_w = jnp.transpose(head_weights, (1, 0, 2)).reshape(3 * fut_total, channels)

    def cells(rows):
        return SLOT + rows * stride

    first_cells = cells(height + 4)
    last_cells = cells(height + 2)
    own_cells = -(-cells(height) // 128) * 128
    padded, active, slope = pl.pallas_call(
        functools.partial(first_layer, geom),
        out_shape=(
            shape((cells(height + 6), channels), BF16),
            shape((first_cells, channels), BF16),
            shape((height * width, own), F32),
        ),
        in_specs=[SMEM] + [VMEM] * (4 + len(taps[0])),
        out_specs=(VMEM,) * 3,
        scratch_shapes=[pltpu.VMEM((3 * channels, 3 * channels), BF16)]
        + [pltpu.VMEM((first_cells + 16, channels), F32)] * 3,
        compiler_params=PARAMS,
        name="first_layer",
    )(scal, mid, top, bottom, tiles, *taps[0])

    half = shape((9, own // 2, channels), F32)
    kept, sent, first_kept, first_sent, small = pl.pallas_call(
        functools.partial(last_layer, geom, scale),
        out_shape=(half, half, half, half, shape((-(-(3 * fut_here + 1) // 8) * 8, channels), F32)),
        in_specs=[SMEM] + [VMEM] * (8 + len(taps[-1])),
        out_specs=(VMEM,) * 5,
        scratch_shapes=[pltpu.VMEM((3 * channels, 3 * channels), BF16)]
        + [pltpu.VMEM((last_cells + 16, channels), F32)] * 3
        + [
            pltpu.VMEM((last_cells, channels), BF16),
            pltpu.VMEM((last_cells, channels), F32),
            pltpu.VMEM((last_cells, channels), BF16),
            pltpu.VMEM((own_cells, own), F32),
            pltpu.VMEM((3 * channels, 3 * own), BF16),
        ],
        compiler_params=PARAMS,
        name="last_layer",
    )(scal, active, slope, padded, heads_w, lines, above, below, tile, *taps[-1])

    if rows_total == 4:
        last_sum, first_sum, small = tile_sums(
            (kept, sent), (first_kept, first_sent), small, core, row_at
        )
    else:
        last_sum, first_sum, small = lax.psum(
            (
                ordered(core == 1, kept, sent, 1),
                ordered(core == 1, first_kept, first_sent, 1),
                small,
            ),
            ("rows", "cols"),
        )
    trunk_grad = jnp.stack([first_sum, last_sum])
    head_grad = small[: 3 * fut_here].reshape(fut_here, 3, channels)
    total = small[3 * fut_here, :1] / cell_count
    return (total, trunk_grad, head_grad)


def solution(mesh):
    placed = (
        P("futures", ("groups", "rows"), "cols"),
        P(None, None, "futures", None),
        P(),
        P(None, ("groups", "rows"), "cols"),
        P(("groups", "rows"), "cols"),
        P(("groups", "rows"), "cols"),
    )
    return jax.shard_map(
        local,
        mesh=mesh,
        in_specs=placed,
        out_specs=(P("groups"), P("groups", None, "futures", None), P("futures", "groups", None)),
        check_vma=False,
    )
```

time: 89.6 us -> 77.5 us (0.86)
  starting transfers between devices: 30.8 us -> 21.2 us
  waiting for transfers between devices: 28.9 us -> 32.4 us
  other arithmetic: 7.06 us -> 4.06 us
  local copies, waits for them, and re-layouts: 8.45 us -> 5.64 us
    ppermute x20, waiting for transfers between devices: 21.4 us -> 32.4 us  [swap(): return lax.ppermute(block, axis, [(i, i ^ distance) for i in range(count)])]
    ppermute x4 -> x2, waiting for transfers between devices: 7.51 us -> 0.01 us  [shift(): return lax.ppermute(block, axis, pairs)]
    ppermute x4 -> x2, starting transfers between devices: 11.3 us -> 4.92 us  [shift(): return lax.ppermute(block, axis, pairs)]
    ppermute x20, starting transfers between devices: 19.4 us -> 16.3 us  [swap(): return lax.ppermute(block, axis, [(i, i ^ distance) for i in range(count)])]
    select_n x9 -> x3, other arithmetic: 2.01 us -> 0.11 us  [the longest x1 0.08 us: local(): jnp.where(core == 0, line_rows[:, :, -SLOT:], line_rows[:, :, :SLOT])]
    squeeze x1, local copies, waits for them, and re-layouts: 1.32 us -> 0.01 us  [local(): bottom = shift(with_line(mid[:halo], lines[0]), 'rows', -1)]
    unnamed x30 -> x14, local copies, waits for them, and re-layouts: 5.34 us -> 5.08 us
  transfers between devices with their start and end apart: 24 -> 22, of which waited for: 13 -> 11; matrix products, arithmetic and copies ran while one was open for 8% -> 4% of each run, Pallas kernels for 3% -> 5%
where the time goes in v2:
time: 77.5 us; the launch traced here: 77.1 us
  waiting for transfers between devices  32.4 us (42%)
  starting transfers between devices  21.2 us (27%)
  Pallas kernels  11 us (14%)
  local copies, waits for them, and re-layouts  5.64 us (7%)
  other arithmetic  4.06 us (5%)
  between operations  2.74 us (4%)
    ppermute x20, waiting for transfers between devices, swap(): return lax.ppermute(block, axis, [(i, i ^ distance) for i in range(count)])  32.4 us
    ppermute x20, starting transfers between devices, swap(): return lax.ppermute(block, axis, [(i, i ^ distance) for i in range(count)])  16.3 us
    pallas_call x1, Pallas kernels, local(): pl.pallas_call(functools.partial(last_layer, geom, scale), out_shape=(hal...  7.09 us
    unnamed x14, local copies, waits for them, and re-layouts  5.08 us
    ppermute x2, starting transfers between devices, shift(): return lax.ppermute(block, axis, pairs)  4.92 us
    pallas_call x1, Pallas kernels, local(): pl.pallas_call(functools.partial(first_layer, geom), out_shape=(shape((ce...  3.15 us
    another operation x1, other arithmetic, local(): trunk_grad = jnp.stack([first_sum, last_sum])  1.66 us
  transfers between devices with their start and end apart: 22, of which 11 were waited for; matrix products, arithmetic and copies ran while one was open for 4% of the time, Pallas kernels for 5%

profile of v2, /device:TPU:0, one launch (start us, length us, event | category | flops | bytes accessed | tf_op | source)
XLA Modules:
  0.0 77.1 jit_solution(6271017327058129593)
XLA Ops:
  0.6 1.2 %copy.11 = bf16[128,8,128]{0,2,1:T(8,128)(2,1)S(1)} copy(bf16[128,8,128]{2,1,0:T(8,128)(2,1)} %param.6) | data formatting | bytes 524288 | tf_op args[0]
  1.8 3.0 %collective-permute-start = (bf16[8,128,128]{2,1,0:T(8,128)(2,1)S(1)}, bf16[8,128,128]{2,1,0:T(8,128)(2,1)S(1)}, u32[]{:S(2)}, u32[]{:S(2)}) collective-permute-start(bf16[8,128,128]{2,1,0:T(8,128)(2,1)S(1)} %bitcast.36), channel_id=1, source_target_pairs={{0,1},{1,0},{2,3},{3,2},{4,5},{5,4},{6,7},{7,6},{8,9},{9,8},{10,11... | collective-permute-start | bytes 786440 | tf_op jit(solution)/shard_map/ppermute | solution.py:22
  4.8 0.1 pad_add_fusion.scal
  4.9 1.3 %copy-done = bf16[2,9,128,256]{3,2,1,0:T(8,128)(2,1)S(1)} copy-done((bf16[2,9,128,256]{3,2,1,0:T(8,128)(2,1)S(1)}, bf16[2,9,128,256]{3,2,1,0:T(8,128)(2,1)}, u32[]{:S(2)}) %copy-start) | copy-done | bytes 1179672
  6.2 0.7 copy-done.3
  6.8 0.7 copy-done.4
  7.5 0.7 copy-done.5
  8.2 0.7 prepare.1
  8.9 0.1 collective-permute-start.4
  9.0 2.0 %collective-permute-start.7 = (bf16[9,64,256]{2,1,0:T(8,128)(2,1)S(1)}, bf16[9,64,256]{2,1,0:T(8,128)(2,1)S(1)}, u32[]{:S(2)}, u32[]{:S(2)}) collective-permute-start(bf16[9,64,256]{2,1,0:T(8,128)(2,1)S(1)} %get-tuple-element.31), channel_id=1, source_target_pairs={{0,1},{1,0},{2,3},{3,2},{4,5},{5,4},{6,7},{7,6},{8,9},{9,8},{10,11... | collective-permute-start | bytes 884744 | tf_op jit(solution)/shard_map/ppermute | solution.py:22
  11.0 0.5 collective-permute-done
  11.6 0.0 copy-start.1
  11.6 0.1 fusion.5
  11.6 3.6 %collective-permute-start.1 = (bf16[392,256]{1,0:T(8,128)(2,1)S(1)}, bf16[392,256]{1,0:T(8,128)(2,1)S(1)}, u32[]{:S(2)}, u32[]{:S(2)}) collective-permute-start(bf16[392,256]{1,0:T(8,128)(2,1)S(1)} %fusion.2), channel_id=1, source_target_pairs={{0,4},{4,8},{8,12},{1,5},{5,9},{9,13},{2,6},{6,10},{10,14},{3,7},{... | collective-permute-start | bytes 602120 | tf_op jit(solution)/shard_map/ppermute | solution.py:28
  15.3 1.3 %collective-permute-start.2 = (bf16[392,256]{1,0:T(8,128)(2,1)S(1)}, bf16[392,256]{1,0:T(8,128)(2,1)S(1)}, u32[]{:S(2)}, u32[]{:S(2)}) collective-permute-start(bf16[392,256]{1,0:T(8,128)(2,1)S(1)} %fusion.3), channel_id=1, source_target_pairs={{4,0},{8,4},{12,8},{5,1},{9,5},{13,9},{6,2},{10,6},{14,10},{7,3},{... | collective-permute-start | bytes 602120 | tf_op jit(solution)/shard_map/ppermute | solution.py:28
  16.6 2.3 %collective-permute-done.4.refs_1_ = bf16[9,64,256]{2,1,0:T(8,128)(2,1)S(1)} collective-permute-done((bf16[9,64,256]{2,1,0:T(8,128)(2,1)S(1)}, bf16[9,64,256]{2,1,0:T(8,128)(2,1)S(1)}, u32[]{:S(2)}, u32[]{:S(2)}) %collective-permute-start.4) | collective-permute-done | bytes 294944 | tf_op jit(solution)/shard_map/ppermute | solution.py:22
  18.9 4.9 %collective-permute-done.7.refs_1_ = bf16[9,64,256]{2,1,0:T(8,128)(2,1)S(1)} collective-permute-done((bf16[9,64,256]{2,1,0:T(8,128)(2,1)S(1)}, bf16[9,64,256]{2,1,0:T(8,128)(2,1)S(1)}, u32[]{:S(2)}, u32[]{:S(2)}) %collective-permute-start.7) | collective-permute-done | bytes 294944 | tf_op jit(solution)/shard_map/ppermute | solution.py:22
  23.8 0.0 collective-permute-start.8
  23.8 0.1 slice_select_fusion.2
  23.9 0.5 collective-permute-start.6
  24.4 0.0 copy-start.2
  24.5 0.1 collective-permute-start.3
  24.6 0.1 pad_maximum_fusion.mid
  24.7 1.2 %collective-permute-done.3.tiles = bf16[14,16,256]{2,1,0:T(8,128)(2,1)S(1)} collective-permute-done((bf16[14,16,256]{2,1,0:T(8,128)(2,1)S(1)}, bf16[14,16,256]{2,1,0:T(8,128)(2,1)S(1)}, u32[]{:S(2)}, u32[]{:S(2)}) %collective-permute-start.3) | collective-permute-done | bytes 114720 | tf_op jit(solution)/shard_map/ppermute | solution.py:22
  25.9 0.0 collective-permute-done.5.refs_2_
  25.9 3.1 %first_layer.1 = (bf16[2032,256]{1,0:T(8,128)(2,1)S(1)}, bf16[1744,256]{1,0:T(8,128)(2,1)S(1)}, f32[1024,128]{1,0:T(8,128)S(1)}) custom-call(s32[4]{0:T(128)S(1)} %pad_add_fusion.scal, bf16[8,128,256]{2,1,0:T(8,128)(2,1)S(1)} %pad_maximum_fusion.mid, bf16[3,128,256]{2,1,0:T(8,128)(2,1)S(1)} %bitcast.32, bf16[3,128,256]{2,1,0:T(8,128)(2,1)S(1)} %bitcast.34, ...), custom_call_target="tpu_custom_call" | custom-call | tf_op jit(solution)/shard_map/first_layer/pallas_call | solution.py:488
  29.1 0.0 collective-permute-done.8.refs_2_
  29.1 7.1 %last_layer.1 = (f32[9,64,256]{2,1,0:T(8,128)S(1)}, f32[9,64,256]{2,1,0:T(8,128)S(1)}, f32[9,64,256]{2,1,0:T(8,128)S(1)}, f32[9,64,256]{2,1,0:T(8,128)S(1)}, f32[16,256]{1,0:T(8,128)S(1)}) custom-call(s32[4]{0:T(128)S(1)} %pad_add_fusion.scal, bf16[1744,256]{1,0:T(8,128)(2,1)S(1)} %get-tuple-element.28.active, f32[1024,128]{1,0:T(8,128)S(1)} %get-tuple-element.29.slope, ...), custom_call_target="tpu_custom_call" | custom-call | tf_op jit(solution)/shard_map/last_layer/pallas_call | solution.py:504
  36.2 0.2 collective-permute-start.9
  36.4 0.4 collective-permute-start.15
  36.8 0.2 collective-permute-start.10
  36.9 2.2 %collective-permute-done.10 = f32[16,256]{1,0:T(8,128)S(1)} collective-permute-done((f32[16,256]{1,0:T(8,128)S(1)}, f32[16,256]{1,0:T(8,128)S(1)}, u32[]{:S(2)}, u32[]{:S(2)}) %collective-permute-start.10) | collective-permute-done | bytes 16416 | tf_op jit(solution)/shard_map/ppermute | solution.py:22
  39.1 0.0 collective-permute-done.9
  39.2 1.1 %add.31 = f32[9,64,256]{2,1,0:T(8,128)S(1)} add(f32[9,64,256]{2,1,0:T(8,128)S(1)} %get-tuple-element.32, f32[9,64,256]{2,1,0:T(8,128)} %collective-permute-done.9) | non-fusion elementwise | flops 147456 | bytes 1769472 | tf_op jit(solution)/shard_map/add | solution.py:390
  40.3 1.8 %collective-permute-start.12 = (f32[16,256]{1,0:T(8,128)S(1)}, f32[16,256]{1,0:T(8,128)S(1)}, u32[]{:S(2)}, u32[]{:S(2)}) collective-permute-start(f32[16,256]{1,0:T(8,128)S(1)} %add.32), channel_id=1, source_target_pairs={{0,4},{4,0},{8,12},{12,8},{1,5},{5,1},{9,13},{13,9},{2,6},{6,2},{1... | collective-permute-start | bytes 49160 | tf_op jit(solution)/shard_map/ppermute | solution.py:22
  42.2 0.2 collective-permute-start.11
  42.4 0.0 collective-permute-done.15
  42.4 0.1 add.36
  42.6 1.8 %collective-permute-start.16 = (bf16[9,32,256]{2,1,0:T(8,128)(2,1)S(1)}, bf16[9,32,256]{2,1,0:T(8,128)(2,1)S(1)}, u32[]{:S(2)}, u32[]{:S(2)}) collective-permute-start(bf16[9,32,256]{2,1,0:T(8,128)(2,1)S(1)} %reduce-precision_convert_fusion), channel_id=1, source_target_pairs={{0,4},{4,0},{8,12},{12,8},{1,5},{5,1},{9,13},{13,9},{2,6},{6,2},{1... | collective-permute-start | bytes 442376 | tf_op jit(solution)/shard_map/ppermute | solution.py:22
  44.4 0.0 collective-permute-done.12
  44.4 4.5 %collective-permute-done.11 = bf16[9,32,256]{2,1,0:T(8,128)(2,1)S(1)} collective-permute-done((bf16[9,32,256]{2,1,0:T(8,128)(2,1)S(1)}, bf16[9,32,256]{2,1,0:T(8,128)(2,1)S(1)}, u32[]{:S(2)}, u32[]{:S(2)}) %collective-permute-start.11) | collective-permute-done | bytes 147488 | tf_op jit(solution)/shard_map/ppermute | solution.py:22
  48.9 0.1 fusion.9
  49.0 2.7 %collective-permute-start.14 = (f32[16,256]{1,0:T(8,128)S(1)}, f32[16,256]{1,0:T(8,128)S(1)}, u32[]{:S(2)}, u32[]{:S(2)}) collective-permute-start(f32[16,256]{1,0:T(8,128)S(1)} %add.34), channel_id=1, source_target_pairs={{0,8},{4,12},{8,0},{12,4},{1,9},{5,13},{9,1},{13,5},{2,10},{6,14},... | collective-permute-start | bytes 49160 | tf_op jit(solution)/shard_map/ppermute | solution.py:22
  51.7 0.3 collective-permute-start.13
  52.0 0.0 collective-permute-done.16
  52.0 0.1 fusion.10
  52.1 2.7 %collective-permute-start.17 = (bf16[9,32,256]{2,1,0:T(8,128)(2,1)S(1)}, bf16[9,32,256]{2,1,0:T(8,128)(2,1)S(1)}, u32[]{:S(2)}, u32[]{:S(2)}) collective-permute-start(bf16[9,32,256]{2,1,0:T(8,128)(2,1)S(1)} %fusion.10), channel_id=1, source_target_pairs={{0,8},{4,12},{8,0},{12,4},{1,9},{5,13},{9,1},{13,5},{2,10},{6,14},... | collective-permute-start | bytes 442376 | tf_op jit(solution)/shard_map/ppermute | solution.py:22
  54.7 5.4 %collective-permute-done.14 = f32[16,256]{1,0:T(8,128)S(1)} collective-permute-done((f32[16,256]{1,0:T(8,128)S(1)}, f32[16,256]{1,0:T(8,128)S(1)}, u32[]{:S(2)}, u32[]{:S(2)}) %collective-permute-start.14) | collective-permute-done | bytes 16416 | tf_op jit(solution)/shard_map/ppermute | solution.py:22
  60.1 3.2 %collective-permute-done.13 = bf16[9,32,256]{2,1,0:T(8,128)(2,1)S(1)} collective-permute-done((bf16[9,32,256]{2,1,0:T(8,128)(2,1)S(1)}, bf16[9,32,256]{2,1,0:T(8,128)(2,1)S(1)}, u32[]{:S(2)}, u32[]{:S(2)}) %collective-permute-start.13) | collective-permute-done | bytes 147488 | tf_op jit(solution)/shard_map/ppermute | solution.py:22
  63.2 0.1 add_convert_fusion
  63.3 0.1 collective-permute-start.20
  63.4 2.4 %collective-permute-done.17 = bf16[9,32,256]{2,1,0:T(8,128)(2,1)S(1)} collective-permute-done((bf16[9,32,256]{2,1,0:T(8,128)(2,1)S(1)}, bf16[9,32,256]{2,1,0:T(8,128)(2,1)S(1)}, u32[]{:S(2)}, u32[]{:S(2)}) %collective-permute-start.17) | collective-permute-done | bytes 147488 | tf_op jit(solution)/shard_map/ppermute | solution.py:22
  65.9 0.1 add_convert_fusion.1
  66.0 0.1 collective-permute-start.18
  66.0 3.8 %collective-permute-done.20 = bf16[9,32,256]{2,1,0:T(8,128)(2,1)S(1)} collective-permute-done((bf16[9,32,256]{2,1,0:T(8,128)(2,1)S(1)}, bf16[9,32,256]{2,1,0:T(8,128)(2,1)S(1)}, u32[]{:S(2)}, u32[]{:S(2)}) %collective-permute-start.20) | collective-permute-done | bytes 147488 | tf_op jit(solution)/shard_map/ppermute | solution.py:22
  69.9 0.1 collective-permute-start.21
  70.0 2.1 %collective-permute-done.18 = bf16[9,32,256]{2,1,0:T(8,128)(2,1)S(1)} collective-permute-done((bf16[9,32,256]{2,1,0:T(8,128)(2,1)S(1)}, bf16[9,32,256]{2,1,0:T(8,128)(2,1)S(1)}, u32[]{:S(2)}, u32[]{:S(2)}) %collective-permute-start.18) | collective-permute-done | bytes 147488 | tf_op jit(solution)/shard_map/ppermute | solution.py:22
  72.1 0.1 collective-permute-start.19
  72.2 0.5 slice.108
  72.8 0.6 copy.12
  74.0 0.1 select_bitcast_fusion.1
  74.1 0.0 collective-permute-done.19
  74.2 0.1 select_bitcast_fusion.3
  74.3 1.7 %maximum_convert_fusion = f32[2,9,128,256]{3,2,1,0:T(8,128)} fusion(bf16[1,9,64,256]{3,2,1,0:T(8,128)(2,1)S(1)} %get-tuple-element.58, bf16[1,9,64,256]{3,2,1,0:T(8,128)(2,1)S(1)} %get-tuple-element.57, bf16[1,9,64,256]{3,2,1,0:T(8,128)(2,1)S(1)} %get-tuple-element.56, bf16[1,9,64,256]{3,2,1,0:T(8,128)(2,1)S(1)} %get-tuple-element.55), kind=kLoop, calls=%fused_computation | loop fusion | flops 4718592 | bytes 3538944 | tf_op jit(solution)/shard_map/stack | solution.py:535
  (33 shorter events, 0.4 us)
Async XLA Ops:
  1.8 9.7 %collective-permute-start = (bf16[8,128,128]{2,1,0:T(8,128)(2,1)S(1)}, bf16[8,128,128]{2,1,0:T(8,128)(2,1)S(1)}, u32[]{:S(2)}, u32[]{:S(2)}) collective-permute-start(bf16[8,128,128]{2,1,0:T(8,128)(2,1)S(1)} %bitcast.36), channel_id=1, source_target_pairs={{0,1},{1,0},{2,3},{3,2},{4,5},{5,4},{6,7},{7,6},{8,9},{9,8},{10,11... | collective-permute-start | bytes 786440 | tf_op jit(solution)/shard_map/ppermute | solution.py:22
  4.9 1.3 %copy-start = (bf16[2,9,128,256]{3,2,1,0:T(8,128)(2,1)S(1)}, bf16[2,9,128,256]{3,2,1,0:T(8,128)(2,1)}, u32[]{:S(2)}) copy-start(bf16[2,9,128,256]{3,2,1,0:T(8,128)(2,1)} %refs_0_.3) | copy-start | bytes 3538948
  6.1 0.7 copy-start.3
  6.8 0.7 copy-start.4
  7.5 0.7 copy-start.5
  8.9 10.0 %collective-permute-start.4 = (bf16[9,64,256]{2,1,0:T(8,128)(2,1)S(1)}, bf16[9,64,256]{2,1,0:T(8,128)(2,1)S(1)}, u32[]{:S(2)}, u32[]{:S(2)}) collective-permute-start(bf16[9,64,256]{2,1,0:T(8,128)(2,1)S(1)} %get-tuple-element.27), channel_id=1, source_target_pairs={{0,1},{1,0},{2,3},{3,2},{4,5},{5,4},{6,7},{7,6},{8,9},{9,8},{10,11... | collective-permute-start | bytes 884744 | tf_op jit(solution)/shard_map/ppermute | solution.py:22
  9.0 14.8 %collective-permute-start.7 = (bf16[9,64,256]{2,1,0:T(8,128)(2,1)S(1)}, bf16[9,64,256]{2,1,0:T(8,128)(2,1)S(1)}, u32[]{:S(2)}, u32[]{:S(2)}) collective-permute-start(bf16[9,64,256]{2,1,0:T(8,128)(2,1)S(1)} %get-tuple-element.31), channel_id=1, source_target_pairs={{0,1},{1,0},{2,3},{3,2},{4,5},{5,4},{6,7},{7,6},{8,9},{9,8},{10,11... | collective-permute-start | bytes 884744 | tf_op jit(solution)/shard_map/ppermute | solution.py:22
  11.6 14.4 %copy-start.1 = (bf16[2,9,128,256]{3,2,1,0:T(8,128)(2,1)S(1)}, bf16[2,9,128,256]{3,2,1,0:T(8,128)(2,1)}, u32[]{:S(2)}) copy-start(bf16[2,9,128,256]{3,2,1,0:T(8,128)(2,1)} %refs_0_.3) | copy-start | bytes 3538948
  11.6 12.2 %collective-permute-start.1 = (bf16[392,256]{1,0:T(8,128)(2,1)S(1)}, bf16[392,256]{1,0:T(8,128)(2,1)S(1)}, u32[]{:S(2)}, u32[]{:S(2)}) collective-permute-start(bf16[392,256]{1,0:T(8,128)(2,1)S(1)} %fusion.2), channel_id=1, source_target_pairs={{0,4},{4,8},{8,12},{1,5},{5,9},{9,13},{2,6},{6,10},{10,14},{3,7},{... | collective-permute-start | bytes 602120 | tf_op jit(solution)/shard_map/ppermute | solution.py:28
  15.3 8.5 %collective-permute-start.2 = (bf16[392,256]{1,0:T(8,128)(2,1)S(1)}, bf16[392,256]{1,0:T(8,128)(2,1)S(1)}, u32[]{:S(2)}, u32[]{:S(2)}) collective-permute-start(bf16[392,256]{1,0:T(8,128)(2,1)S(1)} %fusion.3), channel_id=1, source_target_pairs={{4,0},{8,4},{12,8},{5,1},{9,5},{13,9},{6,2},{10,6},{14,10},{7,3},{... | collective-permute-start | bytes 602120 | tf_op jit(solution)/shard_map/ppermute | solution.py:28
  18.9 7.0 %collective-permute-start.5 = (bf16[9,64,256]{2,1,0:T(8,128)(2,1)S(1)}, bf16[9,64,256]{2,1,0:T(8,128)(2,1)S(1)}, u32[]{:S(2)}, u32[]{:S(2)}) collective-permute-start(bf16[9,64,256]{2,1,0:T(8,128)(2,1)S(1)} %collective-permute-done.4.refs_1_), channel_id=1, source_target_pairs={{0,2},{2,0},{1,3},{3,1},{4,6},{6,4},{5,7},{7,5},{8,10},{10,8},{9,1... | collective-permute-start | bytes 884744 | tf_op jit(solution)/shard_map/ppermute | solution.py:22
  23.8 5.3 %collective-permute-start.8 = (bf16[9,64,256]{2,1,0:T(8,128)(2,1)S(1)}, bf16[9,64,256]{2,1,0:T(8,128)(2,1)S(1)}, u32[]{:S(2)}, u32[]{:S(2)}) collective-permute-start(bf16[9,64,256]{2,1,0:T(8,128)(2,1)S(1)} %collective-permute-done.7.refs_1_), channel_id=1, source_target_pairs={{0,2},{2,0},{1,3},{3,1},{4,6},{6,4},{5,7},{7,5},{8,10},{10,8},{9,1... | collective-permute-start | bytes 884744 | tf_op jit(solution)/shard_map/ppermute | solution.py:22
  23.9 5.2 %collective-permute-start.6 = (bf16[10,8,16]{2,1,0:T(8,128)(2,1)S(1)}, bf16[10,8,16]{2,1,0:T(8,128)(2,1)S(1)}, u32[]{:S(2)}, u32[]{:S(2)}) collective-permute-start(bf16[10,8,16]{2,1,0:T(8,128)(2,1)S(1)} %slice_select_fusion.2), channel_id=1, source_target_pairs={{0,2},{2,0},{1,3},{3,1},{4,6},{6,4},{5,7},{7,5},{8,10},{10,8},{9,1... | collective-permute-start | bytes 7688 | tf_op jit(solution)/shard_map/ppermute | solution.py:22
  24.4 4.7 %copy-start.2 = (bf16[8,3,256]{2,0,1:T(8,128)(2,1)S(1)}, bf16[8,3,256]{2,0,1:T(8,128)(2,1)}, u32[]{:S(2)}) copy-start(bf16[8,3,256]{2,0,1:T(8,128)(2,1)} %param.8) | copy-start | bytes 36868
  24.5 1.4 %collective-permute-start.3 = (bf16[14,16,256]{2,1,0:T(8,128)(2,1)S(1)}, bf16[14,16,256]{2,1,0:T(8,128)(2,1)S(1)}, u32[]{:S(2)}, u32[]{:S(2)}) collective-permute-start(bf16[14,16,256]{2,1,0:T(8,128)(2,1)S(1)} %pad_maximum_fusion.3), channel_id=1, source_target_pairs={{0,2},{2,0},{1,3},{3,1},{4,6},{6,4},{5,7},{7,5},{8,10},{10,8},{9,1... | collective-permute-start | bytes 344072 | tf_op jit(solution)/shard_map/ppermute | solution.py:22
  36.2 2.9 %collective-permute-start.9 = (f32[9,64,256]{2,1,0:T(8,128)S(1)}, f32[9,64,256]{2,1,0:T(8,128)}, u32[]{:S(2)}, u32[]{:S(2)}) collective-permute-start(f32[9,64,256]{2,1,0:T(8,128)S(1)} %get-tuple-element.35), channel_id=1, source_target_pairs={{0,2},{2,0},{1,3},{3,1},{4,6},{6,4},{5,7},{7,5},{8,10},{10,8},{9,1... | collective-permute-start | bytes 1769480 | tf_op jit(solution)/shard_map/ppermute | solution.py:22
  36.4 6.0 %collective-permute-start.15 = (f32[9,64,256]{2,1,0:T(8,128)S(1)}, f32[9,64,256]{2,1,0:T(8,128)S(1)}, u32[]{:S(2)}, u32[]{:S(2)}) collective-permute-start(f32[9,64,256]{2,1,0:T(8,128)S(1)} %get-tuple-element.47), channel_id=1, source_target_pairs={{0,2},{2,0},{1,3},{3,1},{4,6},{6,4},{5,7},{7,5},{8,10},{10,8},{9,1... | collective-permute-start | bytes 1769480 | tf_op jit(solution)/shard_map/ppermute | solution.py:22
  36.8 2.4 %collective-permute-start.10 = (f32[16,256]{1,0:T(8,128)S(1)}, f32[16,256]{1,0:T(8,128)S(1)}, u32[]{:S(2)}, u32[]{:S(2)}) collective-permute-start(f32[16,256]{1,0:T(8,128)S(1)} %get-tuple-element.36), channel_id=1, source_target_pairs={{0,2},{2,0},{1,3},{3,1},{4,6},{6,4},{5,7},{7,5},{8,10},{10,8},{9,1... | collective-permute-start | bytes 49160 | tf_op jit(solution)/shard_map/ppermute | solution.py:22
  40.3 4.1 %collective-permute-start.12 = (f32[16,256]{1,0:T(8,128)S(1)}, f32[16,256]{1,0:T(8,128)S(1)}, u32[]{:S(2)}, u32[]{:S(2)}) collective-permute-start(f32[16,256]{1,0:T(8,128)S(1)} %add.32), channel_id=1, source_target_pairs={{0,4},{4,0},{8,12},{12,8},{1,5},{5,1},{9,13},{13,9},{2,6},{6,2},{1... | collective-permute-start | bytes 49160 | tf_op jit(solution)/shard_map/ppermute | solution.py:22
  42.2 6.7 %collective-permute-start.11 = (bf16[9,32,256]{2,1,0:T(8,128)(2,1)S(1)}, bf16[9,32,256]{2,1,0:T(8,128)(2,1)S(1)}, u32[]{:S(2)}, u32[]{:S(2)}) collective-permute-start(bf16[9,32,256]{2,1,0:T(8,128)(2,1)S(1)} %reduce-precision_convert_fusion.1), channel_id=1, source_target_pairs={{0,4},{4,0},{8,12},{12,8},{1,5},{5,1},{9,13},{13,9},{2,6},{6,2},{1... | collective-permute-start | bytes 442376 | tf_op jit(solution)/shard_map/ppermute | solution.py:22
  42.6 9.4 %collective-permute-start.16 = (bf16[9,32,256]{2,1,0:T(8,128)(2,1)S(1)}, bf16[9,32,256]{2,1,0:T(8,128)(2,1)S(1)}, u32[]{:S(2)}, u32[]{:S(2)}) collective-permute-start(bf16[9,32,256]{2,1,0:T(8,128)(2,1)S(1)} %reduce-precision_convert_fusion), channel_id=1, source_target_pairs={{0,4},{4,0},{8,12},{12,8},{1,5},{5,1},{9,13},{13,9},{2,6},{6,2},{1... | collective-permute-start | bytes 442376 | tf_op jit(solution)/shard_map/ppermute | solution.py:22
  49.0 11.1 %collective-permute-start.14 = (f32[16,256]{1,0:T(8,128)S(1)}, f32[16,256]{1,0:T(8,128)S(1)}, u32[]{:S(2)}, u32[]{:S(2)}) collective-permute-start(f32[16,256]{1,0:T(8,128)S(1)} %add.34), channel_id=1, source_target_pairs={{0,8},{4,12},{8,0},{12,4},{1,9},{5,13},{9,1},{13,5},{2,10},{6,14},... | collective-permute-start | bytes 49160 | tf_op jit(solution)/shard_map/ppermute | solution.py:22
  51.7 11.6 %collective-permute-start.13 = (bf16[9,32,256]{2,1,0:T(8,128)(2,1)S(1)}, bf16[9,32,256]{2,1,0:T(8,128)(2,1)S(1)}, u32[]{:S(2)}, u32[]{:S(2)}) collective-permute-start(bf16[9,32,256]{2,1,0:T(8,128)(2,1)S(1)} %fusion.9), channel_id=1, source_target_pairs={{0,8},{4,12},{8,0},{12,4},{1,9},{5,13},{9,1},{13,5},{2,10},{6,14},... | collective-permute-start | bytes 442376 | tf_op jit(solution)/shard_map/ppermute | solution.py:22
  52.1 13.8 %collective-permute-start.17 = (bf16[9,32,256]{2,1,0:T(8,128)(2,1)S(1)}, bf16[9,32,256]{2,1,0:T(8,128)(2,1)S(1)}, u32[]{:S(2)}, u32[]{:S(2)}) collective-permute-start(bf16[9,32,256]{2,1,0:T(8,128)(2,1)S(1)} %fusion.10), channel_id=1, source_target_pairs={{0,8},{4,12},{8,0},{12,4},{1,9},{5,13},{9,1},{13,5},{2,10},{6,14},... | collective-permute-start | bytes 442376 | tf_op jit(solution)/shard_map/ppermute | solution.py:22
  63.3 6.5 %collective-permute-start.20 = (bf16[9,32,256]{2,1,0:T(8,128)(2,1)S(1)}, bf16[9,32,256]{2,1,0:T(8,128)(2,1)S(1)}, u32[]{:S(2)}, u32[]{:S(2)}) collective-permute-start(bf16[9,32,256]{2,1,0:T(8,128)(2,1)S(1)} %add_convert_fusion), channel_id=1, source_target_pairs={{0,4},{4,0},{8,12},{12,8},{1,5},{5,1},{9,13},{13,9},{2,6},{6,2},{1... | collective-permute-start | bytes 442376 | tf_op jit(solution)/shard_map/ppermute | solution.py:22
  66.0 6.1 %collective-permute-start.18 = (bf16[9,32,256]{2,1,0:T(8,128)(2,1)S(1)}, bf16[9,32,256]{2,1,0:T(8,128)(2,1)S(1)}, u32[]{:S(2)}, u32[]{:S(2)}) collective-permute-start(bf16[9,32,256]{2,1,0:T(8,128)(2,1)S(1)} %add_convert_fusion.1), channel_id=1, source_target_pairs={{0,4},{4,0},{8,12},{12,8},{1,5},{5,1},{9,13},{13,9},{2,6},{6,2},{1... | collective-permute-start | bytes 442376 | tf_op jit(solution)/shard_map/ppermute | solution.py:22
  69.9 4.1 %collective-permute-start.21 = (bf16[9,64,256]{2,1,0:T(8,128)(2,1)S(1)}, bf16[9,64,256]{2,1,0:T(8,128)(2,1)S(1)}, u32[]{:S(2)}, u32[]{:S(2)}) collective-permute-start(bf16[9,64,256]{2,1,0:T(8,128)(2,1)S(1)} %pad_maximum_fusion.2), channel_id=1, source_target_pairs={{0,2},{2,0},{1,3},{3,1},{4,6},{6,4},{5,7},{7,5},{8,10},{10,8},{9,1... | collective-permute-start | bytes 884744 | tf_op jit(solution)/shard_map/ppermute | solution.py:22
  72.1 2.0 %collective-permute-start.19 = (bf16[9,64,256]{2,1,0:T(8,128)(2,1)S(1)}, bf16[9,64,256]{2,1,0:T(8,128)(2,1)S(1)}, u32[]{:S(2)}, u32[]{:S(2)}) collective-permute-start(bf16[9,64,256]{2,1,0:T(8,128)(2,1)S(1)} %pad_maximum_fusion.1), channel_id=1, source_target_pairs={{0,2},{2,0},{1,3},{3,1},{4,6},{6,4},{5,7},{7,5},{8,10},{10,8},{9,1... | collective-permute-start | bytes 884744 | tf_op jit(solution)/shard_map/ppermute | solution.py:22

commit v3 on v2

v3 whole, which is shorter than its diff:
```python
import functools
import math

import jax
import jax.numpy as jnp
from jax import lax
from jax.experimental import pallas as pl
from jax.experimental.pallas import tpu as pltpu
from jax.sharding import PartitionSpec as P

BLK = 8
SLOT = 16
CHUNKS = (5, 4, 5, 4)
F32 = jnp.float32
BF16 = jnp.bfloat16
VMEM = pl.BlockSpec(memory_space=pltpu.VMEM)
SMEM = pl.BlockSpec(memory_space=pltpu.SMEM)
PARAMS = pltpu.CompilerParams(vmem_limit_bytes=14 * 1024 * 1024)


def swap(block, axis, distance=1):
    count = lax.axis_size(axis)
    return lax.ppermute(block, axis, [(i, i ^ distance) for i in range(count)])


def shift(block, axis, step):
    count = lax.axis_size(axis)
    pairs = [(i, i + step) for i in range(count) if 0 <= i + step < count]
    return lax.ppermute(block, axis, pairs)


def ordered(flag, first, second, axis):
    return jnp.concatenate(
        [jnp.where(flag, second, first), jnp.where(flag, first, second)], axis=axis
    )


def pieces(total, step):
    return [(lo, min(step, total - lo)) for lo in range(0, total, step)]


def forward_tap(tap, scal, refs):
    if len(refs) == 1:
        return refs[0][tap].T
    own_ref, got_ref, mate_ref = refs
    theirs = ordered(scal[1] == 1, got_ref[tap], mate_ref[tap], 0)
    return ordered(scal[0] == 1, own_ref[tap], theirs, 1)


def forward_taps(scal, refs, mat_ref):
    for tap in range(9):
        row, col = tap // 3, tap % 3
        block = forward_tap(tap, scal, refs)
        channels = block.shape[0]
        mat_ref[
            row * channels : (row + 1) * channels, col * channels : (col + 1) * channels
        ] = block


def own_rows(value, index, count):
    size = value.shape[0] // count
    result = value[:size]
    for part in range(1, count):
        result = jnp.where(index == part, value[part * size : (part + 1) * size], result)
    return result


def clear_ends(low_ref, high_ref, count):
    blank = jnp.zeros((8, low_ref.shape[1]), F32)
    low_ref[:8, :] = blank
    high_ref[8 + count : 16 + count, :] = blank


def row_groups(count, size):
    return [(lo, min(lo + size, count)) for lo in range(0, count, size)]


def convolve(src_ref, mat_ref, low_ref, mid_ref, high_ref, rows, group, stride, finish):
    channels = src_ref.shape[1]
    clear_ends(low_ref, high_ref, SLOT + rows * stride)
    waiting = None
    for first, last in row_groups(rows, group):
        lo = SLOT + first * stride if first else 0
        hi = SLOT + last * stride
        window = jnp.concatenate(
            [src_ref[lo + row * stride : hi + row * stride, :] for row in range(3)], axis=1
        )
        width = mat_ref.shape[1] // 3
        part = jnp.dot(window, mat_ref[...], preferred_element_type=F32)
        for col, ref in enumerate((low_ref, mid_ref, high_ref)):
            ref[8 + lo : 8 + hi, :width] = part[:, col * width : (col + 1) * width]
        if waiting is not None:
            finish(*waiting)
        waiting = (first, last)
    finish(*waiting)


def combined(low_ref, mid_ref, high_ref, lo, size):
    return (
        low_ref[7 + lo : 7 + lo + size, :]
        + mid_ref[8 + lo : 8 + lo + size, :]
        + high_ref[9 + lo : 9 + lo + size, :]
    )


def own_part(value, index, count):
    width = value.shape[1] // count
    result = value[:, :width]
    for part in range(1, count):
        result = jnp.where(index == part, value[:, part * width : (part + 1) * width], result)
    return result


def chunk_of(index):
    for chunk, size in enumerate(CHUNKS):
        if index < size:
            return chunk, index
        index -= size


def kernel_grads(core, grad_ref, src_ref, base, stride, before, kept, sent):
    own = grad_ref.shape[1]
    cells = grad_ref.shape[0]
    turned = grad_ref[...].T
    moved = jnp.concatenate(
        [
            pltpu.roll(turned, cells - 1, 1).astype(BF16),
            turned.astype(BF16),
            pltpu.roll(turned, 1, 1).astype(BF16),
        ],
        axis=0,
    )
    for row in range(3):
        start = base + row * stride
        part = jnp.dot(moved, src_ref[start : start + cells, :], preferred_element_type=F32)
        for col in range(3):
            tap = 3 * row + col
            half = own // 2
            low = part[col * own : col * own + half, :]
            high = part[col * own + half : (col + 1) * own, :]
            chunk, at = chunk_of(before + tap)
            rows = slice(at * half, (at + 1) * half)
            kept[chunk][rows, :] = jnp.where(core == 1, high, low)
            sent[chunk][rows, :] = jnp.where(core == 1, low, high)


def prepare(scal, labels_in, flow_in, winner_in, taps_in, lines, *refs):
    labels, flow, winner, taps, sems = refs[-5:]
    copies = [
        pltpu.make_async_copy(source, target, sems.at[index])
        for index, (source, target) in enumerate(
            ((labels_in, labels), (flow_in, flow), (winner_in, winner), (taps_in, taps))
        )
    ]
    for copy in copies:
        copy.start()
    for copy in copies[:3]:
        copy.wait()
    height, width = labels.shape
    blocks = winner.shape[1]
    at = lax.broadcasted_iota(jnp.int32, (blocks, width), 1)
    block = lax.broadcasted_iota(jnp.int32, (blocks, width), 0)
    spread = ((at >= block * BLK) & (at < block * BLK + BLK)).astype(BF16)
    fields = [labels[...].astype(F32)]
    ids = [
        jnp.dot(winner[row : row + 1, :].astype(F32).astype(BF16), spread, preferred_element_type=F32)
        for row in range(height // BLK)
    ]
    fields.append(jnp.concatenate([jnp.broadcast_to(part, (BLK, width)) for part in ids], axis=0))
    for index in range(2):
        rest = flow[index]
        for _ in range(3):
            piece = rest.astype(BF16).astype(F32)
            fields.append(piece)
            rest = rest - piece
    for row in range(height):
        lines[row] = jnp.concatenate([field[row : row + 1] for field in fields], axis=0).astype(BF16)
    copies[3].wait()
    layers = taps.shape[0]
    turned, sends = refs[:layers], refs[layers:-5]
    for layer in range(layers):
        for tap in range(9):
            block = taps[layer, tap].T
            half = block.shape[0] // 2
            turned[layer][tap] = block
            if sends:
                sends[layer][tap] = jnp.where(scal[1] == 0, block[:half], block[half:])


def first_layer(geom, scal, mid, top, bottom, tiles, *refs):
    taps = refs[:-7]
    padded, active, slope, mat, low, cen, high = refs[-7:]
    height, width, futs, layers = geom
    stride = width + SLOT
    halo = layers + 1
    col = scal[1]
    row_at = scal[2]
    row_count = scal[3]
    slots = height + 2 * halo
    lane = lax.broadcasted_iota(jnp.int32, tiles.shape[1:], 0)
    near = (lane < SLOT // 2).astype(jnp.int32) != col
    blank = jnp.zeros(tiles.shape[1:], BF16)
    padded[:SLOT, :] = jnp.where(near & (col == 1), tiles[0], blank)
    for row in range(slots):
        at = SLOT + row * stride
        if row < halo:
            source = top[row * width : (row + 1) * width, :]
        elif row < halo + height:
            source = mid[row - halo]
        else:
            below = (row - halo - height) * width
            source = bottom[below : below + width, :]
        padded[at : at + width, :] = source
        after = tiles[row + 1] if row + 1 < slots else blank
        padded[at + width : at + stride, :] = jnp.where(
            near, jnp.where(col == 1, after, tiles[row]), blank
        )
    forward_taps(scal, taps, mat)
    spot = lax.broadcasted_iota(jnp.int32, (stride, active.shape[1]), 0)
    inside = (spot < width) | ((col == 0) & (spot < width + SLOT // 2)) | (
        (col == 1) & (spot >= width + SLOT // 2)
    )

    bump = ((spot >= width) & (col == 1)).astype(jnp.int32)

    def finish(at, size, keep):
        pre = combined(low, cen, high, at, size)
        sigma = jax.nn.sigmoid(pre)
        active[at : at + size, :] = jnp.where(keep, pre * sigma, 0.0).astype(BF16)
        return pre, sigma

    edge = halo - 1

    def finish_rows(begin, end):
        if begin == 0:
            finish(0, SLOT, (col == 1) & (row_at * height - edge >= 0))
        for row in range(begin, end):
            at = SLOT + row * stride
            place = row_at * height + row - edge
            keep = inside & (bump + place >= 0) & (bump + place < row_count * height)
            pre, sigma = finish(at, stride, keep)
            if edge <= row < edge + height:
                mine = (row - edge) * width
                own_pre = own_part(pre[:width], scal[0], futs)
                own_sig = own_part(sigma[:width], scal[0], futs)
                slope[mine : mine + width, :] = own_sig * (1.0 + own_pre * (1.0 - own_sig))

    convolve(padded, mat, low, cen, high, height + 2 * edge, 3, stride, finish_rows)


def cell_data(scal, lines, above, below, tile, height, width):
    stride = width + SLOT
    count = height + 2
    core, row_at, row_count = scal[1], scal[2], scal[3]
    beside = [block[block.shape[0] - 8 :, :width] for block in (above, below)]
    rows = beside[:1] + [lines[row] for row in range(height)] + beside[1:]
    blank = jnp.zeros(tile.shape[1:], F32)
    tiles = [blank] + [tile[row].astype(F32) for row in range(count)] + [blank]
    parts = []
    for row in range(count + 1):
        parts.append(jnp.where(core == 1, tiles[row + 1], tiles[row]))
        if row < count:
            parts.append(rows[row].astype(F32))
    flat = jnp.concatenate(parts, axis=1)
    place = lax.broadcasted_iota(jnp.int32, (8, flat.shape[1]), 1)
    line = jnp.full_like(place, -2)
    spot = place
    for row in range(count + 1):
        begin = row * stride
        line = jnp.where(place >= begin, row - 1, line)
        spot = jnp.where(place >= begin, place - (begin + SLOT), spot)
    main = spot >= 0
    right = (spot == -SLOT) & (core == 0)
    left = (spot == -1) & (core == 1)
    own = main & (line >= 0) & (line < height)
    line = line - right.astype(jnp.int32)
    at = row_at * height + line
    real = (at >= 0) & (at < row_count * height) & (line >= -1) & (line <= height)
    valid = real & (main | right | left)
    return (
        flat[0:1],
        flat[2:3] + flat[3:4] + flat[4:5],
        flat[5:6] + flat[6:7] + flat[7:8],
        flat[1:2],
        jnp.where(valid, 1.0, 0.0)[:1],
        jnp.where(own, 1.0, 0.0)[:1],
    )


def last_layer(
    geom, scale, scal, active, slope, padded, heads_w, lines, above, below, tile, *refs
):
    count = len(CHUNKS)
    taps, outs = refs[: -(10 + 2 * count)], refs[-(10 + 2 * count) : -9]
    kept, sent, small = outs[:count], outs[count:-1], outs[-1]
    mat, low, cen, high, out, bend, grad, own_grad, back_mat = refs[-9:]
    height, width, futs, layers = geom
    stride = width + SLOT
    count = grad.shape[0]
    forward_taps(scal, taps, mat)

    def finish_rows(begin, end):
        lo = SLOT + begin * stride if begin else 0
        for at, size in pieces(SLOT + end * stride - lo, stride):
            at += lo
            pre = combined(low, cen, high, at, size)
            sigma = jax.nn.sigmoid(pre)
            bend[at : at + size, :] = sigma * (1.0 + pre * (1.0 - sigma))
            out[at : at + size, :] = (pre * sigma).astype(BF16)

    convolve(active, mat, low, cen, high, height + 2, 4, stride, finish_rows)
    nfut = heads_w.shape[0] // 3
    heads = lax.dot_general(
        heads_w[...], out[...], (((1,), (1,)), ((), ())), preferred_element_type=F32
    )
    logit = heads[:nfut]
    target, flow_one, flow_two, picks, valid, own = cell_data(
        scal, lines, above, below, tile, height, width
    )
    first = heads[nfut : 2 * nfut] - flow_one
    second = heads[2 * nfut :] - flow_two
    future = lax.broadcasted_iota(jnp.int32, logit.shape, 0).astype(F32)
    mask = jnp.where(picks == future, valid, 0.0)
    cell = (
        jnp.maximum(logit, 0.0)
        + jnp.log1p(jnp.exp(-jnp.abs(logit)))
        - target * logit
        + 0.5 * (first * first + second * second)
    )
    loss = jnp.sum(jnp.where(mask * own > 0.0, cell, 0.0))
    picked = mask > 0.0
    grads = jnp.concatenate(
        [
            jnp.where(picked, (jax.nn.sigmoid(logit) - target) * scale, 0.0),
            jnp.where(picked, first * scale, 0.0),
            jnp.where(picked, second * scale, 0.0),
        ],
        axis=0,
    )
    mine = jnp.where(own > 0.0, grads, 0.0).astype(BF16)
    grads = grads.astype(BF16)
    by_head = jnp.dot(mine, out[...], preferred_element_type=F32)
    fut_here = nfut // futs
    lines = []
    for index in range(fut_here):
        for kind in range(3):
            at = kind * nfut + index
            line = by_head[at : at + 1, :]
            for part in range(1, futs):
                other = at + part * fut_here
                line = jnp.where(scal[0] == part, by_head[other : other + 1, :], line)
            lines.append(line)
    lines.append(jnp.broadcast_to(loss, (small.shape[0] - len(lines), small.shape[1])))
    totals = jnp.concatenate(lines, axis=0)
    small[...] = totals
    sent[0][kept[0].shape[0] :, :] = totals
    up = lax.dot_general(
        grads, heads_w[...], (((0,), (0,)), ((), ())), preferred_element_type=F32
    )
    low[: count, :] = up
    own_grad[...] = jnp.zeros_like(own_grad)

    def back(lo, size):
        value = (low[lo : lo + size, :] * bend[lo : lo + size, :]).astype(BF16)
        grad[lo : lo + size, :] = value
        return value

    back(0, SLOT)
    for row in range(height + 2):
        at = SLOT + row * stride
        value = back(at, stride)
        if 1 <= row <= height:
            mine_at = SLOT + (row - 1) * stride
            own_grad[mine_at : mine_at + width, :] = own_part(
                value[:width].astype(F32), scal[0], futs
            )
    kernel_grads(scal[1], own_grad, active, stride, stride, 0, kept, sent)
    back_layer(
        geom, scal, grad, taps, slope, padded, kept, sent, back_mat, low, cen, high,
        own_grad,
    )


def back_layer(
    geom, scal, grad, taps, slope, padded, kept, sent, mat, low, cen, high, own_grad
):
    height, width, futs, layers = geom
    stride = width + SLOT
    channels = grad.shape[1]
    own = channels // futs
    for tap in range(9):
        row, col = tap // 3, tap % 3
        mat[
            (2 - row) * channels : (3 - row) * channels, (2 - col) * own : (3 - col) * own
        ] = own_rows(forward_tap(tap, scal, taps), scal[0], futs).T
    own_grad[...] = jnp.zeros_like(own_grad)

    def finish_rows(begin, end):
        for row in range(begin, end):
            at = SLOT + row * stride
            up = (
                low[7 + at : 7 + at + width, :own]
                + cen[8 + at : 8 + at + width, :own]
                + high[9 + at : 9 + at + width, :own]
            )
            value = (up * slope[row * width : (row + 1) * width, :]).astype(BF16)
            own_grad[at : at + width, :] = value.astype(F32)

    convolve(grad, mat, low, cen, high, height, 4, stride, finish_rows)
    kernel_grads(scal[1], own_grad, padded, layers * stride, stride, 9, kept, sent)


def tap_parts(mine, got, after=None):
    if after is not None:
        got, _ = tied(got, after)
    return (mine, got, swap(got, "cols"))


def tied(*blocks):
    return lax.optimization_barrier(blocks)


def in_order(arrived, ready):
    return [
        tied(block, ready[index + 1])[0] if index + 1 < len(arrived) else block
        for index, block in enumerate(arrived)
    ]


def one_by_one(blocks, axis):
    arrived = []
    for block in blocks:
        if arrived:
            block = tied(block, arrived[-1])[0]
        arrived.append(swap(block, axis))
    return arrived


def split3(value):
    high = rounded(value)
    rest = value - high
    mid = rounded(rest)
    return [high.astype(BF16), mid.astype(BF16), rounded(rest - mid).astype(BF16)]


def joined(block, small):
    return jnp.concatenate([block.reshape(-1, block.shape[-1]), *split3(small)], axis=0)


def parted(block, like, small):
    size = block.shape[0] - 3 * small.shape[0]
    parts = block[size:].astype(F32).reshape(3, *small.shape)
    return block[:size].reshape(like.shape), small + (parts[0] + parts[1] + parts[2])


def tile_sums(kept, sent, small, core, row_at, half):
    bit = row_at & 1
    channels = small.shape[1]
    got = [swap(block, "cols") for block in sent]
    size = kept[0].shape[0]
    small = small + got[0][size:]
    got[0] = got[0][:size]
    blocks = [(mine + more).reshape(-1, half, channels) for mine, more in zip(kept, got)]
    half = half // 2
    kept = [jnp.where(bit == 1, block[:, half:], block[:, :half]) for block in blocks]
    sent = [jnp.where(bit == 1, block[:, :half], block[:, half:]) for block in blocks]
    ready = [rounded(block).astype(BF16) for block in sent]
    ready[0] = joined(ready[0], small)
    got = in_order([swap(block, "rows") for block in ready], ready)
    got[0], small = parted(got[0], kept[0], small)
    pairs = [rounded(mine + more.astype(F32)) for mine, more in zip(kept, got)]
    ready = [block.astype(BF16) for block in pairs]
    ready[0] = joined(ready[0], small)
    got = in_order([swap(block, "rows", 2) for block in ready], ready)
    got[0], small = parted(got[0], pairs[0], small)
    ready = [(mine + more.astype(F32)).astype(BF16) for mine, more in zip(pairs, got)]
    got = in_order([swap(block, "rows") for block in ready], ready)
    ready[-1], small = tied(ready[-1], small)
    ready = [ordered(bit == 1, mine, more, 1) for mine, more in zip(ready, got)]
    got = in_order([swap(block, "cols") for block in ready], ready)
    return [ordered(core == 1, mine, more, 1) for mine, more in zip(ready, got)], small


def rounded(value):
    return lax.reduce_precision(value, 8, 7)


def local(features, trunk_weights, head_weights, flow_target, labels, winner):
    own, height, width = features.shape
    layers, _, _, channels = trunk_weights.shape
    fut_total = head_weights.shape[0]
    futs = lax.axis_size("futures")
    fut_here = fut_total // futs
    rows_total = lax.axis_size("rows")
    fut = lax.axis_index("futures")
    core = lax.axis_index("cols")
    row_at = lax.axis_index("rows")
    cell_count = height * width * rows_total * lax.axis_size("cols")
    scale = 1.0 / math.sqrt(cell_count)
    halo = layers + 1
    stride = width + SLOT
    geom = (height, width, futs, layers)
    scal = jnp.stack([fut, core, row_at, jnp.int32(rows_total)]).astype(jnp.int32)

    shape = jax.ShapeDtypeStruct
    mine = jnp.transpose(features, (1, 2, 0))
    half_taps = shape((9, channels // 2, own), BF16)
    lines, *turned = pl.pallas_call(
        prepare,
        out_shape=(shape((height, 8, width), BF16),)
        + (shape((9, channels, own), BF16),) * layers
        + ((half_taps,) * layers if futs == 2 else ()),
        in_specs=[SMEM] + [pl.BlockSpec(memory_space=pltpu.HBM)] * 4,
        out_specs=(VMEM,) * (1 + layers + (layers if futs == 2 else 0)),
        scratch_shapes=[
            pltpu.VMEM(labels.shape, labels.dtype),
            pltpu.VMEM(flow_target.shape, F32),
            pltpu.VMEM(winner.shape, winner.dtype),
            pltpu.VMEM(trunk_weights.shape, BF16),
            pltpu.SemaphoreType.DMA((4,)),
        ],
        compiler_params=PARAMS,
        name="prepare",
    )(
        scal,
        *[
            pltpu.with_memory_space_constraint(array, pltpu.HBM)
            for array in (labels, flow_target, winner, trunk_weights)
        ],
    )
    if futs == 2:
        outer = jnp.concatenate([mine[:halo], mine[-halo:]], axis=0)
        theirs = swap(outer, "futures")
        outer = ordered(fut == 1, outer, theirs, 2)
        sends = tied(theirs, *turned[layers + 1 :])[1:]
        inner = tied(mine[halo:-halo], lines)[0]
        inner_theirs = swap(inner, "futures")
        first, last = outer[:halo], outer[halo:]
        got_taps = [swap(send, "futures") for send in [turned[layers], *sends]]
        taps = tap_parts(turned[0], got_taps[0])
    else:
        mid = lax.all_gather(mine, "futures", axis=2, tiled=True)
        first, last = mid[:halo], mid[-halo:]
        whole_taps = lax.all_gather(trunk_weights, "futures", axis=2, tiled=True)
        taps = (whole_taps[0],)

    def with_line(block, line):
        line = jnp.pad(line, ((0, 0), (0, channels - width)))
        return jnp.concatenate([block.reshape(-1, channels), line], axis=0)

    top = shift(with_line(last, lines[-1]), "rows", 1)
    bottom = shift(with_line(first, lines[0]), "rows", -1)
    if futs == 2:
        top, bottom, inner_theirs = tied(top, bottom, inner_theirs)
        inner = ordered(fut == 1, inner, inner_theirs, 2)
        mid = jnp.concatenate([first, inner, last], axis=0)

    def halo_rows(block):
        return block[: halo * width].reshape(halo, width, channels)

    def line_of(block):
        return block[halo * width :, :width]

    def edge_of(block):
        return jnp.where(core == 0, block[..., -SLOT:, :], block[..., :SLOT, :])

    tiles = swap(
        jnp.concatenate([edge_of(halo_rows(top)), edge_of(mid), edge_of(halo_rows(bottom))], axis=0), "cols"
    )
    line_rows = jnp.concatenate([line_of(top)[None], lines, line_of(bottom)[None]], axis=0)
    tile = swap(
        jnp.where(core == 0, line_rows[:, :, -SLOT:], line_rows[:, :, :SLOT]), "cols"
    )
    heads_w = jnp.transpose(head_weights, (1, 0, 2)).reshape(3 * fut_total, channels)

    def cells(rows):
        return SLOT + rows * stride

    first_cells = cells(height + 4)
    last_cells = cells(height + 2)
    own_cells = -(-cells(height) // 128) * 128
    padded, active, slope = pl.pallas_call(
        functools.partial(first_layer, geom),
        out_shape=(
            shape((cells(height + 6), channels), BF16),
            shape((first_cells, channels), BF16),
            shape((height * width, own), F32),
        ),
        in_specs=[SMEM] + [VMEM] * (4 + len(taps)),
        out_specs=(VMEM,) * 3,
        scratch_shapes=[pltpu.VMEM((3 * channels, 3 * channels), BF16)]
        + [pltpu.VMEM((first_cells + 16, channels), F32)] * 3,
        compiler_params=PARAMS,
        name="first_layer",
    )(scal, mid, top, bottom, tiles, *taps)

    if futs == 2:
        taps = tap_parts(turned[layers - 1], got_taps[layers - 1], active)
    else:
        taps = (whole_taps[layers - 1],)
    lines_out = -(-(3 * fut_here + 1) // 8) * 8
    sizes = [size * (own // 2) for size in CHUNKS]
    kept_out = tuple(shape((size, channels), F32) for size in sizes)
    sizes[0] += lines_out
    sent_out = tuple(shape((size, channels), F32) for size in sizes)
    *parts, small = pl.pallas_call(
        functools.partial(last_layer, geom, scale),
        out_shape=kept_out + sent_out + (shape((lines_out, channels), F32),),
        in_specs=[SMEM] + [VMEM] * (8 + len(taps)),
        out_specs=(VMEM,) * (2 * len(CHUNKS) + 1),
        scratch_shapes=[pltpu.VMEM((3 * channels, 3 * channels), BF16)]
        + [pltpu.VMEM((last_cells + 16, channels), F32)] * 3
        + [
            pltpu.VMEM((last_cells, channels), BF16),
            pltpu.VMEM((last_cells, channels), F32),
            pltpu.VMEM((last_cells, channels), BF16),
            pltpu.VMEM((own_cells, own), F32),
            pltpu.VMEM((3 * channels, 3 * own), BF16),
        ],
        compiler_params=PARAMS,
        name="last_layer",
    )(scal, active, slope, padded, heads_w, lines, top, bottom, tile, *taps)

    kept, sent = parts[: len(CHUNKS)], parts[len(CHUNKS) :]
    if rows_total == 4:
        sums, small = tile_sums(kept, sent, small, core, row_at, own // 2)
    else:
        sent[0] = sent[0][:-lines_out]
        sums = [
            ordered(core == 1, *[part.reshape(-1, own // 2, channels) for part in both], 1)
            for both in zip(kept, sent)
        ]
        sums, small = lax.psum((sums, small), ("rows", "cols"))
    taps_of = []
    for layer in range(layers):
        low = 9 * (layers - 1 - layer)
        begin = 0
        for block in sums:
            first = max(low - begin, 0)
            last = min(low + 9 - begin, block.shape[0])
            if first < last:
                taps_of.append(block[first:last])
            begin += block.shape[0]
    trunk_grad = jnp.concatenate(taps_of, axis=0).astype(F32).reshape(layers, 9, own, channels)
    head_grad = small[: 3 * fut_here].reshape(fut_here, 3, channels)
    total = small[3 * fut_here, :1] / cell_count
    return (total, trunk_grad, head_grad)


def solution(mesh):
    placed = (
        P("futures", ("groups", "rows"), "cols"),
        P(None, None, "futures", None),
        P(),
        P(None, ("groups", "rows"), "cols"),
        P(("groups", "rows"), "cols"),
        P(("groups", "rows"), "cols"),
    )
    return jax.shard_map(
        local,
        mesh=mesh,
        in_specs=placed,
        out_specs=(P("groups"), P("groups", None, "futures", None), P("futures", "groups", None)),
        check_vma=False,
    )
```

time: 77.5 us -> 70.8 us (0.914)
  waiting for transfers between devices: 32.4 us -> 19 us
  starting transfers between devices: 21.2 us -> 30 us
  local copies, waits for them, and re-layouts: 5.64 us -> 2.36 us
  Pallas kernels: 11 us -> 12.3 us
    ppermute x20 -> x28, waiting for transfers between devices: 32.4 us -> 17.7 us  [swap(): return lax.ppermute(block, axis, [(i, i ^ distance) for i in range(count)])]
    ppermute x20 -> x28, starting transfers between devices: 16.3 us -> 24.9 us  [swap(): return lax.ppermute(block, axis, [(i, i ^ distance) for i in range(count)])]
    unnamed x14 -> x4, local copies, waits for them, and re-layouts: 5.08 us -> 1.76 us
    another operation x1 -> x0, other arithmetic: 1.66 us -> none  [local(): trunk_grad = jnp.stack([first_sum, last_sum])]
    convert_element_type x6 -> x19, other arithmetic: 0.42 us -> 2.05 us  [the longest x1 1.67 us: local(): jnp.concatenate(taps_of, axis=0).astype(F32)]
    pallas_call x1, Pallas kernels: 0.74 us -> 2.25 us  [local(): pl.pallas_call(prepare, out_shape=(shape((height, 8, width), BF16),) + (s...]
    ppermute x2, waiting for transfers between devices: 0.01 us -> 1.32 us  [shift(): return lax.ppermute(block, axis, pairs)]
    add x5, other arithmetic: 1.24 us -> 0.17 us  [the longest x4 0.16 us: tile_sums(): mine + more]
  transfers between devices with their start and end apart: 22 -> 30, of which waited for: 11 -> 12; matrix products, arithmetic and copies ran while one was open for 4% -> 4% of each run, Pallas kernels for 5% -> 8%
where the time goes in v3:
time: 70.8 us; the launch traced here: 70.4 us
  starting transfers between devices  30 us (42%)
  waiting for transfers between devices  19 us (27%)
  Pallas kernels  12.3 us (17%)
  other arithmetic  3.75 us (5%)
  between operations  2.89 us (4%)
  local copies, waits for them, and re-layouts  2.36 us (3%)
    ppermute x28, starting transfers between devices, swap(): return lax.ppermute(block, axis, [(i, i ^ distance) for i in range(count)])  24.9 us
    ppermute x28, waiting for transfers between devices, swap(): return lax.ppermute(block, axis, [(i, i ^ distance) for i in range(count)])  17.7 us
    pallas_call x1, Pallas kernels, local(): pl.pallas_call(functools.partial(last_layer, geom, scale), out_shape=kept...  6.94 us
    ppermute x2, starting transfers between devices, shift(): return lax.ppermute(block, axis, pairs)  5.15 us
    pallas_call x1, Pallas kernels, local(): pl.pallas_call(functools.partial(first_layer, geom), out_shape=(shape((ce...  3.14 us
    pallas_call x1, Pallas kernels, local(): pl.pallas_call(prepare, out_shape=(shape((height, 8, width), BF16),) + (s...  2.25 us
    unnamed x4, local copies, waits for them, and re-layouts  1.76 us
    convert_element_type x1, other arithmetic, local(): jnp.concatenate(taps_of, axis=0).astype(F32)  1.67 us
  transfers between devices with their start and end apart: 30, of which 12 were waited for; matrix products, arithmetic and copies ran while one was open for 4% of the time, Pallas kernels for 8%

profile of v3, /device:TPU:0, one launch (start us, length us, event | category | flops | bytes accessed | tf_op | source)
XLA Modules:
  0.0 70.4 jit_solution(9427727165993218911)
XLA Ops:
  0.6 1.2 %copy.11 = bf16[128,8,128]{0,2,1:T(8,128)(2,1)S(1)} copy(bf16[128,8,128]{2,1,0:T(8,128)(2,1)} %param.6) | data formatting | bytes 524288 | tf_op args[0]
  1.8 3.0 %collective-permute-start = (bf16[6,128,128]{2,1,0:T(8,128)(2,1)S(1)}, bf16[6,128,128]{2,1,0:T(8,128)(2,1)S(1)}, u32[]{:S(2)}, u32[]{:S(2)}) collective-permute-start(bf16[6,128,128]{2,1,0:T(8,128)(2,1)S(1)} %pad_maximum_fusion.2), channel_id=1, source_target_pairs={{0,1},{1,0},{2,3},{3,2},{4,5},{5,4},{6,7},{7,6},{8,9},{9,8},{10,11... | collective-permute-start | bytes 589832 | tf_op jit(solution)/shard_map/ppermute | solution.py:23
  4.8 0.1 pad_add_fusion.scal
  4.9 2.3 %prepare.1 = (bf16[8,8,128]{2,1,0:T(8,128)(2,1)S(1)}, bf16[9,256,128]{2,1,0:T(8,128)(2,1)S(1)}, bf16[9,256,128]{2,1,0:T(8,128)(2,1)S(1)}, bf16[9,128,128]{2,1,0:T(8,128)(2,1)S(1)}, bf16[9,128,128]{2,1,0:T(8,128)(2,1)S(1)}) custom-call(s32[4]{0:T(128)S(1)} %pad_add_fusion.scal, s32[8,128]{1,0:T(8,128)} %labels_in.1, f32[2,8,128]{2,1,0:T(8,128)} %flow_in.1, ...), custom_call_target="tpu_custom_call" | custom-call | tf_op jit(solution)/shard_map/prepare/pallas_call | solution.py:508
  7.2 0.1 collective-permute-start.5
  7.3 2.9 %collective-permute-done = bf16[6,128,128]{2,1,0:T(8,128)(2,1)S(1)} collective-permute-done((bf16[6,128,128]{2,1,0:T(8,128)(2,1)S(1)}, bf16[6,128,128]{2,1,0:T(8,128)(2,1)S(1)}, u32[]{:S(2)}, u32[]{:S(2)}) %collective-permute-start) | collective-permute-done | bytes 196640 | tf_op jit(solution)/shard_map/ppermute | solution.py:23
  10.3 3.9 %collective-permute-start.1 = (bf16[392,256]{1,0:T(8,128)(2,1)S(1)}, bf16[392,256]{1,0:T(8,128)(2,1)S(1)}, u32[]{:S(2)}, u32[]{:S(2)}) collective-permute-start(bf16[392,256]{1,0:T(8,128)(2,1)S(1)} %fusion.2), channel_id=1, source_target_pairs={{0,4},{4,8},{8,12},{1,5},{5,9},{9,13},{2,6},{6,10},{10,14},{3,7},{... | collective-permute-start | bytes 602120 | tf_op jit(solution)/shard_map/ppermute | solution.py:29
  14.1 0.7 fusion.3
  14.8 1.3 %collective-permute-start.2 = (bf16[392,256]{1,0:T(8,128)(2,1)}, bf16[392,256]{1,0:T(8,128)(2,1)S(1)}, u32[]{:S(2)}, u32[]{:S(2)}) collective-permute-start(bf16[392,256]{1,0:T(8,128)(2,1)} %fusion.3), channel_id=1, source_target_pairs={{4,0},{8,4},{12,8},{5,1},{9,5},{13,9},{6,2},{10,6},{14,10},{7,3},{... | collective-permute-start | bytes 602120 | tf_op jit(solution)/shard_map/ppermute | solution.py:29
  16.1 2.2 %collective-permute-start.3 = (bf16[2,128,128]{2,1,0:T(8,128)(2,1)S(1)}, bf16[2,128,128]{2,1,0:T(8,128)(2,1)S(1)}, u32[]{:S(2)}, u32[]{:S(2)}) collective-permute-start(bf16[2,128,128]{2,1,0:T(8,128)(2,1)S(1)} %slice.182), channel_id=1, source_target_pairs={{0,1},{1,0},{2,3},{3,2},{4,5},{5,4},{6,7},{7,6},{8,9},{9,8},{10,11... | collective-permute-start | bytes 196616 | tf_op jit(solution)/shard_map/ppermute | solution.py:23
  18.3 0.1 collective-permute-start.8
  18.4 2.9 %collective-permute-done.3 = bf16[2,128,128]{2,1,0:T(8,128)(2,1)S(1)} collective-permute-done((bf16[2,128,128]{2,1,0:T(8,128)(2,1)S(1)}, bf16[2,128,128]{2,1,0:T(8,128)(2,1)S(1)}, u32[]{:S(2)}, u32[]{:S(2)}) %collective-permute-start.3) | collective-permute-done | bytes 65568 | tf_op jit(solution)/shard_map/ppermute | solution.py:23
  21.3 0.0 collective-permute-done.1.top.above
  21.3 1.3 %collective-permute-done.2.bottom.below = bf16[392,256]{1,0:T(8,128)(2,1)S(1)} collective-permute-done((bf16[392,256]{1,0:T(8,128)(2,1)}, bf16[392,256]{1,0:T(8,128)(2,1)S(1)}, u32[]{:S(2)}, u32[]{:S(2)}) %collective-permute-start.2) | collective-permute-done | bytes 200736 | tf_op jit(solution)/shard_map/ppermute | solution.py:29
  22.7 0.0 copy-start
  22.8 0.1 collective-permute-start.4
  22.9 1.3 %collective-permute-done.4.tiles = bf16[14,16,256]{2,1,0:T(8,128)(2,1)S(1)} collective-permute-done((bf16[14,16,256]{2,1,0:T(8,128)(2,1)S(1)}, bf16[14,16,256]{2,1,0:T(8,128)(2,1)S(1)}, u32[]{:S(2)}, u32[]{:S(2)}) %collective-permute-start.4) | collective-permute-done | bytes 114720 | tf_op jit(solution)/shard_map/ppermute | solution.py:23
  24.2 3.1 %first_layer.1 = (bf16[2032,256]{1,0:T(8,128)(2,1)S(1)}, bf16[1744,256]{1,0:T(8,128)(2,1)S(1)}, f32[1024,128]{1,0:T(8,128)S(1)}) custom-call(s32[4]{0:T(128)S(1)} %pad_add_fusion.scal, bf16[8,128,256]{2,1,0:T(8,128)(2,1)S(1)} %pad_maximum_fusion.mid, bf16[392,256]{1,0:T(8,128)(2,1)S(1)} %collective-permute-done.1.top.above, ...), custom_call_target="tpu_custom_call" | custom-call | tf_op jit(solution)/shard_map/first_layer/pallas_call | solution.py:582
  27.4 0.0 collective-permute-done.8.refs_1_
  27.4 0.2 collective-permute-start.9
  27.6 0.1 slice_select_fusion.3
  27.7 0.4 collective-permute-start.7
  28.0 1.0 %collective-permute-done.7.tile = bf16[10,8,16]{2,1,0:T(8,128)(2,1)S(1)} collective-permute-done((bf16[10,8,16]{2,1,0:T(8,128)(2,1)S(1)}, bf16[10,8,16]{2,1,0:T(8,128)(2,1)S(1)}, u32[]{:S(2)}, u32[]{:S(2)}) %collective-permute-start.7) | collective-permute-done | bytes 2592 | tf_op jit(solution)/shard_map/ppermute | solution.py:23
  29.0 0.0 collective-permute-done.9.refs_2_
  29.1 6.9 %last_layer.1 = (f32[320,256]{1,0:T(8,128)S(1)}, f32[256,256]{1,0:T(8,128)S(1)}, f32[320,256]{1,0:T(8,128)S(1)}, f32[256,256]{1,0:T(8,128)S(1)}, f32[336,256]{1,...) custom-call(s32[4]{0:T(128)S(1)} %pad_add_fusion.scal, ...), custom_call_target="tpu_custom_call" | custom-call | tf_op jit(solution)/shard_map/last_layer/pallas_call | solution.py:606
  36.0 0.3 collective-permute-start.10
  36.3 0.3 collective-permute-start.15
  36.6 0.2 collective-permute-start.18
  36.8 0.3 collective-permute-start.13
  37.1 0.5 collective-permute-done.10
  37.7 1.6 %collective-permute-start.11 = (bf16[4,32,256]{2,1,0:T(8,128)(2,1)S(1)}, bf16[4,32,256]{2,1,0:T(8,128)(2,1)S(1)}, u32[]{:S(2)}, u32[]{:S(2)}) collective-permute-start(bf16[4,32,256]{2,1,0:T(8,128)(2,1)S(1)} %reduce-precision_convert_fusion.3), channel_id=1, source_target_pairs={{0,4},{4,0},{8,12},{12,8},{1,5},{5,1},{9,13},{13,9},{2,6},{6,2},{1... | collective-permute-start | bytes 196616 | tf_op jit(solution)/shard_map/ppermute | solution.py:23
  39.3 0.0 collective-permute-done.15
  39.4 0.5 collective-permute-start.17
  40.0 1.6 %collective-permute-start.19 = (bf16[5,32,256]{2,1,0:T(8,128)(2,1)S(1)}, bf16[5,32,256]{2,1,0:T(8,128)(2,1)S(1)}, u32[]{:S(2)}, u32[]{:S(2)}) collective-permute-start(bf16[5,32,256]{2,1,0:T(8,128)(2,1)S(1)} %reduce-precision_convert_fusion), channel_id=1, source_target_pairs={{0,4},{4,0},{8,12},{12,8},{1,5},{5,1},{9,13},{13,9},{2,6},{6,2},{1... | collective-permute-start | bytes 245768 | tf_op jit(solution)/shard_map/ppermute | solution.py:23
  41.6 0.5 collective-permute-done.11
  42.1 2.9 %collective-permute-start.12 = (bf16[4,32,256]{2,1,0:T(8,128)(2,1)S(1)}, bf16[4,32,256]{2,1,0:T(8,128)(2,1)S(1)}, u32[]{:S(2)}, u32[]{:S(2)}) collective-permute-start(bf16[4,32,256]{2,1,0:T(8,128)(2,1)S(1)} %fusion.13), channel_id=1, source_target_pairs={{0,8},{4,12},{8,0},{12,4},{1,9},{5,13},{9,1},{13,5},{2,10},{6,14},... | collective-permute-start | bytes 196616 | tf_op jit(solution)/shard_map/ppermute | solution.py:23
  45.1 1.8 %collective-permute-start.26 = (bf16[4,32,256]{2,1,0:T(8,128)(2,1)S(1)}, bf16[4,32,256]{2,1,0:T(8,128)(2,1)S(1)}, u32[]{:S(2)}, u32[]{:S(2)}) collective-permute-start(bf16[4,32,256]{2,1,0:T(8,128)(2,1)S(1)} %fusion.14), channel_id=1, source_target_pairs={{0,8},{4,12},{8,0},{12,4},{1,9},{5,13},{9,1},{13,5},{2,10},{6,14},... | collective-permute-start | bytes 196616 | tf_op jit(solution)/shard_map/ppermute | solution.py:23
  46.9 0.0 collective-permute-done.13
  47.0 1.3 %collective-permute-start.14 = (bf16[208,256]{1,0:T(8,128)(2,1)S(1)}, bf16[208,256]{1,0:T(8,128)(2,1)S(1)}, u32[]{:S(2)}, u32[]{:S(2)}) collective-permute-start(bf16[208,256]{1,0:T(8,128)(2,1)S(1)} %pad_maximum_fusion.8), channel_id=1, source_target_pairs={{0,4},{4,0},{8,12},{12,8},{1,5},{5,1},{9,13},{13,9},{2,6},{6,2},{1... | collective-permute-start | bytes 319496 | tf_op jit(solution)/shard_map/ppermute | solution.py:23
  48.3 1.7 %collective-permute-done.12 = bf16[4,32,256]{2,1,0:T(8,128)(2,1)S(1)} collective-permute-done((bf16[4,32,256]{2,1,0:T(8,128)(2,1)S(1)}, bf16[4,32,256]{2,1,0:T(8,128)(2,1)S(1)}, u32[]{:S(2)}, u32[]{:S(2)}) %collective-permute-start.12) | collective-permute-done | bytes 65568 | tf_op jit(solution)/shard_map/ppermute | solution.py:23
  50.0 0.3 collective-permute-start.23
  50.4 0.0 collective-permute-done.19
  50.4 3.2 %collective-permute-start.20 = (bf16[5,32,256]{2,1,0:T(8,128)(2,1)S(1)}, bf16[5,32,256]{2,1,0:T(8,128)(2,1)S(1)}, u32[]{:S(2)}, u32[]{:S(2)}) collective-permute-start(bf16[5,32,256]{2,1,0:T(8,128)(2,1)S(1)} %fusion.15), channel_id=1, source_target_pairs={{0,8},{4,12},{8,0},{12,4},{1,9},{5,13},{9,1},{13,5},{2,10},{6,14},... | collective-permute-start | bytes 245768 | tf_op jit(solution)/shard_map/ppermute | solution.py:23
  53.6 0.0 collective-permute-done.26
  53.7 0.1 collective-permute-start.28
  53.8 0.0 collective-permute-done.14
  53.9 1.6 %collective-permute-start.16 = (bf16[208,256]{1,0:T(8,128)(2,1)S(1)}, bf16[208,256]{1,0:T(8,128)(2,1)S(1)}, u32[]{:S(2)}, u32[]{:S(2)}) collective-permute-start(bf16[208,256]{1,0:T(8,128)(2,1)S(1)} %pad_maximum_fusion.9), channel_id=1, source_target_pairs={{0,8},{4,12},{8,0},{12,4},{1,9},{5,13},{9,1},{13,5},{2,10},{6,14},... | collective-permute-start | bytes 319496 | tf_op jit(solution)/shard_map/ppermute | solution.py:23
  55.5 2.7 %collective-permute-done.20 = bf16[5,32,256]{2,1,0:T(8,128)(2,1)S(1)} collective-permute-done((bf16[5,32,256]{2,1,0:T(8,128)(2,1)S(1)}, bf16[5,32,256]{2,1,0:T(8,128)(2,1)S(1)}, u32[]{:S(2)}, u32[]{:S(2)}) %collective-permute-start.20) | collective-permute-done | bytes 81952 | tf_op jit(solution)/shard_map/ppermute | solution.py:23
  58.3 0.2 collective-permute-start.21
  58.6 1.2 %collective-permute-done.28 = bf16[4,32,256]{2,1,0:T(8,128)(2,1)S(1)} collective-permute-done((bf16[4,32,256]{2,1,0:T(8,128)(2,1)S(1)}, bf16[4,32,256]{2,1,0:T(8,128)(2,1)S(1)}, u32[]{:S(2)}, u32[]{:S(2)}) %collective-permute-start.28) | collective-permute-done | bytes 65568 | tf_op jit(solution)/shard_map/ppermute | solution.py:23
  59.8 0.1 collective-permute-start.29
  59.8 0.0 collective-permute-done.16
  59.9 0.5 slice.175
  60.5 0.6 copy.12
  61.1 1.7 %collective-permute-start.25 = (bf16[5,32,256]{2,1,0:T(8,128)(2,1)S(1)}, bf16[5,32,256]{2,1,0:T(8,128)(2,1)S(1)}, u32[]{:S(2)}, u32[]{:S(2)}) collective-permute-start(bf16[5,32,256]{2,1,0:T(8,128)(2,1)S(1)} %fusion.5), channel_id=1, source_target_pairs={{0,4},{4,0},{8,12},{12,8},{1,5},{5,1},{9,13},{13,9},{2,6},{6,2},{1... | collective-permute-start | bytes 245768 | tf_op jit(solution)/shard_map/ppermute | solution.py:23
  62.8 0.1 collective-permute-start.24
  63.6 0.6 collective-permute-start.22
  64.2 1.7 %collective-permute-done.25 = bf16[5,32,256]{2,1,0:T(8,128)(2,1)S(1)} collective-permute-done((bf16[5,32,256]{2,1,0:T(8,128)(2,1)S(1)}, bf16[5,32,256]{2,1,0:T(8,128)(2,1)S(1)}, u32[]{:S(2)}, u32[]{:S(2)}) %collective-permute-start.25) | collective-permute-done | bytes 81952 | tf_op jit(solution)/shard_map/ppermute | solution.py:23
  66.0 0.1 collective-permute-start.27
  66.1 0.1 broadcast_select_fusion.5
  66.2 1.2 %collective-permute-done.27 = bf16[5,64,256]{2,1,0:T(8,128)(2,1)S(1)} collective-permute-done((bf16[5,64,256]{2,1,0:T(8,128)(2,1)S(1)}, bf16[5,64,256]{2,1,0:T(8,128)(2,1)S(1)}, u32[]{:S(2)}, u32[]{:S(2)}) %collective-permute-start.27) | collective-permute-done | bytes 163872 | tf_op jit(solution)/shard_map/ppermute | solution.py:23
  67.4 0.1 broadcast_select_fusion.3
  67.5 0.1 maximum_maximum_fusion
  67.6 1.7 %convert.5 = f32[2,9,128,256]{3,2,1,0:T(8,128)} convert(bf16[2,9,128,256]{3,2,1,0:T(8,128)(2,1)S(1)} %bitcast.40) | non-fusion elementwise | flops 589824 | bytes 3538944 | tf_op jit(solution)/shard_map/convert_element_type | solution.py:644
  (65 shorter events, 1.1 us)
Async XLA Ops:
  1.8 8.3 %collective-permute-start = (bf16[6,128,128]{2,1,0:T(8,128)(2,1)S(1)}, bf16[6,128,128]{2,1,0:T(8,128)(2,1)S(1)}, u32[]{:S(2)}, u32[]{:S(2)}) collective-permute-start(bf16[6,128,128]{2,1,0:T(8,128)(2,1)S(1)} %pad_maximum_fusion.2), channel_id=1, source_target_pairs={{0,1},{1,0},{2,3},{3,2},{4,5},{5,4},{6,7},{7,6},{8,9},{9,8},{10,11... | collective-permute-start | bytes 589832 | tf_op jit(solution)/shard_map/ppermute | solution.py:23
  7.2 11.2 %collective-permute-start.5 = (bf16[9,128,128]{2,1,0:T(8,128)(2,1)S(1)}, bf16[9,128,128]{2,1,0:T(8,128)(2,1)S(1)}, u32[]{:S(2)}, u32[]{:S(2)}) collective-permute-start(bf16[9,128,128]{2,1,0:T(8,128)(2,1)S(1)} %get-tuple-element.46), channel_id=1, source_target_pairs={{0,1},{1,0},{2,3},{3,2},{4,5},{5,4},{6,7},{7,6},{8,9},{9,8},{10,11... | collective-permute-start | bytes 884744 | tf_op jit(solution)/shard_map/ppermute | solution.py:23
  10.3 11.1 %collective-permute-start.1 = (bf16[392,256]{1,0:T(8,128)(2,1)S(1)}, bf16[392,256]{1,0:T(8,128)(2,1)S(1)}, u32[]{:S(2)}, u32[]{:S(2)}) collective-permute-start(bf16[392,256]{1,0:T(8,128)(2,1)S(1)} %fusion.2), channel_id=1, source_target_pairs={{0,4},{4,8},{8,12},{1,5},{5,9},{9,13},{2,6},{6,10},{10,14},{3,7},{... | collective-permute-start | bytes 602120 | tf_op jit(solution)/shard_map/ppermute | solution.py:29
  14.8 7.8 %collective-permute-start.2 = (bf16[392,256]{1,0:T(8,128)(2,1)}, bf16[392,256]{1,0:T(8,128)(2,1)S(1)}, u32[]{:S(2)}, u32[]{:S(2)}) collective-permute-start(bf16[392,256]{1,0:T(8,128)(2,1)} %fusion.3), channel_id=1, source_target_pairs={{4,0},{8,4},{12,8},{5,1},{9,5},{13,9},{6,2},{10,6},{14,10},{7,3},{... | collective-permute-start | bytes 602120 | tf_op jit(solution)/shard_map/ppermute | solution.py:29
  16.1 5.2 %collective-permute-start.3 = (bf16[2,128,128]{2,1,0:T(8,128)(2,1)S(1)}, bf16[2,128,128]{2,1,0:T(8,128)(2,1)S(1)}, u32[]{:S(2)}, u32[]{:S(2)}) collective-permute-start(bf16[2,128,128]{2,1,0:T(8,128)(2,1)S(1)} %slice.182), channel_id=1, source_target_pairs={{0,1},{1,0},{2,3},{3,2},{4,5},{5,4},{6,7},{7,6},{8,9},{9,8},{10,11... | collective-permute-start | bytes 196616 | tf_op jit(solution)/shard_map/ppermute | solution.py:23
  18.3 9.1 %collective-permute-start.8 = (bf16[9,128,128]{2,1,0:T(8,128)(2,1)S(1)}, bf16[9,128,128]{2,1,0:T(8,128)(2,1)S(1)}, u32[]{:S(2)}, u32[]{:S(2)}) collective-permute-start(bf16[9,128,128]{2,1,0:T(8,128)(2,1)S(1)} %get-tuple-element.52), channel_id=1, source_target_pairs={{0,1},{1,0},{2,3},{3,2},{4,5},{5,4},{6,7},{7,6},{8,9},{9,8},{10,11... | collective-permute-start | bytes 884744 | tf_op jit(solution)/shard_map/ppermute | solution.py:23
  18.4 5.8 %collective-permute-start.6 = (bf16[9,128,128]{2,1,0:T(8,128)(2,1)S(1)}, bf16[9,128,128]{2,1,0:T(8,128)(2,1)S(1)}, u32[]{:S(2)}, u32[]{:S(2)}) collective-permute-start(bf16[9,128,128]{2,1,0:T(8,128)(2,1)S(1)} %collective-permute-done.5.refs_1_), channel_id=1, source_target_pairs={{0,2},{2,0},{1,3},{3,1},{4,6},{6,4},{5,7},{7,5},{8,10},{10,8},{9,1... | collective-permute-start | bytes 884744 | tf_op jit(solution)/shard_map/ppermute | solution.py:23
  22.7 6.4 %copy-start = (bf16[8,3,256]{2,0,1:T(8,128)(2,1)S(1)}, bf16[8,3,256]{2,0,1:T(8,128)(2,1)}, u32[]{:S(2)}) copy-start(bf16[8,3,256]{2,0,1:T(8,128)(2,1)} %param.8) | copy-start | bytes 36868
  22.8 1.4 %collective-permute-start.4 = (bf16[14,16,256]{2,1,0:T(8,128)(2,1)S(1)}, bf16[14,16,256]{2,1,0:T(8,128)(2,1)S(1)}, u32[]{:S(2)}, u32[]{:S(2)}) collective-permute-start(bf16[14,16,256]{2,1,0:T(8,128)(2,1)S(1)} %pad_maximum_fusion.7), channel_id=1, source_target_pairs={{0,2},{2,0},{1,3},{3,1},{4,6},{6,4},{5,7},{7,5},{8,10},{10,8},{9,1... | collective-permute-start | bytes 344072 | tf_op jit(solution)/shard_map/ppermute | solution.py:23
  27.4 1.7 %collective-permute-start.9 = (bf16[9,128,128]{2,1,0:T(8,128)(2,1)S(1)}, bf16[9,128,128]{2,1,0:T(8,128)(2,1)S(1)}, u32[]{:S(2)}, u32[]{:S(2)}) collective-permute-start(bf16[9,128,128]{2,1,0:T(8,128)(2,1)S(1)} %collective-permute-done.8.refs_1_), channel_id=1, source_target_pairs={{0,2},{2,0},{1,3},{3,1},{4,6},{6,4},{5,7},{7,5},{8,10},{10,8},{9,1... | collective-permute-start | bytes 884744 | tf_op jit(solution)/shard_map/ppermute | solution.py:23
  27.7 1.4 %collective-permute-start.7 = (bf16[10,8,16]{2,1,0:T(8,128)(2,1)S(1)}, bf16[10,8,16]{2,1,0:T(8,128)(2,1)S(1)}, u32[]{:S(2)}, u32[]{:S(2)}) collective-permute-start(bf16[10,8,16]{2,1,0:T(8,128)(2,1)S(1)} %slice_select_fusion.3), channel_id=1, source_target_pairs={{0,2},{2,0},{1,3},{3,1},{4,6},{6,4},{5,7},{7,5},{8,10},{10,8},{9,1... | collective-permute-start | bytes 7688 | tf_op jit(solution)/shard_map/ppermute | solution.py:23
  36.0 1.6 %collective-permute-start.10 = (f32[256,256]{1,0:T(8,128)S(1)}, f32[256,256]{1,0:T(8,128)S(1)}, u32[]{:S(2)}, u32[]{:S(2)}) collective-permute-start(f32[256,256]{1,0:T(8,128)S(1)} %get-tuple-element.55), channel_id=1, source_target_pairs={{0,2},{2,0},{1,3},{3,1},{4,6},{6,4},{5,7},{7,5},{8,10},{10,8},{9,1... | collective-permute-start | bytes 786440 | tf_op jit(solution)/shard_map/ppermute | solution.py:23
  36.3 3.0 %collective-permute-start.15 = (f32[256,256]{1,0:T(8,128)S(1)}, f32[256,256]{1,0:T(8,128)S(1)}, u32[]{:S(2)}, u32[]{:S(2)}) collective-permute-start(f32[256,256]{1,0:T(8,128)S(1)} %get-tuple-element.60), channel_id=1, source_target_pairs={{0,2},{2,0},{1,3},{3,1},{4,6},{6,4},{5,7},{7,5},{8,10},{10,8},{9,1... | collective-permute-start | bytes 786440 | tf_op jit(solution)/shard_map/ppermute | solution.py:23
  36.6 3.3 %collective-permute-start.18 = (f32[320,256]{1,0:T(8,128)S(1)}, f32[320,256]{1,0:T(8,128)S(1)}, u32[]{:S(2)}, u32[]{:S(2)}) collective-permute-start(f32[320,256]{1,0:T(8,128)S(1)} %get-tuple-element.63), channel_id=1, source_target_pairs={{0,2},{2,0},{1,3},{3,1},{4,6},{6,4},{5,7},{7,5},{8,10},{10,8},{9,1... | collective-permute-start | bytes 983048 | tf_op jit(solution)/shard_map/ppermute | solution.py:23
  36.8 10.1 %collective-permute-start.13 = (f32[336,256]{1,0:T(8,128)S(1)}, f32[336,256]{1,0:T(8,128)S(1)}, u32[]{:S(2)}, u32[]{:S(2)}) collective-permute-start(f32[336,256]{1,0:T(8,128)S(1)} %get-tuple-element.57), channel_id=1, source_target_pairs={{0,2},{2,0},{1,3},{3,1},{4,6},{6,4},{5,7},{7,5},{8,10},{10,8},{9,1... | collective-permute-start | bytes 1032200 | tf_op jit(solution)/shard_map/ppermute | solution.py:23
  37.7 4.4 %collective-permute-start.11 = (bf16[4,32,256]{2,1,0:T(8,128)(2,1)S(1)}, bf16[4,32,256]{2,1,0:T(8,128)(2,1)S(1)}, u32[]{:S(2)}, u32[]{:S(2)}) collective-permute-start(bf16[4,32,256]{2,1,0:T(8,128)(2,1)S(1)} %reduce-precision_convert_fusion.3), channel_id=1, source_target_pairs={{0,4},{4,0},{8,12},{12,8},{1,5},{5,1},{9,13},{13,9},{2,6},{6,2},{1... | collective-permute-start | bytes 196616 | tf_op jit(solution)/shard_map/ppermute | solution.py:23
  39.4 5.7 %collective-permute-start.17 = (bf16[4,32,256]{2,1,0:T(8,128)(2,1)S(1)}, bf16[4,32,256]{2,1,0:T(8,128)(2,1)S(1)}, u32[]{:S(2)}, u32[]{:S(2)}) collective-permute-start(bf16[4,32,256]{2,1,0:T(8,128)(2,1)S(1)} %reduce-precision_convert_fusion.2), channel_id=1, source_target_pairs={{0,4},{4,0},{8,12},{12,8},{1,5},{5,1},{9,13},{13,9},{2,6},{6,2},{1... | collective-permute-start | bytes 196616 | tf_op jit(solution)/shard_map/ppermute | solution.py:23
  40.0 10.4 %collective-permute-start.19 = (bf16[5,32,256]{2,1,0:T(8,128)(2,1)S(1)}, bf16[5,32,256]{2,1,0:T(8,128)(2,1)S(1)}, u32[]{:S(2)}, u32[]{:S(2)}) collective-permute-start(bf16[5,32,256]{2,1,0:T(8,128)(2,1)S(1)} %reduce-precision_convert_fusion), channel_id=1, source_target_pairs={{0,4},{4,0},{8,12},{12,8},{1,5},{5,1},{9,13},{13,9},{2,6},{6,2},{1... | collective-permute-start | bytes 245768 | tf_op jit(solution)/shard_map/ppermute | solution.py:23
  42.1 7.8 %collective-permute-start.12 = (bf16[4,32,256]{2,1,0:T(8,128)(2,1)S(1)}, bf16[4,32,256]{2,1,0:T(8,128)(2,1)S(1)}, u32[]{:S(2)}, u32[]{:S(2)}) collective-permute-start(bf16[4,32,256]{2,1,0:T(8,128)(2,1)S(1)} %fusion.13), channel_id=1, source_target_pairs={{0,8},{4,12},{8,0},{12,4},{1,9},{5,13},{9,1},{13,5},{2,10},{6,14},... | collective-permute-start | bytes 196616 | tf_op jit(solution)/shard_map/ppermute | solution.py:23
  45.1 8.6 %collective-permute-start.26 = (bf16[4,32,256]{2,1,0:T(8,128)(2,1)S(1)}, bf16[4,32,256]{2,1,0:T(8,128)(2,1)S(1)}, u32[]{:S(2)}, u32[]{:S(2)}) collective-permute-start(bf16[4,32,256]{2,1,0:T(8,128)(2,1)S(1)} %fusion.14), channel_id=1, source_target_pairs={{0,8},{4,12},{8,0},{12,4},{1,9},{5,13},{9,1},{13,5},{2,10},{6,14},... | collective-permute-start | bytes 196616 | tf_op jit(solution)/shard_map/ppermute | solution.py:23
  47.0 6.8 %collective-permute-start.14 = (bf16[208,256]{1,0:T(8,128)(2,1)S(1)}, bf16[208,256]{1,0:T(8,128)(2,1)S(1)}, u32[]{:S(2)}, u32[]{:S(2)}) collective-permute-start(bf16[208,256]{1,0:T(8,128)(2,1)S(1)} %pad_maximum_fusion.8), channel_id=1, source_target_pairs={{0,4},{4,0},{8,12},{12,8},{1,5},{5,1},{9,13},{13,9},{2,6},{6,2},{1... | collective-permute-start | bytes 319496 | tf_op jit(solution)/shard_map/ppermute | solution.py:23
  50.0 12.8 %collective-permute-start.23 = (bf16[4,32,256]{2,1,0:T(8,128)(2,1)S(1)}, bf16[4,32,256]{2,1,0:T(8,128)(2,1)S(1)}, u32[]{:S(2)}, u32[]{:S(2)}) collective-permute-start(bf16[4,32,256]{2,1,0:T(8,128)(2,1)S(1)} %add_convert_fusion.2), channel_id=1, source_target_pairs={{0,4},{4,0},{8,12},{12,8},{1,5},{5,1},{9,13},{13,9},{2,6},{6,2},{1... | collective-permute-start | bytes 196616 | tf_op jit(solution)/shard_map/ppermute | solution.py:23
  50.4 7.9 %collective-permute-start.20 = (bf16[5,32,256]{2,1,0:T(8,128)(2,1)S(1)}, bf16[5,32,256]{2,1,0:T(8,128)(2,1)S(1)}, u32[]{:S(2)}, u32[]{:S(2)}) collective-permute-start(bf16[5,32,256]{2,1,0:T(8,128)(2,1)S(1)} %fusion.15), channel_id=1, source_target_pairs={{0,8},{4,12},{8,0},{12,4},{1,9},{5,13},{9,1},{13,5},{2,10},{6,14},... | collective-permute-start | bytes 245768 | tf_op jit(solution)/shard_map/ppermute | solution.py:23
  53.7 6.0 %collective-permute-start.28 = (bf16[4,32,256]{2,1,0:T(8,128)(2,1)S(1)}, bf16[4,32,256]{2,1,0:T(8,128)(2,1)S(1)}, u32[]{:S(2)}, u32[]{:S(2)}) collective-permute-start(bf16[4,32,256]{2,1,0:T(8,128)(2,1)S(1)} %add_convert_fusion.1), channel_id=1, source_target_pairs={{0,4},{4,0},{8,12},{12,8},{1,5},{5,1},{9,13},{13,9},{2,6},{6,2},{1... | collective-permute-start | bytes 196616 | tf_op jit(solution)/shard_map/ppermute | solution.py:23
  53.9 6.0 %collective-permute-start.16 = (bf16[208,256]{1,0:T(8,128)(2,1)S(1)}, bf16[208,256]{1,0:T(8,128)(2,1)S(1)}, u32[]{:S(2)}, u32[]{:S(2)}) collective-permute-start(bf16[208,256]{1,0:T(8,128)(2,1)S(1)} %pad_maximum_fusion.9), channel_id=1, source_target_pairs={{0,8},{4,12},{8,0},{12,4},{1,9},{5,13},{9,1},{13,5},{2,10},{6,14},... | collective-permute-start | bytes 319496 | tf_op jit(solution)/shard_map/ppermute | solution.py:23
  58.3 5.2 %collective-permute-start.21 = (bf16[5,32,256]{2,1,0:T(8,128)(2,1)S(1)}, bf16[5,32,256]{2,1,0:T(8,128)(2,1)S(1)}, u32[]{:S(2)}, u32[]{:S(2)}) collective-permute-start(bf16[5,32,256]{2,1,0:T(8,128)(2,1)S(1)} %add_convert_fusion), channel_id=1, source_target_pairs={{0,4},{4,0},{8,12},{12,8},{1,5},{5,1},{9,13},{13,9},{2,6},{6,2},{1... | collective-permute-start | bytes 245768 | tf_op jit(solution)/shard_map/ppermute | solution.py:23
  59.8 4.4 %collective-permute-start.29 = (bf16[4,64,256]{2,1,0:T(8,128)(2,1)S(1)}, bf16[4,64,256]{2,1,0:T(8,128)(2,1)S(1)}, u32[]{:S(2)}, u32[]{:S(2)}) collective-permute-start(bf16[4,64,256]{2,1,0:T(8,128)(2,1)S(1)} %pad_maximum_fusion.6), channel_id=1, source_target_pairs={{0,2},{2,0},{1,3},{3,1},{4,6},{6,4},{5,7},{7,5},{8,10},{10,8},{9,1... | collective-permute-start | bytes 393224 | tf_op jit(solution)/shard_map/ppermute | solution.py:23
  61.1 4.8 %collective-permute-start.25 = (bf16[5,32,256]{2,1,0:T(8,128)(2,1)S(1)}, bf16[5,32,256]{2,1,0:T(8,128)(2,1)S(1)}, u32[]{:S(2)}, u32[]{:S(2)}) collective-permute-start(bf16[5,32,256]{2,1,0:T(8,128)(2,1)S(1)} %fusion.5), channel_id=1, source_target_pairs={{0,4},{4,0},{8,12},{12,8},{1,5},{5,1},{9,13},{13,9},{2,6},{6,2},{1... | collective-permute-start | bytes 245768 | tf_op jit(solution)/shard_map/ppermute | solution.py:23
  62.8 3.2 %collective-permute-start.24 = (bf16[4,64,256]{2,1,0:T(8,128)(2,1)S(1)}, bf16[4,64,256]{2,1,0:T(8,128)(2,1)S(1)}, u32[]{:S(2)}, u32[]{:S(2)}) collective-permute-start(bf16[4,64,256]{2,1,0:T(8,128)(2,1)S(1)} %pad_maximum_fusion.5), channel_id=1, source_target_pairs={{0,2},{2,0},{1,3},{3,1},{4,6},{6,4},{5,7},{7,5},{8,10},{10,8},{9,1... | collective-permute-start | bytes 393224 | tf_op jit(solution)/shard_map/ppermute | solution.py:23
  63.6 2.5 %collective-permute-start.22 = (bf16[5,64,256]{2,1,0:T(8,128)(2,1)S(1)}, bf16[5,64,256]{2,1,0:T(8,128)(2,1)S(1)}, u32[]{:S(2)}, u32[]{:S(2)}) collective-permute-start(bf16[5,64,256]{2,1,0:T(8,128)(2,1)S(1)} %pad_maximum_fusion.3), channel_id=1, source_target_pairs={{0,2},{2,0},{1,3},{3,1},{4,6},{6,4},{5,7},{7,5},{8,10},{10,8},{9,1... | collective-permute-start | bytes 491528 | tf_op jit(solution)/shard_map/ppermute | solution.py:23
  66.0 1.5 %collective-permute-start.27 = (bf16[5,64,256]{2,1,0:T(8,128)(2,1)S(1)}, bf16[5,64,256]{2,1,0:T(8,128)(2,1)S(1)}, u32[]{:S(2)}, u32[]{:S(2)}) collective-permute-start(bf16[5,64,256]{2,1,0:T(8,128)(2,1)S(1)} %pad_maximum_fusion.4), channel_id=1, source_target_pairs={{0,2},{2,0},{1,3},{3,1},{4,6},{6,4},{5,7},{7,5},{8,10},{10,8},{9,1... | collective-permute-start | bytes 491528 | tf_op jit(solution)/shard_map/ppermute | solution.py:23

commit v4 on v3

--- a/solution.py
+++ b/solution.py
@@ -15,7 +15,10 @@
 BF16 = jnp.bfloat16
 VMEM = pl.BlockSpec(memory_space=pltpu.VMEM)
 SMEM = pl.BlockSpec(memory_space=pltpu.SMEM)
-PARAMS = pltpu.CompilerParams(vmem_limit_bytes=14 * 1024 * 1024)
+
+
+def limited(mebibytes):
+    return pltpu.CompilerParams(vmem_limit_bytes=mebibytes * 1024 * 1024)
 
 
 def swap(block, axis, distance=1):
@@ -121,12 +124,12 @@
 def kernel_grads(core, grad_ref, src_ref, base, stride, before, kept, sent):
     own = grad_ref.shape[1]
     cells = grad_ref.shape[0]
-    turned = grad_ref[...].T
+    turned = grad_ref[...].T.astype(BF16)
     moved = jnp.concatenate(
         [
-            pltpu.roll(turned, cells - 1, 1).astype(BF16),
-            turned.astype(BF16),
-            pltpu.roll(turned, 1, 1).astype(BF16),
+            pltpu.roll(turned, cells - 1, 1),
+            turned,
+            pltpu.roll(turned, 1, 1),
         ],
         axis=0,
     )
@@ -197,9 +200,10 @@
     row_at = scal[2]
     row_count = scal[3]
     slots = height + 2 * halo
-    lane = lax.broadcasted_iota(jnp.int32, tiles.shape[1:], 0)
+    tiles = [tiles[row * SLOT : (row + 1) * SLOT, :] for row in range(slots)]
+    lane = lax.broadcasted_iota(jnp.int32, tiles[0].shape, 0)
     near = (lane < SLOT // 2).astype(jnp.int32) != col
-    blank = jnp.zeros(tiles.shape[1:], BF16)
+    blank = jnp.zeros(tiles[0].shape, BF16)
     padded[:SLOT, :] = jnp.where(near & (col == 1), tiles[0], blank)
     for row in range(slots):
         at = SLOT + row * stride
@@ -254,8 +258,10 @@
     core, row_at, row_count = scal[1], scal[2], scal[3]
     beside = [block[block.shape[0] - 8 :, :width] for block in (above, below)]
     rows = beside[:1] + [lines[row] for row in range(height)] + beside[1:]
-    blank = jnp.zeros(tile.shape[1:], F32)
-    tiles = [blank] + [tile[row].astype(F32) for row in range(count)] + [blank]
+    blank = jnp.zeros((8, SLOT), F32)
+    begin = tile.shape[0] - 8 * count
+    tiles = [tile[begin + 8 * row : begin + 8 * row + 8, :SLOT].astype(F32) for row in range(count)]
+    tiles = [blank, *tiles, blank]
     parts = []
     for row in range(count + 1):
         parts.append(jnp.where(core == 1, tiles[row + 1], tiles[row]))
@@ -519,7 +525,7 @@
             pltpu.VMEM(trunk_weights.shape, BF16),
             pltpu.SemaphoreType.DMA((4,)),
         ],
-        compiler_params=PARAMS,
+        compiler_params=limited(4),
         name="prepare",
     )(
         scal,
@@ -548,8 +554,8 @@
         line = jnp.pad(line, ((0, 0), (0, channels - width)))
         return jnp.concatenate([block.reshape(-1, channels), line], axis=0)
 
-    top = shift(with_line(last, lines[-1]), "rows", 1)
-    bottom = shift(with_line(first, lines[0]), "rows", -1)
+    top, bottom = tied(with_line(last, lines[-1]), with_line(first, lines[0]))
+    top, bottom = shift(top, "rows", 1), shift(bottom, "rows", -1)
     if futs == 2:
         top, bottom, inner_theirs = tied(top, bottom, inner_theirs)
         inner = ordered(fut == 1, inner, inner_theirs, 2)
@@ -564,12 +570,13 @@
     def edge_of(block):
         return jnp.where(core == 0, block[..., -SLOT:, :], block[..., :SLOT, :])
 
+    line_rows = jnp.concatenate([line_of(top)[None], lines, line_of(bottom)[None]], axis=0)
+    edges = jnp.where(core == 0, line_rows[:, :, -SLOT:], line_rows[:, :, :SLOT])
+    edges = jnp.pad(edges.reshape(-1, SLOT), ((0, 0), (0, channels - SLOT)))
+    blocks = [edge_of(halo_rows(top)), edge_of(mid), edge_of(halo_rows(bottom))]
     tiles = swap(
-        jnp.concatenate([edge_of(halo_rows(top)), edge_of(mid), edge_of(halo_rows(bottom))], axis=0), "cols"
-    )
-    line_rows = jnp.concatenate([line_of(top)[None], lines, line_of(bottom)[None]], axis=0)
-    tile = swap(
-        jnp.where(core == 0, line_rows[:, :, -SLOT:], line_rows[:, :, :SLOT]), "cols"
+        jnp.concatenate([block.reshape(-1, channels) for block in blocks] + [edges], axis=0),
+        "cols",
     )
     heads_w = jnp.transpose(head_weights, (1, 0, 2)).reshape(3 * fut_total, channels)
 
@@ -590,7 +597,7 @@
         out_specs=(VMEM,) * 3,
         scratch_shapes=[pltpu.VMEM((3 * channels, 3 * channels), BF16)]
         + [pltpu.VMEM((first_cells + 16, channels), F32)] * 3,
-        compiler_params=PARAMS,
+        compiler_params=limited(8),
         name="first_layer",
     )(scal, mid, top, bottom, tiles, *taps)
 
@@ -617,9 +624,9 @@
             pltpu.VMEM((own_cells, own), F32),
             pltpu.VMEM((3 * channels, 3 * own), BF16),
         ],
-        compiler_params=PARAMS,
+        compiler_params=limited(12),
         name="last_layer",
-    )(scal, active, slope, padded, heads_w, lines, top, bottom, tile, *taps)
+    )(scal, active, slope, padded, heads_w, lines, top, bottom, tiles, *taps)
 
     kept, sent = parts[: len(CHUNKS)], parts[len(CHUNKS) :]
     if rows_total == 4:

time: 70.8 us -> 70.2 us (level)
    ppermute x28 -> x27, starting transfers between devices: 24.9 us -> 24.5 us  [swap(): return lax.ppermute(block, axis, [(i, i ^ distance) for i in range(count)])]
    ppermute x28 -> x27, waiting for transfers between devices: 17.7 us -> 18 us  [swap(): return lax.ppermute(block, axis, [(i, i ^ distance) for i in range(count)])]
  transfers between devices with their start and end apart: 30 -> 29, of which waited for: 12 -> 12; matrix products, arithmetic and copies ran while one was open for 4% -> 4% of each run, Pallas kernels for 8% -> 8%
where the time goes in v4:
time: 70.2 us; the launch traced here: 70 us
  starting transfers between devices  29.7 us (42%)
  waiting for transfers between devices  19.1 us (27%)
  Pallas kernels  12.2 us (17%)
  other arithmetic  3.78 us (5%)
  between operations  2.88 us (4%)
  local copies, waits for them, and re-layouts  2.36 us (3%)
    ppermute x27, starting transfers between devices, swap(): return lax.ppermute(block, axis, [(i, i ^ distance) for i in range(count)])  24.5 us
    ppermute x27, waiting for transfers between devices, swap(): return lax.ppermute(block, axis, [(i, i ^ distance) for i in range(count)])  18 us
    pallas_call x1, Pallas kernels, local(): pl.pallas_call(functools.partial(last_layer, geom, scale), out_shape=kept...  6.79 us
    ppermute x2, starting transfers between devices, shift(): return lax.ppermute(block, axis, pairs)  5.15 us
    pallas_call x1, Pallas kernels, local(): pl.pallas_call(functools.partial(first_layer, geom), out_shape=(shape((ce...  3.11 us
    pallas_call x1, Pallas kernels, local(): pl.pallas_call(prepare, out_shape=(shape((height, 8, width), BF16),) + (s...  2.25 us
    unnamed x4, local copies, waits for them, and re-layouts  1.76 us
    convert_element_type x1, other arithmetic, local(): jnp.concatenate(taps_of, axis=0).astype(F32)  1.67 us
  transfers between devices with their start and end apart: 29, of which 12 were waited for; matrix products, arithmetic and copies ran while one was open for 4% of the time, Pallas kernels for 8%

profile of v4, /device:TPU:0, one launch (start us, length us, event | category | flops | bytes accessed | tf_op | source)
XLA Modules:
  0.0 70.0 jit_solution(18331540385730275919)
XLA Ops:
  0.6 1.2 %copy.11 = bf16[128,8,128]{0,2,1:T(8,128)(2,1)S(1)} copy(bf16[128,8,128]{2,1,0:T(8,128)(2,1)} %param.6) | data formatting | bytes 524288 | tf_op args[0]
  1.8 3.0 %collective-permute-start = (bf16[6,128,128]{2,1,0:T(8,128)(2,1)S(1)}, bf16[6,128,128]{2,1,0:T(8,128)(2,1)S(1)}, u32[]{:S(2)}, u32[]{:S(2)}) collective-permute-start(bf16[6,128,128]{2,1,0:T(8,128)(2,1)S(1)} %pad_maximum_fusion.2), channel_id=1, source_target_pairs={{0,1},{1,0},{2,3},{3,2},{4,5},{5,4},{6,7},{7,6},{8,9},{9,8},{10,11... | collective-permute-start | bytes 589832 | tf_op jit(solution)/shard_map/ppermute | solution.py:26
  4.8 0.1 pad_add_fusion.scal
  4.9 2.3 %prepare.1 = (bf16[8,8,128]{2,1,0:T(8,128)(2,1)S(1)}, bf16[9,256,128]{2,1,0:T(8,128)(2,1)S(1)}, bf16[9,256,128]{2,1,0:T(8,128)(2,1)S(1)}, bf16[9,128,128]{2,1,0:T(8,128)(2,1)S(1)}, bf16[9,128,128]{2,1,0:T(8,128)(2,1)S(1)}) custom-call(s32[4]{0:T(128)S(1)} %pad_add_fusion.scal, s32[8,128]{1,0:T(8,128)} %labels_in.1, f32[2,8,128]{2,1,0:T(8,128)} %flow_in.1, ...), custom_call_target="tpu_custom_call" | custom-call | tf_op jit(solution)/shard_map/prepare/pallas_call | solution.py:514
  7.2 0.1 collective-permute-start.5
  7.3 2.9 %collective-permute-done = bf16[6,128,128]{2,1,0:T(8,128)(2,1)S(1)} collective-permute-done((bf16[6,128,128]{2,1,0:T(8,128)(2,1)S(1)}, bf16[6,128,128]{2,1,0:T(8,128)(2,1)S(1)}, u32[]{:S(2)}, u32[]{:S(2)}) %collective-permute-start) | collective-permute-done | bytes 196640 | tf_op jit(solution)/shard_map/ppermute | solution.py:26
  10.2 0.7 %fusion.3 = (bf16[392,256]{1,0:T(8,128)(2,1)}, bf16[392,256]{1,0:T(8,128)(2,1)S(1)}) fusion(bf16[8,128]{1,0:T(8,128)(2,1)S(1)} %get-tuple-element.120, bf16[384,256]{1,0:T(8,128)(2,1)S(1)} %bitcast.53, bf16[8,128]{1,0:T(8,128)(2,1)S(1)} %get-tuple-element.119, bf16[384,256]{1,0:T(8,128)(2,1)S(1)} %bitcast.52), kind=kLoop, calls=%fused_computation.10 | loop fusion | flops 1103872 | bytes 798720 | tf_op jit(solution)/shard_map/concatenate | solution.py:555
  10.9 3.9 %collective-permute-start.1 = (bf16[392,256]{1,0:T(8,128)(2,1)}, bf16[392,256]{1,0:T(8,128)(2,1)S(1)}, u32[]{:S(2)}, u32[]{:S(2)}) collective-permute-start(bf16[392,256]{1,0:T(8,128)(2,1)} %get-tuple-element.43), channel_id=1, source_target_pairs={{0,4},{4,8},{8,12},{1,5},{5,9},{9,13},{2,6},{6,10},{10,14},{3,7},{... | collective-permute-start | bytes 602120 | tf_op jit(solution)/shard_map/ppermute | solution.py:32
  14.8 1.3 %collective-permute-start.2 = (bf16[392,256]{1,0:T(8,128)(2,1)S(1)}, bf16[392,256]{1,0:T(8,128)(2,1)S(1)}, u32[]{:S(2)}, u32[]{:S(2)}) collective-permute-start(bf16[392,256]{1,0:T(8,128)(2,1)S(1)} %get-tuple-element.44), channel_id=1, source_target_pairs={{4,0},{8,4},{12,8},{5,1},{9,5},{13,9},{6,2},{10,6},{14,10},{7,3},{... | collective-permute-start | bytes 602120 | tf_op jit(solution)/shard_map/ppermute | solution.py:32
  16.1 2.2 %collective-permute-start.3 = (bf16[2,128,128]{2,1,0:T(8,128)(2,1)S(1)}, bf16[2,128,128]{2,1,0:T(8,128)(2,1)S(1)}, u32[]{:S(2)}, u32[]{:S(2)}) collective-permute-start(bf16[2,128,128]{2,1,0:T(8,128)(2,1)S(1)} %slice.182), channel_id=1, source_target_pairs={{0,1},{1,0},{2,3},{3,2},{4,5},{5,4},{6,7},{7,6},{8,9},{9,8},{10,11... | collective-permute-start | bytes 196616 | tf_op jit(solution)/shard_map/ppermute | solution.py:26
  18.3 0.1 collective-permute-start.7
  18.4 0.0 collective-permute-done.5.refs_1_
  18.4 2.9 %collective-permute-done.3 = bf16[2,128,128]{2,1,0:T(8,128)(2,1)S(1)} collective-permute-done((bf16[2,128,128]{2,1,0:T(8,128)(2,1)S(1)}, bf16[2,128,128]{2,1,0:T(8,128)(2,1)S(1)}, u32[]{:S(2)}, u32[]{:S(2)}) %collective-permute-start.3) | collective-permute-done | bytes 65568 | tf_op jit(solution)/shard_map/ppermute | solution.py:26
  21.3 1.1 %collective-permute-done.2.bottom.below = bf16[392,256]{1,0:T(8,128)(2,1)S(1)} collective-permute-done((bf16[392,256]{1,0:T(8,128)(2,1)S(1)}, bf16[392,256]{1,0:T(8,128)(2,1)S(1)}, u32[]{:S(2)}, u32[]{:S(2)}) %collective-permute-start.2) | collective-permute-done | bytes 200736 | tf_op jit(solution)/shard_map/ppermute | solution.py:32
  22.4 0.0 copy-start
  22.6 0.1 fusion.9
  22.7 0.1 collective-permute-start.4
  22.8 1.4 %collective-permute-done.4.tiles.tile = bf16[304,256]{1,0:T(8,128)(2,1)S(1)} collective-permute-done((bf16[304,256]{1,0:T(8,128)(2,1)S(1)}, bf16[304,256]{1,0:T(8,128)(2,1)S(1)}, u32[]{:S(2)}, u32[]{:S(2)}) %collective-permute-start.4) | collective-permute-done | bytes 155680 | tf_op jit(solution)/shard_map/ppermute | solution.py:26
  24.2 0.0 collective-permute-done.6.refs_2_
  24.2 3.1 %first_layer.1 = (bf16[2032,256]{1,0:T(8,128)(2,1)S(1)}, bf16[1744,256]{1,0:T(8,128)(2,1)S(1)}, f32[1024,128]{1,0:T(8,128)S(1)}) custom-call(s32[4]{0:T(128)S(1)} %pad_add_fusion.scal, bf16[8,128,256]{2,1,0:T(8,128)(2,1)S(1)} %pad_maximum_fusion.mid, bf16[392,256]{1,0:T(8,128)(2,1)S(1)} %collective-permute-done.1.top.above, ...), custom_call_target="tpu_custom_call" | custom-call | tf_op jit(solution)/shard_map/first_layer/pallas_call | solution.py:589
  27.3 0.0 collective-permute-done.7.refs_1_
  27.3 0.2 collective-permute-start.8
  27.5 1.4 %collective-permute-done.8.refs_2_ = bf16[9,128,128]{2,1,0:T(8,128)(2,1)S(1)} collective-permute-done((bf16[9,128,128]{2,1,0:T(8,128)(2,1)S(1)}, bf16[9,128,128]{2,1,0:T(8,128)(2,1)S(1)}, u32[]{:S(2)}, u32[]{:S(2)}) %collective-permute-start.8) | collective-permute-done | bytes 294944 | tf_op jit(solution)/shard_map/ppermute | solution.py:26
  29.0 6.8 %last_layer.1 = (f32[320,256]{1,0:T(8,128)S(1)}, f32[256,256]{1,0:T(8,128)S(1)}, f32[320,256]{1,0:T(8,128)S(1)}, f32[256,256]{1,0:T(8,128)S(1)}, f32[336,256]{1,...) custom-call(s32[4]{0:T(128)S(1)} %pad_add_fusion.scal, ...), custom_call_target="tpu_custom_call" | custom-call | tf_op jit(solution)/shard_map/last_layer/pallas_call | solution.py:613
  35.7 0.2 collective-permute-start.9
  36.0 0.4 collective-permute-start.14
  36.3 0.1 collective-permute-start.17
  36.5 0.4 collective-permute-start.12
  36.8 0.5 collective-permute-done.9
  37.4 1.6 %collective-permute-start.10 = (bf16[4,32,256]{2,1,0:T(8,128)(2,1)S(1)}, bf16[4,32,256]{2,1,0:T(8,128)(2,1)S(1)}, u32[]{:S(2)}, u32[]{:S(2)}) collective-permute-start(bf16[4,32,256]{2,1,0:T(8,128)(2,1)S(1)} %reduce-precision_convert_fusion.3), channel_id=1, source_target_pairs={{0,4},{4,0},{8,12},{12,8},{1,5},{5,1},{9,13},{13,9},{2,6},{6,2},{1... | collective-permute-start | bytes 196616 | tf_op jit(solution)/shard_map/ppermute | solution.py:26
  39.0 0.0 collective-permute-done.14
  39.1 0.5 collective-permute-start.16
  39.7 1.6 %collective-permute-start.18 = (bf16[5,32,256]{2,1,0:T(8,128)(2,1)S(1)}, bf16[5,32,256]{2,1,0:T(8,128)(2,1)S(1)}, u32[]{:S(2)}, u32[]{:S(2)}) collective-permute-start(bf16[5,32,256]{2,1,0:T(8,128)(2,1)S(1)} %reduce-precision_convert_fusion), channel_id=1, source_target_pairs={{0,4},{4,0},{8,12},{12,8},{1,5},{5,1},{9,13},{13,9},{2,6},{6,2},{1... | collective-permute-start | bytes 245768 | tf_op jit(solution)/shard_map/ppermute | solution.py:26
  41.3 0.5 collective-permute-done.10
  41.9 2.7 %collective-permute-start.11 = (bf16[4,32,256]{2,1,0:T(8,128)(2,1)S(1)}, bf16[4,32,256]{2,1,0:T(8,128)(2,1)S(1)}, u32[]{:S(2)}, u32[]{:S(2)}) collective-permute-start(bf16[4,32,256]{2,1,0:T(8,128)(2,1)S(1)} %fusion.16), channel_id=1, source_target_pairs={{0,8},{4,12},{8,0},{12,4},{1,9},{5,13},{9,1},{13,5},{2,10},{6,14},... | collective-permute-start | bytes 196616 | tf_op jit(solution)/shard_map/ppermute | solution.py:26
  44.6 0.0 collective-permute-done.16
  44.6 2.2 %collective-permute-start.25 = (bf16[4,32,256]{2,1,0:T(8,128)(2,1)S(1)}, bf16[4,32,256]{2,1,0:T(8,128)(2,1)S(1)}, u32[]{:S(2)}, u32[]{:S(2)}) collective-permute-start(bf16[4,32,256]{2,1,0:T(8,128)(2,1)S(1)} %fusion.17), channel_id=1, source_target_pairs={{0,8},{4,12},{8,0},{12,4},{1,9},{5,13},{9,1},{13,5},{2,10},{6,14},... | collective-permute-start | bytes 196616 | tf_op jit(solution)/shard_map/ppermute | solution.py:26
  46.8 0.0 collective-permute-done.12
  46.9 1.3 %collective-permute-start.13 = (bf16[208,256]{1,0:T(8,128)(2,1)S(1)}, bf16[208,256]{1,0:T(8,128)(2,1)S(1)}, u32[]{:S(2)}, u32[]{:S(2)}) collective-permute-start(bf16[208,256]{1,0:T(8,128)(2,1)S(1)} %pad_maximum_fusion.7), channel_id=1, source_target_pairs={{0,4},{4,0},{8,12},{12,8},{1,5},{5,1},{9,13},{13,9},{2,6},{6,2},{1... | collective-permute-start | bytes 319496 | tf_op jit(solution)/shard_map/ppermute | solution.py:26
  48.2 1.4 %collective-permute-done.11 = bf16[4,32,256]{2,1,0:T(8,128)(2,1)S(1)} collective-permute-done((bf16[4,32,256]{2,1,0:T(8,128)(2,1)S(1)}, bf16[4,32,256]{2,1,0:T(8,128)(2,1)S(1)}, u32[]{:S(2)}, u32[]{:S(2)}) %collective-permute-start.11) | collective-permute-done | bytes 65568 | tf_op jit(solution)/shard_map/ppermute | solution.py:26
  49.7 0.4 collective-permute-start.22
  50.1 0.0 collective-permute-done.18
  50.1 2.9 %collective-permute-start.19 = (bf16[5,32,256]{2,1,0:T(8,128)(2,1)S(1)}, bf16[5,32,256]{2,1,0:T(8,128)(2,1)S(1)}, u32[]{:S(2)}, u32[]{:S(2)}) collective-permute-start(bf16[5,32,256]{2,1,0:T(8,128)(2,1)S(1)} %fusion.18), channel_id=1, source_target_pairs={{0,8},{4,12},{8,0},{12,4},{1,9},{5,13},{9,1},{13,5},{2,10},{6,14},... | collective-permute-start | bytes 245768 | tf_op jit(solution)/shard_map/ppermute | solution.py:26
  53.1 0.1 collective-permute-start.27
  53.3 1.8 %collective-permute-start.15 = (bf16[208,256]{1,0:T(8,128)(2,1)S(1)}, bf16[208,256]{1,0:T(8,128)(2,1)S(1)}, u32[]{:S(2)}, u32[]{:S(2)}) collective-permute-start(bf16[208,256]{1,0:T(8,128)(2,1)S(1)} %pad_maximum_fusion.8), channel_id=1, source_target_pairs={{0,8},{4,12},{8,0},{12,4},{1,9},{5,13},{9,1},{13,5},{2,10},{6,14},... | collective-permute-start | bytes 319496 | tf_op jit(solution)/shard_map/ppermute | solution.py:26
  55.1 2.8 %collective-permute-done.19 = bf16[5,32,256]{2,1,0:T(8,128)(2,1)S(1)} collective-permute-done((bf16[5,32,256]{2,1,0:T(8,128)(2,1)S(1)}, bf16[5,32,256]{2,1,0:T(8,128)(2,1)S(1)}, u32[]{:S(2)}, u32[]{:S(2)}) %collective-permute-start.19) | collective-permute-done | bytes 81952 | tf_op jit(solution)/shard_map/ppermute | solution.py:26
  58.0 0.3 collective-permute-start.20
  58.3 1.0 %collective-permute-done.27 = bf16[4,32,256]{2,1,0:T(8,128)(2,1)S(1)} collective-permute-done((bf16[4,32,256]{2,1,0:T(8,128)(2,1)S(1)}, bf16[4,32,256]{2,1,0:T(8,128)(2,1)S(1)}, u32[]{:S(2)}, u32[]{:S(2)}) %collective-permute-start.27) | collective-permute-done | bytes 65568 | tf_op jit(solution)/shard_map/ppermute | solution.py:26
  59.3 0.1 collective-permute-start.28
  59.4 0.0 collective-permute-done.15
  59.5 0.1 fusion.6
  59.5 0.5 slice.175
  60.1 0.6 copy.12
  60.7 1.5 %collective-permute-start.24 = (bf16[5,32,256]{2,1,0:T(8,128)(2,1)S(1)}, bf16[5,32,256]{2,1,0:T(8,128)(2,1)S(1)}, u32[]{:S(2)}, u32[]{:S(2)}) collective-permute-start(bf16[5,32,256]{2,1,0:T(8,128)(2,1)S(1)} %fusion.6), channel_id=1, source_target_pairs={{0,4},{4,0},{8,12},{12,8},{1,5},{5,1},{9,13},{13,9},{2,6},{6,2},{1... | collective-permute-start | bytes 245768 | tf_op jit(solution)/shard_map/ppermute | solution.py:26
  62.2 0.1 collective-permute-start.23
  63.0 0.6 collective-permute-start.21
  63.6 0.0 collective-permute-done.28
  63.6 1.9 %collective-permute-done.24 = bf16[5,32,256]{2,1,0:T(8,128)(2,1)S(1)} collective-permute-done((bf16[5,32,256]{2,1,0:T(8,128)(2,1)S(1)}, bf16[5,32,256]{2,1,0:T(8,128)(2,1)S(1)}, u32[]{:S(2)}, u32[]{:S(2)}) %collective-permute-start.24) | collective-permute-done | bytes 81952 | tf_op jit(solution)/shard_map/ppermute | solution.py:26
  65.5 0.1 collective-permute-start.26
  65.7 0.1 broadcast_select_fusion.5
  65.8 1.2 %collective-permute-done.26 = bf16[5,64,256]{2,1,0:T(8,128)(2,1)S(1)} collective-permute-done((bf16[5,64,256]{2,1,0:T(8,128)(2,1)S(1)}, bf16[5,64,256]{2,1,0:T(8,128)(2,1)S(1)}, u32[]{:S(2)}, u32[]{:S(2)}) %collective-permute-start.26) | collective-permute-done | bytes 163872 | tf_op jit(solution)/shard_map/ppermute | solution.py:26
  67.0 0.1 broadcast_select_fusion.3
  67.1 0.1 maximum_maximum_fusion
  67.2 1.7 %convert.5 = f32[2,9,128,256]{3,2,1,0:T(8,128)} convert(bf16[2,9,128,256]{3,2,1,0:T(8,128)(2,1)S(1)} %bitcast.45) | non-fusion elementwise | flops 589824 | bytes 3538944 | tf_op jit(solution)/shard_map/convert_element_type | solution.py:651
  (64 shorter events, 1.1 us)
Async XLA Ops:
  1.8 8.3 %collective-permute-start = (bf16[6,128,128]{2,1,0:T(8,128)(2,1)S(1)}, bf16[6,128,128]{2,1,0:T(8,128)(2,1)S(1)}, u32[]{:S(2)}, u32[]{:S(2)}) collective-permute-start(bf16[6,128,128]{2,1,0:T(8,128)(2,1)S(1)} %pad_maximum_fusion.2), channel_id=1, source_target_pairs={{0,1},{1,0},{2,3},{3,2},{4,5},{5,4},{6,7},{7,6},{8,9},{9,8},{10,11... | collective-permute-start | bytes 589832 | tf_op jit(solution)/shard_map/ppermute | solution.py:26
  7.2 11.2 %collective-permute-start.5 = (bf16[9,128,128]{2,1,0:T(8,128)(2,1)S(1)}, bf16[9,128,128]{2,1,0:T(8,128)(2,1)S(1)}, u32[]{:S(2)}, u32[]{:S(2)}) collective-permute-start(bf16[9,128,128]{2,1,0:T(8,128)(2,1)S(1)} %get-tuple-element.50), channel_id=1, source_target_pairs={{0,1},{1,0},{2,3},{3,2},{4,5},{5,4},{6,7},{7,6},{8,9},{9,8},{10,11... | collective-permute-start | bytes 884744 | tf_op jit(solution)/shard_map/ppermute | solution.py:26
  10.9 10.4 %collective-permute-start.1 = (bf16[392,256]{1,0:T(8,128)(2,1)}, bf16[392,256]{1,0:T(8,128)(2,1)S(1)}, u32[]{:S(2)}, u32[]{:S(2)}) collective-permute-start(bf16[392,256]{1,0:T(8,128)(2,1)} %get-tuple-element.43), channel_id=1, source_target_pairs={{0,4},{4,8},{8,12},{1,5},{5,9},{9,13},{2,6},{6,10},{10,14},{3,7},{... | collective-permute-start | bytes 602120 | tf_op jit(solution)/shard_map/ppermute | solution.py:32
  14.8 7.6 %collective-permute-start.2 = (bf16[392,256]{1,0:T(8,128)(2,1)S(1)}, bf16[392,256]{1,0:T(8,128)(2,1)S(1)}, u32[]{:S(2)}, u32[]{:S(2)}) collective-permute-start(bf16[392,256]{1,0:T(8,128)(2,1)S(1)} %get-tuple-element.44), channel_id=1, source_target_pairs={{4,0},{8,4},{12,8},{5,1},{9,5},{13,9},{6,2},{10,6},{14,10},{7,3},{... | collective-permute-start | bytes 602120 | tf_op jit(solution)/shard_map/ppermute | solution.py:32
  16.1 5.2 %collective-permute-start.3 = (bf16[2,128,128]{2,1,0:T(8,128)(2,1)S(1)}, bf16[2,128,128]{2,1,0:T(8,128)(2,1)S(1)}, u32[]{:S(2)}, u32[]{:S(2)}) collective-permute-start(bf16[2,128,128]{2,1,0:T(8,128)(2,1)S(1)} %slice.182), channel_id=1, source_target_pairs={{0,1},{1,0},{2,3},{3,2},{4,5},{5,4},{6,7},{7,6},{8,9},{9,8},{10,11... | collective-permute-start | bytes 196616 | tf_op jit(solution)/shard_map/ppermute | solution.py:26
  18.3 9.0 %collective-permute-start.7 = (bf16[9,128,128]{2,1,0:T(8,128)(2,1)S(1)}, bf16[9,128,128]{2,1,0:T(8,128)(2,1)S(1)}, u32[]{:S(2)}, u32[]{:S(2)}) collective-permute-start(bf16[9,128,128]{2,1,0:T(8,128)(2,1)S(1)} %get-tuple-element.56), channel_id=1, source_target_pairs={{0,1},{1,0},{2,3},{3,2},{4,5},{5,4},{6,7},{7,6},{8,9},{9,8},{10,11... | collective-permute-start | bytes 884744 | tf_op jit(solution)/shard_map/ppermute | solution.py:26
  18.4 5.8 %collective-permute-start.6 = (bf16[9,128,128]{2,1,0:T(8,128)(2,1)S(1)}, bf16[9,128,128]{2,1,0:T(8,128)(2,1)S(1)}, u32[]{:S(2)}, u32[]{:S(2)}) collective-permute-start(bf16[9,128,128]{2,1,0:T(8,128)(2,1)S(1)} %collective-permute-done.5.refs_1_), channel_id=1, source_target_pairs={{0,2},{2,0},{1,3},{3,1},{4,6},{6,4},{5,7},{7,5},{8,10},{10,8},{9,1... | collective-permute-start | bytes 884744 | tf_op jit(solution)/shard_map/ppermute | solution.py:26
  22.4 6.5 %copy-start = (bf16[8,3,256]{2,0,1:T(8,128)(2,1)S(1)}, bf16[8,3,256]{2,0,1:T(8,128)(2,1)}, u32[]{:S(2)}) copy-start(bf16[8,3,256]{2,0,1:T(8,128)(2,1)} %param.8) | copy-start | bytes 36868
  22.7 1.4 %collective-permute-start.4 = (bf16[304,256]{1,0:T(8,128)(2,1)S(1)}, bf16[304,256]{1,0:T(8,128)(2,1)S(1)}, u32[]{:S(2)}, u32[]{:S(2)}) collective-permute-start(bf16[304,256]{1,0:T(8,128)(2,1)S(1)} %fusion.8), channel_id=1, source_target_pairs={{0,2},{2,0},{1,3},{3,1},{4,6},{6,4},{5,7},{7,5},{8,10},{10,8},{9,1... | collective-permute-start | bytes 466952 | tf_op jit(solution)/shard_map/ppermute | solution.py:26
  27.3 1.6 %collective-permute-start.8 = (bf16[9,128,128]{2,1,0:T(8,128)(2,1)S(1)}, bf16[9,128,128]{2,1,0:T(8,128)(2,1)S(1)}, u32[]{:S(2)}, u32[]{:S(2)}) collective-permute-start(bf16[9,128,128]{2,1,0:T(8,128)(2,1)S(1)} %collective-permute-done.7.refs_1_), channel_id=1, source_target_pairs={{0,2},{2,0},{1,3},{3,1},{4,6},{6,4},{5,7},{7,5},{8,10},{10,8},{9,1... | collective-permute-start | bytes 884744 | tf_op jit(solution)/shard_map/ppermute | solution.py:26
  35.7 1.6 %collective-permute-start.9 = (f32[256,256]{1,0:T(8,128)S(1)}, f32[256,256]{1,0:T(8,128)S(1)}, u32[]{:S(2)}, u32[]{:S(2)}) collective-permute-start(f32[256,256]{1,0:T(8,128)S(1)} %get-tuple-element.59), channel_id=1, source_target_pairs={{0,2},{2,0},{1,3},{3,1},{4,6},{6,4},{5,7},{7,5},{8,10},{10,8},{9,1... | collective-permute-start | bytes 786440 | tf_op jit(solution)/shard_map/ppermute | solution.py:26
  36.0 3.1 %collective-permute-start.14 = (f32[256,256]{1,0:T(8,128)S(1)}, f32[256,256]{1,0:T(8,128)S(1)}, u32[]{:S(2)}, u32[]{:S(2)}) collective-permute-start(f32[256,256]{1,0:T(8,128)S(1)} %get-tuple-element.64), channel_id=1, source_target_pairs={{0,2},{2,0},{1,3},{3,1},{4,6},{6,4},{5,7},{7,5},{8,10},{10,8},{9,1... | collective-permute-start | bytes 786440 | tf_op jit(solution)/shard_map/ppermute | solution.py:26
  36.3 3.3 %collective-permute-start.17 = (f32[320,256]{1,0:T(8,128)S(1)}, f32[320,256]{1,0:T(8,128)S(1)}, u32[]{:S(2)}, u32[]{:S(2)}) collective-permute-start(f32[320,256]{1,0:T(8,128)S(1)} %get-tuple-element.67), channel_id=1, source_target_pairs={{0,2},{2,0},{1,3},{3,1},{4,6},{6,4},{5,7},{7,5},{8,10},{10,8},{9,1... | collective-permute-start | bytes 983048 | tf_op jit(solution)/shard_map/ppermute | solution.py:26
  36.5 10.4 %collective-permute-start.12 = (f32[336,256]{1,0:T(8,128)S(1)}, f32[336,256]{1,0:T(8,128)S(1)}, u32[]{:S(2)}, u32[]{:S(2)}) collective-permute-start(f32[336,256]{1,0:T(8,128)S(1)} %get-tuple-element.61), channel_id=1, source_target_pairs={{0,2},{2,0},{1,3},{3,1},{4,6},{6,4},{5,7},{7,5},{8,10},{10,8},{9,1... | collective-permute-start | bytes 1032200 | tf_op jit(solution)/shard_map/ppermute | solution.py:26
  37.4 4.5 %collective-permute-start.10 = (bf16[4,32,256]{2,1,0:T(8,128)(2,1)S(1)}, bf16[4,32,256]{2,1,0:T(8,128)(2,1)S(1)}, u32[]{:S(2)}, u32[]{:S(2)}) collective-permute-start(bf16[4,32,256]{2,1,0:T(8,128)(2,1)S(1)} %reduce-precision_convert_fusion.3), channel_id=1, source_target_pairs={{0,4},{4,0},{8,12},{12,8},{1,5},{5,1},{9,13},{13,9},{2,6},{6,2},{1... | collective-permute-start | bytes 196616 | tf_op jit(solution)/shard_map/ppermute | solution.py:26
  39.1 5.5 %collective-permute-start.16 = (bf16[4,32,256]{2,1,0:T(8,128)(2,1)S(1)}, bf16[4,32,256]{2,1,0:T(8,128)(2,1)S(1)}, u32[]{:S(2)}, u32[]{:S(2)}) collective-permute-start(bf16[4,32,256]{2,1,0:T(8,128)(2,1)S(1)} %reduce-precision_convert_fusion.2), channel_id=1, source_target_pairs={{0,4},{4,0},{8,12},{12,8},{1,5},{5,1},{9,13},{13,9},{2,6},{6,2},{1... | collective-permute-start | bytes 196616 | tf_op jit(solution)/shard_map/ppermute | solution.py:26
  39.7 10.4 %collective-permute-start.18 = (bf16[5,32,256]{2,1,0:T(8,128)(2,1)S(1)}, bf16[5,32,256]{2,1,0:T(8,128)(2,1)S(1)}, u32[]{:S(2)}, u32[]{:S(2)}) collective-permute-start(bf16[5,32,256]{2,1,0:T(8,128)(2,1)S(1)} %reduce-precision_convert_fusion), channel_id=1, source_target_pairs={{0,4},{4,0},{8,12},{12,8},{1,5},{5,1},{9,13},{13,9},{2,6},{6,2},{1... | collective-permute-start | bytes 245768 | tf_op jit(solution)/shard_map/ppermute | solution.py:26
  41.9 7.7 %collective-permute-start.11 = (bf16[4,32,256]{2,1,0:T(8,128)(2,1)S(1)}, bf16[4,32,256]{2,1,0:T(8,128)(2,1)S(1)}, u32[]{:S(2)}, u32[]{:S(2)}) collective-permute-start(bf16[4,32,256]{2,1,0:T(8,128)(2,1)S(1)} %fusion.16), channel_id=1, source_target_pairs={{0,8},{4,12},{8,0},{12,4},{1,9},{5,13},{9,1},{13,5},{2,10},{6,14},... | collective-permute-start | bytes 196616 | tf_op jit(solution)/shard_map/ppermute | solution.py:26
  44.6 8.4 %collective-permute-start.25 = (bf16[4,32,256]{2,1,0:T(8,128)(2,1)S(1)}, bf16[4,32,256]{2,1,0:T(8,128)(2,1)S(1)}, u32[]{:S(2)}, u32[]{:S(2)}) collective-permute-start(bf16[4,32,256]{2,1,0:T(8,128)(2,1)S(1)} %fusion.17), channel_id=1, source_target_pairs={{0,8},{4,12},{8,0},{12,4},{1,9},{5,13},{9,1},{13,5},{2,10},{6,14},... | collective-permute-start | bytes 196616 | tf_op jit(solution)/shard_map/ppermute | solution.py:26
  46.9 6.2 %collective-permute-start.13 = (bf16[208,256]{1,0:T(8,128)(2,1)S(1)}, bf16[208,256]{1,0:T(8,128)(2,1)S(1)}, u32[]{:S(2)}, u32[]{:S(2)}) collective-permute-start(bf16[208,256]{1,0:T(8,128)(2,1)S(1)} %pad_maximum_fusion.7), channel_id=1, source_target_pairs={{0,4},{4,0},{8,12},{12,8},{1,5},{5,1},{9,13},{13,9},{2,6},{6,2},{1... | collective-permute-start | bytes 319496 | tf_op jit(solution)/shard_map/ppermute | solution.py:26
  49.7 12.5 %collective-permute-start.22 = (bf16[4,32,256]{2,1,0:T(8,128)(2,1)S(1)}, bf16[4,32,256]{2,1,0:T(8,128)(2,1)S(1)}, u32[]{:S(2)}, u32[]{:S(2)}) collective-permute-start(bf16[4,32,256]{2,1,0:T(8,128)(2,1)S(1)} %add_convert_fusion.2), channel_id=1, source_target_pairs={{0,4},{4,0},{8,12},{12,8},{1,5},{5,1},{9,13},{13,9},{2,6},{6,2},{1... | collective-permute-start | bytes 196616 | tf_op jit(solution)/shard_map/ppermute | solution.py:26
  50.1 7.8 %collective-permute-start.19 = (bf16[5,32,256]{2,1,0:T(8,128)(2,1)S(1)}, bf16[5,32,256]{2,1,0:T(8,128)(2,1)S(1)}, u32[]{:S(2)}, u32[]{:S(2)}) collective-permute-start(bf16[5,32,256]{2,1,0:T(8,128)(2,1)S(1)} %fusion.18), channel_id=1, source_target_pairs={{0,8},{4,12},{8,0},{12,4},{1,9},{5,13},{9,1},{13,5},{2,10},{6,14},... | collective-permute-start | bytes 245768 | tf_op jit(solution)/shard_map/ppermute | solution.py:26
  53.1 6.2 %collective-permute-start.27 = (bf16[4,32,256]{2,1,0:T(8,128)(2,1)S(1)}, bf16[4,32,256]{2,1,0:T(8,128)(2,1)S(1)}, u32[]{:S(2)}, u32[]{:S(2)}) collective-permute-start(bf16[4,32,256]{2,1,0:T(8,128)(2,1)S(1)} %add_convert_fusion.1), channel_id=1, source_target_pairs={{0,4},{4,0},{8,12},{12,8},{1,5},{5,1},{9,13},{13,9},{2,6},{6,2},{1... | collective-permute-start | bytes 196616 | tf_op jit(solution)/shard_map/ppermute | solution.py:26
  53.3 6.1 %collective-permute-start.15 = (bf16[208,256]{1,0:T(8,128)(2,1)S(1)}, bf16[208,256]{1,0:T(8,128)(2,1)S(1)}, u32[]{:S(2)}, u32[]{:S(2)}) collective-permute-start(bf16[208,256]{1,0:T(8,128)(2,1)S(1)} %pad_maximum_fusion.8), channel_id=1, source_target_pairs={{0,8},{4,12},{8,0},{12,4},{1,9},{5,13},{9,1},{13,5},{2,10},{6,14},... | collective-permute-start | bytes 319496 | tf_op jit(solution)/shard_map/ppermute | solution.py:26
  58.0 5.0 %collective-permute-start.20 = (bf16[5,32,256]{2,1,0:T(8,128)(2,1)S(1)}, bf16[5,32,256]{2,1,0:T(8,128)(2,1)S(1)}, u32[]{:S(2)}, u32[]{:S(2)}) collective-permute-start(bf16[5,32,256]{2,1,0:T(8,128)(2,1)S(1)} %add_convert_fusion), channel_id=1, source_target_pairs={{0,4},{4,0},{8,12},{12,8},{1,5},{5,1},{9,13},{13,9},{2,6},{6,2},{1... | collective-permute-start | bytes 245768 | tf_op jit(solution)/shard_map/ppermute | solution.py:26
  59.3 4.2 %collective-permute-start.28 = (bf16[4,64,256]{2,1,0:T(8,128)(2,1)S(1)}, bf16[4,64,256]{2,1,0:T(8,128)(2,1)S(1)}, u32[]{:S(2)}, u32[]{:S(2)}) collective-permute-start(bf16[4,64,256]{2,1,0:T(8,128)(2,1)S(1)} %pad_maximum_fusion.6), channel_id=1, source_target_pairs={{0,2},{2,0},{1,3},{3,1},{4,6},{6,4},{5,7},{7,5},{8,10},{10,8},{9,1... | collective-permute-start | bytes 393224 | tf_op jit(solution)/shard_map/ppermute | solution.py:26
  60.7 4.8 %collective-permute-start.24 = (bf16[5,32,256]{2,1,0:T(8,128)(2,1)S(1)}, bf16[5,32,256]{2,1,0:T(8,128)(2,1)S(1)}, u32[]{:S(2)}, u32[]{:S(2)}) collective-permute-start(bf16[5,32,256]{2,1,0:T(8,128)(2,1)S(1)} %fusion.6), channel_id=1, source_target_pairs={{0,4},{4,0},{8,12},{12,8},{1,5},{5,1},{9,13},{13,9},{2,6},{6,2},{1... | collective-permute-start | bytes 245768 | tf_op jit(solution)/shard_map/ppermute | solution.py:26
  62.2 3.4 %collective-permute-start.23 = (bf16[4,64,256]{2,1,0:T(8,128)(2,1)S(1)}, bf16[4,64,256]{2,1,0:T(8,128)(2,1)S(1)}, u32[]{:S(2)}, u32[]{:S(2)}) collective-permute-start(bf16[4,64,256]{2,1,0:T(8,128)(2,1)S(1)} %pad_maximum_fusion.5), channel_id=1, source_target_pairs={{0,2},{2,0},{1,3},{3,1},{4,6},{6,4},{5,7},{7,5},{8,10},{10,8},{9,1... | collective-permute-start | bytes 393224 | tf_op jit(solution)/shard_map/ppermute | solution.py:26
  63.0 2.7 %collective-permute-start.21 = (bf16[5,64,256]{2,1,0:T(8,128)(2,1)S(1)}, bf16[5,64,256]{2,1,0:T(8,128)(2,1)S(1)}, u32[]{:S(2)}, u32[]{:S(2)}) collective-permute-start(bf16[5,64,256]{2,1,0:T(8,128)(2,1)S(1)} %pad_maximum_fusion.3), channel_id=1, source_target_pairs={{0,2},{2,0},{1,3},{3,1},{4,6},{6,4},{5,7},{7,5},{8,10},{10,8},{9,1... | collective-permute-start | bytes 491528 | tf_op jit(solution)/shard_map/ppermute | solution.py:26
  65.5 1.5 %collective-permute-start.26 = (bf16[5,64,256]{2,1,0:T(8,128)(2,1)S(1)}, bf16[5,64,256]{2,1,0:T(8,128)(2,1)S(1)}, u32[]{:S(2)}, u32[]{:S(2)}) collective-permute-start(bf16[5,64,256]{2,1,0:T(8,128)(2,1)S(1)} %pad_maximum_fusion.4), channel_id=1, source_target_pairs={{0,2},{2,0},{1,3},{3,1},{4,6},{6,4},{5,7},{7,5},{8,10},{10,8},{9,1... | collective-permute-start | bytes 491528 | tf_op jit(solution)/shard_map/ppermute | solution.py:26

commit v5 on v4

--- a/solution.py
+++ b/solution.py
@@ -483,6 +483,7 @@
     got = in_order([swap(block, "rows") for block in ready], ready)
     ready[-1], small = tied(ready[-1], small)
     ready = [ordered(bit == 1, mine, more, 1) for mine, more in zip(ready, got)]
+    ready = [jnp.concatenate([ready[i] for i in group], axis=0) for group in ((0,), (1,), (2, 3))]
     got = in_order([swap(block, "cols") for block in ready], ready)
     return [ordered(core == 1, mine, more, 1) for mine, more in zip(ready, got)], small
 

time: 70.2 us -> 69.8 us (level)
    ppermute x27 -> x26, starting transfers between devices: 24.5 us -> 24 us  [swap(): return lax.ppermute(block, axis, [(i, i ^ distance) for i in range(count)])]
    ppermute x27 -> x26, waiting for transfers between devices: 18 us -> 18.2 us  [swap(): return lax.ppermute(block, axis, [(i, i ^ distance) for i in range(count)])]
  transfers between devices with their start and end apart: 29 -> 28, of which waited for: 12 -> 12; matrix products, arithmetic and copies ran while one was open for 4% -> 4% of each run, Pallas kernels for 8% -> 8%
where the time goes in v5:
time: 69.8 us; the launch traced here: 69.6 us
  starting transfers between devices  29.1 us (42%)
  waiting for transfers between devices  19.3 us (28%)
  Pallas kernels  12.2 us (17%)
  other arithmetic  3.79 us (5%)
  between operations  2.88 us (4%)
  local copies, waits for them, and re-layouts  2.36 us (3%)
    ppermute x26, starting transfers between devices, swap(): return lax.ppermute(block, axis, [(i, i ^ distance) for i in range(count)])  24 us
    ppermute x26, waiting for transfers between devices, swap(): return lax.ppermute(block, axis, [(i, i ^ distance) for i in range(count)])  18.2 us
    pallas_call x1, Pallas kernels, local(): pl.pallas_call(functools.partial(last_layer, geom, scale), out_shape=kept...  6.79 us
    ppermute x2, starting transfers between devices, shift(): return lax.ppermute(block, axis, pairs)  5.15 us
    pallas_call x1, Pallas kernels, local(): pl.pallas_call(functools.partial(first_layer, geom), out_shape=(shape((ce...  3.11 us
    pallas_call x1, Pallas kernels, local(): pl.pallas_call(prepare, out_shape=(shape((height, 8, width), BF16),) + (s...  2.25 us
    unnamed x4, local copies, waits for them, and re-layouts  1.76 us
    convert_element_type x1, other arithmetic, local(): jnp.concatenate(taps_of, axis=0).astype(F32)  1.67 us
  transfers between devices with their start and end apart: 28, of which 12 were waited for; matrix products, arithmetic and copies ran while one was open for 4% of the time, Pallas kernels for 8%

profile of v5, /device:TPU:0, one launch (start us, length us, event | category | flops | bytes accessed | tf_op | source)
XLA Modules:
  0.0 69.6 jit_solution(17408695442069620774)
XLA Ops:
  0.6 1.2 %copy.11 = bf16[128,8,128]{0,2,1:T(8,128)(2,1)S(1)} copy(bf16[128,8,128]{2,1,0:T(8,128)(2,1)} %param.6) | data formatting | bytes 524288 | tf_op args[0]
  1.8 3.0 %collective-permute-start = (bf16[6,128,128]{2,1,0:T(8,128)(2,1)S(1)}, bf16[6,128,128]{2,1,0:T(8,128)(2,1)S(1)}, u32[]{:S(2)}, u32[]{:S(2)}) collective-permute-start(bf16[6,128,128]{2,1,0:T(8,128)(2,1)S(1)} %pad_maximum_fusion.2), channel_id=1, source_target_pairs={{0,1},{1,0},{2,3},{3,2},{4,5},{5,4},{6,7},{7,6},{8,9},{9,8},{10,11... | collective-permute-start | bytes 589832 | tf_op jit(solution)/shard_map/ppermute | solution.py:26
  4.8 0.1 pad_add_fusion.scal
  4.9 2.3 %prepare.1 = (bf16[8,8,128]{2,1,0:T(8,128)(2,1)S(1)}, bf16[9,256,128]{2,1,0:T(8,128)(2,1)S(1)}, bf16[9,256,128]{2,1,0:T(8,128)(2,1)S(1)}, bf16[9,128,128]{2,1,0:T(8,128)(2,1)S(1)}, bf16[9,128,128]{2,1,0:T(8,128)(2,1)S(1)}) custom-call(s32[4]{0:T(128)S(1)} %pad_add_fusion.scal, s32[8,128]{1,0:T(8,128)} %labels_in.1, f32[2,8,128]{2,1,0:T(8,128)} %flow_in.1, ...), custom_call_target="tpu_custom_call" | custom-call | tf_op jit(solution)/shard_map/prepare/pallas_call | solution.py:515
  7.2 0.1 collective-permute-start.5
  7.3 2.9 %collective-permute-done = bf16[6,128,128]{2,1,0:T(8,128)(2,1)S(1)} collective-permute-done((bf16[6,128,128]{2,1,0:T(8,128)(2,1)S(1)}, bf16[6,128,128]{2,1,0:T(8,128)(2,1)S(1)}, u32[]{:S(2)}, u32[]{:S(2)}) %collective-permute-start) | collective-permute-done | bytes 196640 | tf_op jit(solution)/shard_map/ppermute | solution.py:26
  10.2 0.7 %fusion.3 = (bf16[392,256]{1,0:T(8,128)(2,1)}, bf16[392,256]{1,0:T(8,128)(2,1)S(1)}) fusion(bf16[8,128]{1,0:T(8,128)(2,1)S(1)} %get-tuple-element.116, bf16[384,256]{1,0:T(8,128)(2,1)S(1)} %bitcast.53, bf16[8,128]{1,0:T(8,128)(2,1)S(1)} %get-tuple-element.115, bf16[384,256]{1,0:T(8,128)(2,1)S(1)} %bitcast.52), kind=kLoop, calls=%fused_computation.13 | loop fusion | flops 1103872 | bytes 798720 | tf_op jit(solution)/shard_map/concatenate | solution.py:556
  10.9 3.9 %collective-permute-start.1 = (bf16[392,256]{1,0:T(8,128)(2,1)}, bf16[392,256]{1,0:T(8,128)(2,1)S(1)}, u32[]{:S(2)}, u32[]{:S(2)}) collective-permute-start(bf16[392,256]{1,0:T(8,128)(2,1)} %get-tuple-element.42), channel_id=1, source_target_pairs={{0,4},{4,8},{8,12},{1,5},{5,9},{9,13},{2,6},{6,10},{10,14},{3,7},{... | collective-permute-start | bytes 602120 | tf_op jit(solution)/shard_map/ppermute | solution.py:32
  14.8 1.3 %collective-permute-start.2 = (bf16[392,256]{1,0:T(8,128)(2,1)S(1)}, bf16[392,256]{1,0:T(8,128)(2,1)S(1)}, u32[]{:S(2)}, u32[]{:S(2)}) collective-permute-start(bf16[392,256]{1,0:T(8,128)(2,1)S(1)} %get-tuple-element.43), channel_id=1, source_target_pairs={{4,0},{8,4},{12,8},{5,1},{9,5},{13,9},{6,2},{10,6},{14,10},{7,3},{... | collective-permute-start | bytes 602120 | tf_op jit(solution)/shard_map/ppermute | solution.py:32
  16.1 2.2 %collective-permute-start.3 = (bf16[2,128,128]{2,1,0:T(8,128)(2,1)S(1)}, bf16[2,128,128]{2,1,0:T(8,128)(2,1)S(1)}, u32[]{:S(2)}, u32[]{:S(2)}) collective-permute-start(bf16[2,128,128]{2,1,0:T(8,128)(2,1)S(1)} %slice.182), channel_id=1, source_target_pairs={{0,1},{1,0},{2,3},{3,2},{4,5},{5,4},{6,7},{7,6},{8,9},{9,8},{10,11... | collective-permute-start | bytes 196616 | tf_op jit(solution)/shard_map/ppermute | solution.py:26
  18.3 0.1 collective-permute-start.7
  18.4 0.0 collective-permute-done.5.refs_1_
  18.4 0.0 collective-permute-start.6
  18.4 2.9 %collective-permute-done.3 = bf16[2,128,128]{2,1,0:T(8,128)(2,1)S(1)} collective-permute-done((bf16[2,128,128]{2,1,0:T(8,128)(2,1)S(1)}, bf16[2,128,128]{2,1,0:T(8,128)(2,1)S(1)}, u32[]{:S(2)}, u32[]{:S(2)}) %collective-permute-start.3) | collective-permute-done | bytes 65568 | tf_op jit(solution)/shard_map/ppermute | solution.py:26
  21.3 1.1 %collective-permute-done.2.bottom.below = bf16[392,256]{1,0:T(8,128)(2,1)S(1)} collective-permute-done((bf16[392,256]{1,0:T(8,128)(2,1)S(1)}, bf16[392,256]{1,0:T(8,128)(2,1)S(1)}, u32[]{:S(2)}, u32[]{:S(2)}) %collective-permute-start.2) | collective-permute-done | bytes 200736 | tf_op jit(solution)/shard_map/ppermute | solution.py:32
  22.4 0.0 copy-start
  22.6 0.1 fusion.9
  22.7 0.1 collective-permute-start.4
  22.8 1.4 %collective-permute-done.4.tiles.tile = bf16[304,256]{1,0:T(8,128)(2,1)S(1)} collective-permute-done((bf16[304,256]{1,0:T(8,128)(2,1)S(1)}, bf16[304,256]{1,0:T(8,128)(2,1)S(1)}, u32[]{:S(2)}, u32[]{:S(2)}) %collective-permute-start.4) | collective-permute-done | bytes 155680 | tf_op jit(solution)/shard_map/ppermute | solution.py:26
  24.2 0.0 collective-permute-done.6.refs_2_
  24.2 3.1 %first_layer.1 = (bf16[2032,256]{1,0:T(8,128)(2,1)S(1)}, bf16[1744,256]{1,0:T(8,128)(2,1)S(1)}, f32[1024,128]{1,0:T(8,128)S(1)}) custom-call(s32[4]{0:T(128)S(1)} %pad_add_fusion.scal, bf16[8,128,256]{2,1,0:T(8,128)(2,1)S(1)} %pad_maximum_fusion.mid, bf16[392,256]{1,0:T(8,128)(2,1)S(1)} %collective-permute-done.1.top.above, ...), custom_call_target="tpu_custom_call" | custom-call | tf_op jit(solution)/shard_map/first_layer/pallas_call | solution.py:590
  27.3 0.0 collective-permute-done.7.refs_1_
  27.3 0.2 collective-permute-start.8
  27.5 1.4 %collective-permute-done.8.refs_2_ = bf16[9,128,128]{2,1,0:T(8,128)(2,1)S(1)} collective-permute-done((bf16[9,128,128]{2,1,0:T(8,128)(2,1)S(1)}, bf16[9,128,128]{2,1,0:T(8,128)(2,1)S(1)}, u32[]{:S(2)}, u32[]{:S(2)}) %collective-permute-start.8) | collective-permute-done | bytes 294944 | tf_op jit(solution)/shard_map/ppermute | solution.py:26
  29.0 6.8 %last_layer.1 = (f32[320,256]{1,0:T(8,128)S(1)}, f32[256,256]{1,0:T(8,128)S(1)}, f32[320,256]{1,0:T(8,128)S(1)}, f32[256,256]{1,0:T(8,128)S(1)}, f32[336,256]{1,...) custom-call(s32[4]{0:T(128)S(1)} %pad_add_fusion.scal, ...), custom_call_target="tpu_custom_call" | custom-call | tf_op jit(solution)/shard_map/last_layer/pallas_call | solution.py:614
  35.7 0.2 collective-permute-start.9
  36.0 0.4 collective-permute-start.14
  36.3 0.1 collective-permute-start.17
  36.5 0.4 collective-permute-start.12
  36.8 0.5 collective-permute-done.9
  37.4 1.6 %collective-permute-start.10 = (bf16[4,32,256]{2,1,0:T(8,128)(2,1)S(1)}, bf16[4,32,256]{2,1,0:T(8,128)(2,1)S(1)}, u32[]{:S(2)}, u32[]{:S(2)}) collective-permute-start(bf16[4,32,256]{2,1,0:T(8,128)(2,1)S(1)} %reduce-precision_convert_fusion.3), channel_id=1, source_target_pairs={{0,4},{4,0},{8,12},{12,8},{1,5},{5,1},{9,13},{13,9},{2,6},{6,2},{1... | collective-permute-start | bytes 196616 | tf_op jit(solution)/shard_map/ppermute | solution.py:26
  39.0 0.0 collective-permute-done.14
  39.1 0.5 collective-permute-start.16
  39.7 1.6 %collective-permute-start.18 = (bf16[5,32,256]{2,1,0:T(8,128)(2,1)S(1)}, bf16[5,32,256]{2,1,0:T(8,128)(2,1)S(1)}, u32[]{:S(2)}, u32[]{:S(2)}) collective-permute-start(bf16[5,32,256]{2,1,0:T(8,128)(2,1)S(1)} %reduce-precision_convert_fusion), channel_id=1, source_target_pairs={{0,4},{4,0},{8,12},{12,8},{1,5},{5,1},{9,13},{13,9},{2,6},{6,2},{1... | collective-permute-start | bytes 245768 | tf_op jit(solution)/shard_map/ppermute | solution.py:26
  41.3 0.5 collective-permute-done.10
  41.9 2.7 %collective-permute-start.11 = (bf16[4,32,256]{2,1,0:T(8,128)(2,1)S(1)}, bf16[4,32,256]{2,1,0:T(8,128)(2,1)S(1)}, u32[]{:S(2)}, u32[]{:S(2)}) collective-permute-start(bf16[4,32,256]{2,1,0:T(8,128)(2,1)S(1)} %fusion.16), channel_id=1, source_target_pairs={{0,8},{4,12},{8,0},{12,4},{1,9},{5,13},{9,1},{13,5},{2,10},{6,14},... | collective-permute-start | bytes 196616 | tf_op jit(solution)/shard_map/ppermute | solution.py:26
  44.6 0.0 collective-permute-done.16
  44.6 2.2 %collective-permute-start.24 = (bf16[4,32,256]{2,1,0:T(8,128)(2,1)S(1)}, bf16[4,32,256]{2,1,0:T(8,128)(2,1)S(1)}, u32[]{:S(2)}, u32[]{:S(2)}) collective-permute-start(bf16[4,32,256]{2,1,0:T(8,128)(2,1)S(1)} %fusion.17), channel_id=1, source_target_pairs={{0,8},{4,12},{8,0},{12,4},{1,9},{5,13},{9,1},{13,5},{2,10},{6,14},... | collective-permute-start | bytes 196616 | tf_op jit(solution)/shard_map/ppermute | solution.py:26
  46.8 0.0 collective-permute-done.12
  46.9 1.3 %collective-permute-start.13 = (bf16[208,256]{1,0:T(8,128)(2,1)S(1)}, bf16[208,256]{1,0:T(8,128)(2,1)S(1)}, u32[]{:S(2)}, u32[]{:S(2)}) collective-permute-start(bf16[208,256]{1,0:T(8,128)(2,1)S(1)} %pad_maximum_fusion.5), channel_id=1, source_target_pairs={{0,4},{4,0},{8,12},{12,8},{1,5},{5,1},{9,13},{13,9},{2,6},{6,2},{1... | collective-permute-start | bytes 319496 | tf_op jit(solution)/shard_map/ppermute | solution.py:26
  48.2 1.4 %collective-permute-done.11 = bf16[4,32,256]{2,1,0:T(8,128)(2,1)S(1)} collective-permute-done((bf16[4,32,256]{2,1,0:T(8,128)(2,1)S(1)}, bf16[4,32,256]{2,1,0:T(8,128)(2,1)S(1)}, u32[]{:S(2)}, u32[]{:S(2)}) %collective-permute-start.11) | collective-permute-done | bytes 65568 | tf_op jit(solution)/shard_map/ppermute | solution.py:26
  49.7 0.4 collective-permute-start.21
  50.1 0.0 collective-permute-done.18
  50.1 2.9 %collective-permute-start.19 = (bf16[5,32,256]{2,1,0:T(8,128)(2,1)S(1)}, bf16[5,32,256]{2,1,0:T(8,128)(2,1)S(1)}, u32[]{:S(2)}, u32[]{:S(2)}) collective-permute-start(bf16[5,32,256]{2,1,0:T(8,128)(2,1)S(1)} %fusion.18), channel_id=1, source_target_pairs={{0,8},{4,12},{8,0},{12,4},{1,9},{5,13},{9,1},{13,5},{2,10},{6,14},... | collective-permute-start | bytes 245768 | tf_op jit(solution)/shard_map/ppermute | solution.py:26
  53.1 0.1 collective-permute-start.26
  53.3 1.8 %collective-permute-start.15 = (bf16[208,256]{1,0:T(8,128)(2,1)S(1)}, bf16[208,256]{1,0:T(8,128)(2,1)S(1)}, u32[]{:S(2)}, u32[]{:S(2)}) collective-permute-start(bf16[208,256]{1,0:T(8,128)(2,1)S(1)} %pad_maximum_fusion.6), channel_id=1, source_target_pairs={{0,8},{4,12},{8,0},{12,4},{1,9},{5,13},{9,1},{13,5},{2,10},{6,14},... | collective-permute-start | bytes 319496 | tf_op jit(solution)/shard_map/ppermute | solution.py:26
  55.1 2.8 %collective-permute-done.19 = bf16[5,32,256]{2,1,0:T(8,128)(2,1)S(1)} collective-permute-done((bf16[5,32,256]{2,1,0:T(8,128)(2,1)S(1)}, bf16[5,32,256]{2,1,0:T(8,128)(2,1)S(1)}, u32[]{:S(2)}, u32[]{:S(2)}) %collective-permute-start.19) | collective-permute-done | bytes 81952 | tf_op jit(solution)/shard_map/ppermute | solution.py:26
  58.0 0.3 collective-permute-start.20
  58.3 1.0 %collective-permute-done.26 = bf16[4,32,256]{2,1,0:T(8,128)(2,1)S(1)} collective-permute-done((bf16[4,32,256]{2,1,0:T(8,128)(2,1)S(1)}, bf16[4,32,256]{2,1,0:T(8,128)(2,1)S(1)}, u32[]{:S(2)}, u32[]{:S(2)}) %collective-permute-start.26) | collective-permute-done | bytes 65568 | tf_op jit(solution)/shard_map/ppermute | solution.py:26
  59.3 0.1 collective-permute-start.27
  59.4 0.0 collective-permute-done.15
  59.5 0.1 fusion.6
  59.5 0.6 copy.12
  60.2 1.5 %collective-permute-start.23 = (bf16[5,32,256]{2,1,0:T(8,128)(2,1)S(1)}, bf16[5,32,256]{2,1,0:T(8,128)(2,1)S(1)}, u32[]{:S(2)}, u32[]{:S(2)}) collective-permute-start(bf16[5,32,256]{2,1,0:T(8,128)(2,1)S(1)} %fusion.6), channel_id=1, source_target_pairs={{0,4},{4,0},{8,12},{12,8},{1,5},{5,1},{9,13},{13,9},{2,6},{6,2},{1... | collective-permute-start | bytes 245768 | tf_op jit(solution)/shard_map/ppermute | solution.py:26
  61.7 0.5 slice.175
  62.9 0.1 collective-permute-start.22
  63.0 0.0 collective-permute-done.27
  63.0 2.0 %collective-permute-done.23 = bf16[5,32,256]{2,1,0:T(8,128)(2,1)S(1)} collective-permute-done((bf16[5,32,256]{2,1,0:T(8,128)(2,1)S(1)}, bf16[5,32,256]{2,1,0:T(8,128)(2,1)S(1)}, u32[]{:S(2)}, u32[]{:S(2)}) %collective-permute-start.23) | collective-permute-done | bytes 81952 | tf_op jit(solution)/shard_map/ppermute | solution.py:26
  65.0 0.1 collective-permute-start.25
  65.2 1.3 %collective-permute-done.25 = bf16[5,64,256]{2,1,0:T(8,128)(2,1)S(1)} collective-permute-done((bf16[5,64,256]{2,1,0:T(8,128)(2,1)S(1)}, bf16[5,64,256]{2,1,0:T(8,128)(2,1)S(1)}, u32[]{:S(2)}, u32[]{:S(2)}) %collective-permute-start.25) | collective-permute-done | bytes 163872 | tf_op jit(solution)/shard_map/ppermute | solution.py:26
  66.5 0.1 broadcast_select_fusion.5
  66.6 0.1 broadcast_select_fusion.1
  66.7 0.1 maximum_maximum_fusion
  66.8 1.7 %convert.5 = f32[2,9,128,256]{3,2,1,0:T(8,128)} convert(bf16[2,9,128,256]{3,2,1,0:T(8,128)(2,1)S(1)} %bitcast.45) | non-fusion elementwise | flops 589824 | bytes 3538944 | tf_op jit(solution)/shard_map/convert_element_type | solution.py:652
  (60 shorter events, 1.0 us)
Async XLA Ops:
  1.8 8.3 %collective-permute-start = (bf16[6,128,128]{2,1,0:T(8,128)(2,1)S(1)}, bf16[6,128,128]{2,1,0:T(8,128)(2,1)S(1)}, u32[]{:S(2)}, u32[]{:S(2)}) collective-permute-start(bf16[6,128,128]{2,1,0:T(8,128)(2,1)S(1)} %pad_maximum_fusion.2), channel_id=1, source_target_pairs={{0,1},{1,0},{2,3},{3,2},{4,5},{5,4},{6,7},{7,6},{8,9},{9,8},{10,11... | collective-permute-start | bytes 589832 | tf_op jit(solution)/shard_map/ppermute | solution.py:26
  7.2 11.2 %collective-permute-start.5 = (bf16[9,128,128]{2,1,0:T(8,128)(2,1)S(1)}, bf16[9,128,128]{2,1,0:T(8,128)(2,1)S(1)}, u32[]{:S(2)}, u32[]{:S(2)}) collective-permute-start(bf16[9,128,128]{2,1,0:T(8,128)(2,1)S(1)} %get-tuple-element.49), channel_id=1, source_target_pairs={{0,1},{1,0},{2,3},{3,2},{4,5},{5,4},{6,7},{7,6},{8,9},{9,8},{10,11... | collective-permute-start | bytes 884744 | tf_op jit(solution)/shard_map/ppermute | solution.py:26
  10.9 10.4 %collective-permute-start.1 = (bf16[392,256]{1,0:T(8,128)(2,1)}, bf16[392,256]{1,0:T(8,128)(2,1)S(1)}, u32[]{:S(2)}, u32[]{:S(2)}) collective-permute-start(bf16[392,256]{1,0:T(8,128)(2,1)} %get-tuple-element.42), channel_id=1, source_target_pairs={{0,4},{4,8},{8,12},{1,5},{5,9},{9,13},{2,6},{6,10},{10,14},{3,7},{... | collective-permute-start | bytes 602120 | tf_op jit(solution)/shard_map/ppermute | solution.py:32
  14.8 7.6 %collective-permute-start.2 = (bf16[392,256]{1,0:T(8,128)(2,1)S(1)}, bf16[392,256]{1,0:T(8,128)(2,1)S(1)}, u32[]{:S(2)}, u32[]{:S(2)}) collective-permute-start(bf16[392,256]{1,0:T(8,128)(2,1)S(1)} %get-tuple-element.43), channel_id=1, source_target_pairs={{4,0},{8,4},{12,8},{5,1},{9,5},{13,9},{6,2},{10,6},{14,10},{7,3},{... | collective-permute-start | bytes 602120 | tf_op jit(solution)/shard_map/ppermute | solution.py:32
  16.1 5.2 %collective-permute-start.3 = (bf16[2,128,128]{2,1,0:T(8,128)(2,1)S(1)}, bf16[2,128,128]{2,1,0:T(8,128)(2,1)S(1)}, u32[]{:S(2)}, u32[]{:S(2)}) collective-permute-start(bf16[2,128,128]{2,1,0:T(8,128)(2,1)S(1)} %slice.182), channel_id=1, source_target_pairs={{0,1},{1,0},{2,3},{3,2},{4,5},{5,4},{6,7},{7,6},{8,9},{9,8},{10,11... | collective-permute-start | bytes 196616 | tf_op jit(solution)/shard_map/ppermute | solution.py:26
  18.3 9.0 %collective-permute-start.7 = (bf16[9,128,128]{2,1,0:T(8,128)(2,1)S(1)}, bf16[9,128,128]{2,1,0:T(8,128)(2,1)S(1)}, u32[]{:S(2)}, u32[]{:S(2)}) collective-permute-start(bf16[9,128,128]{2,1,0:T(8,128)(2,1)S(1)} %get-tuple-element.55), channel_id=1, source_target_pairs={{0,1},{1,0},{2,3},{3,2},{4,5},{5,4},{6,7},{7,6},{8,9},{9,8},{10,11... | collective-permute-start | bytes 884744 | tf_op jit(solution)/shard_map/ppermute | solution.py:26
  18.4 5.8 %collective-permute-start.6 = (bf16[9,128,128]{2,1,0:T(8,128)(2,1)S(1)}, bf16[9,128,128]{2,1,0:T(8,128)(2,1)S(1)}, u32[]{:S(2)}, u32[]{:S(2)}) collective-permute-start(bf16[9,128,128]{2,1,0:T(8,128)(2,1)S(1)} %collective-permute-done.5.refs_1_), channel_id=1, source_target_pairs={{0,2},{2,0},{1,3},{3,1},{4,6},{6,4},{5,7},{7,5},{8,10},{10,8},{9,1... | collective-permute-start | bytes 884744 | tf_op jit(solution)/shard_map/ppermute | solution.py:26
  22.4 6.5 %copy-start = (bf16[8,3,256]{2,0,1:T(8,128)(2,1)S(1)}, bf16[8,3,256]{2,0,1:T(8,128)(2,1)}, u32[]{:S(2)}) copy-start(bf16[8,3,256]{2,0,1:T(8,128)(2,1)} %param.8) | copy-start | bytes 36868
  22.7 1.4 %collective-permute-start.4 = (bf16[304,256]{1,0:T(8,128)(2,1)S(1)}, bf16[304,256]{1,0:T(8,128)(2,1)S(1)}, u32[]{:S(2)}, u32[]{:S(2)}) collective-permute-start(bf16[304,256]{1,0:T(8,128)(2,1)S(1)} %fusion.8), channel_id=1, source_target_pairs={{0,2},{2,0},{1,3},{3,1},{4,6},{6,4},{5,7},{7,5},{8,10},{10,8},{9,1... | collective-permute-start | bytes 466952 | tf_op jit(solution)/shard_map/ppermute | solution.py:26
  27.3 1.6 %collective-permute-start.8 = (bf16[9,128,128]{2,1,0:T(8,128)(2,1)S(1)}, bf16[9,128,128]{2,1,0:T(8,128)(2,1)S(1)}, u32[]{:S(2)}, u32[]{:S(2)}) collective-permute-start(bf16[9,128,128]{2,1,0:T(8,128)(2,1)S(1)} %collective-permute-done.7.refs_1_), channel_id=1, source_target_pairs={{0,2},{2,0},{1,3},{3,1},{4,6},{6,4},{5,7},{7,5},{8,10},{10,8},{9,1... | collective-permute-start | bytes 884744 | tf_op jit(solution)/shard_map/ppermute | solution.py:26
  35.7 1.6 %collective-permute-start.9 = (f32[256,256]{1,0:T(8,128)S(1)}, f32[256,256]{1,0:T(8,128)S(1)}, u32[]{:S(2)}, u32[]{:S(2)}) collective-permute-start(f32[256,256]{1,0:T(8,128)S(1)} %get-tuple-element.58), channel_id=1, source_target_pairs={{0,2},{2,0},{1,3},{3,1},{4,6},{6,4},{5,7},{7,5},{8,10},{10,8},{9,1... | collective-permute-start | bytes 786440 | tf_op jit(solution)/shard_map/ppermute | solution.py:26
  36.0 3.1 %collective-permute-start.14 = (f32[256,256]{1,0:T(8,128)S(1)}, f32[256,256]{1,0:T(8,128)S(1)}, u32[]{:S(2)}, u32[]{:S(2)}) collective-permute-start(f32[256,256]{1,0:T(8,128)S(1)} %get-tuple-element.63), channel_id=1, source_target_pairs={{0,2},{2,0},{1,3},{3,1},{4,6},{6,4},{5,7},{7,5},{8,10},{10,8},{9,1... | collective-permute-start | bytes 786440 | tf_op jit(solution)/shard_map/ppermute | solution.py:26
  36.3 3.3 %collective-permute-start.17 = (f32[320,256]{1,0:T(8,128)S(1)}, f32[320,256]{1,0:T(8,128)S(1)}, u32[]{:S(2)}, u32[]{:S(2)}) collective-permute-start(f32[320,256]{1,0:T(8,128)S(1)} %get-tuple-element.66), channel_id=1, source_target_pairs={{0,2},{2,0},{1,3},{3,1},{4,6},{6,4},{5,7},{7,5},{8,10},{10,8},{9,1... | collective-permute-start | bytes 983048 | tf_op jit(solution)/shard_map/ppermute | solution.py:26
  36.5 10.4 %collective-permute-start.12 = (f32[336,256]{1,0:T(8,128)S(1)}, f32[336,256]{1,0:T(8,128)S(1)}, u32[]{:S(2)}, u32[]{:S(2)}) collective-permute-start(f32[336,256]{1,0:T(8,128)S(1)} %get-tuple-element.60), channel_id=1, source_target_pairs={{0,2},{2,0},{1,3},{3,1},{4,6},{6,4},{5,7},{7,5},{8,10},{10,8},{9,1... | collective-permute-start | bytes 1032200 | tf_op jit(solution)/shard_map/ppermute | solution.py:26
  37.4 4.5 %collective-permute-start.10 = (bf16[4,32,256]{2,1,0:T(8,128)(2,1)S(1)}, bf16[4,32,256]{2,1,0:T(8,128)(2,1)S(1)}, u32[]{:S(2)}, u32[]{:S(2)}) collective-permute-start(bf16[4,32,256]{2,1,0:T(8,128)(2,1)S(1)} %reduce-precision_convert_fusion.3), channel_id=1, source_target_pairs={{0,4},{4,0},{8,12},{12,8},{1,5},{5,1},{9,13},{13,9},{2,6},{6,2},{1... | collective-permute-start | bytes 196616 | tf_op jit(solution)/shard_map/ppermute | solution.py:26
  39.1 5.5 %collective-permute-start.16 = (bf16[4,32,256]{2,1,0:T(8,128)(2,1)S(1)}, bf16[4,32,256]{2,1,0:T(8,128)(2,1)S(1)}, u32[]{:S(2)}, u32[]{:S(2)}) collective-permute-start(bf16[4,32,256]{2,1,0:T(8,128)(2,1)S(1)} %reduce-precision_convert_fusion.2), channel_id=1, source_target_pairs={{0,4},{4,0},{8,12},{12,8},{1,5},{5,1},{9,13},{13,9},{2,6},{6,2},{1... | collective-permute-start | bytes 196616 | tf_op jit(solution)/shard_map/ppermute | solution.py:26
  39.7 10.4 %collective-permute-start.18 = (bf16[5,32,256]{2,1,0:T(8,128)(2,1)S(1)}, bf16[5,32,256]{2,1,0:T(8,128)(2,1)S(1)}, u32[]{:S(2)}, u32[]{:S(2)}) collective-permute-start(bf16[5,32,256]{2,1,0:T(8,128)(2,1)S(1)} %reduce-precision_convert_fusion), channel_id=1, source_target_pairs={{0,4},{4,0},{8,12},{12,8},{1,5},{5,1},{9,13},{13,9},{2,6},{6,2},{1... | collective-permute-start | bytes 245768 | tf_op jit(solution)/shard_map/ppermute | solution.py:26
  41.9 7.7 %collective-permute-start.11 = (bf16[4,32,256]{2,1,0:T(8,128)(2,1)S(1)}, bf16[4,32,256]{2,1,0:T(8,128)(2,1)S(1)}, u32[]{:S(2)}, u32[]{:S(2)}) collective-permute-start(bf16[4,32,256]{2,1,0:T(8,128)(2,1)S(1)} %fusion.16), channel_id=1, source_target_pairs={{0,8},{4,12},{8,0},{12,4},{1,9},{5,13},{9,1},{13,5},{2,10},{6,14},... | collective-permute-start | bytes 196616 | tf_op jit(solution)/shard_map/ppermute | solution.py:26
  44.6 8.4 %collective-permute-start.24 = (bf16[4,32,256]{2,1,0:T(8,128)(2,1)S(1)}, bf16[4,32,256]{2,1,0:T(8,128)(2,1)S(1)}, u32[]{:S(2)}, u32[]{:S(2)}) collective-permute-start(bf16[4,32,256]{2,1,0:T(8,128)(2,1)S(1)} %fusion.17), channel_id=1, source_target_pairs={{0,8},{4,12},{8,0},{12,4},{1,9},{5,13},{9,1},{13,5},{2,10},{6,14},... | collective-permute-start | bytes 196616 | tf_op jit(solution)/shard_map/ppermute | solution.py:26
  46.9 6.2 %collective-permute-start.13 = (bf16[208,256]{1,0:T(8,128)(2,1)S(1)}, bf16[208,256]{1,0:T(8,128)(2,1)S(1)}, u32[]{:S(2)}, u32[]{:S(2)}) collective-permute-start(bf16[208,256]{1,0:T(8,128)(2,1)S(1)} %pad_maximum_fusion.5), channel_id=1, source_target_pairs={{0,4},{4,0},{8,12},{12,8},{1,5},{5,1},{9,13},{13,9},{2,6},{6,2},{1... | collective-permute-start | bytes 319496 | tf_op jit(solution)/shard_map/ppermute | solution.py:26
  49.7 12.0 %collective-permute-start.21 = (bf16[4,32,256]{2,1,0:T(8,128)(2,1)S(1)}, bf16[4,32,256]{2,1,0:T(8,128)(2,1)S(1)}, u32[]{:S(2)}, u32[]{:S(2)}) collective-permute-start(bf16[4,32,256]{2,1,0:T(8,128)(2,1)S(1)} %add_convert_fusion.2), channel_id=1, source_target_pairs={{0,4},{4,0},{8,12},{12,8},{1,5},{5,1},{9,13},{13,9},{2,6},{6,2},{1... | collective-permute-start | bytes 196616 | tf_op jit(solution)/shard_map/ppermute | solution.py:26
  50.1 7.8 %collective-permute-start.19 = (bf16[5,32,256]{2,1,0:T(8,128)(2,1)S(1)}, bf16[5,32,256]{2,1,0:T(8,128)(2,1)S(1)}, u32[]{:S(2)}, u32[]{:S(2)}) collective-permute-start(bf16[5,32,256]{2,1,0:T(8,128)(2,1)S(1)} %fusion.18), channel_id=1, source_target_pairs={{0,8},{4,12},{8,0},{12,4},{1,9},{5,13},{9,1},{13,5},{2,10},{6,14},... | collective-permute-start | bytes 245768 | tf_op jit(solution)/shard_map/ppermute | solution.py:26
  53.1 6.2 %collective-permute-start.26 = (bf16[4,32,256]{2,1,0:T(8,128)(2,1)S(1)}, bf16[4,32,256]{2,1,0:T(8,128)(2,1)S(1)}, u32[]{:S(2)}, u32[]{:S(2)}) collective-permute-start(bf16[4,32,256]{2,1,0:T(8,128)(2,1)S(1)} %add_convert_fusion.1), channel_id=1, source_target_pairs={{0,4},{4,0},{8,12},{12,8},{1,5},{5,1},{9,13},{13,9},{2,6},{6,2},{1... | collective-permute-start | bytes 196616 | tf_op jit(solution)/shard_map/ppermute | solution.py:26
  53.3 6.1 %collective-permute-start.15 = (bf16[208,256]{1,0:T(8,128)(2,1)S(1)}, bf16[208,256]{1,0:T(8,128)(2,1)S(1)}, u32[]{:S(2)}, u32[]{:S(2)}) collective-permute-start(bf16[208,256]{1,0:T(8,128)(2,1)S(1)} %pad_maximum_fusion.6), channel_id=1, source_target_pairs={{0,8},{4,12},{8,0},{12,4},{1,9},{5,13},{9,1},{13,5},{2,10},{6,14},... | collective-permute-start | bytes 319496 | tf_op jit(solution)/shard_map/ppermute | solution.py:26
  58.0 4.9 %collective-permute-start.20 = (bf16[5,32,256]{2,1,0:T(8,128)(2,1)S(1)}, bf16[5,32,256]{2,1,0:T(8,128)(2,1)S(1)}, u32[]{:S(2)}, u32[]{:S(2)}) collective-permute-start(bf16[5,32,256]{2,1,0:T(8,128)(2,1)S(1)} %add_convert_fusion), channel_id=1, source_target_pairs={{0,4},{4,0},{8,12},{12,8},{1,5},{5,1},{9,13},{13,9},{2,6},{6,2},{1... | collective-permute-start | bytes 245768 | tf_op jit(solution)/shard_map/ppermute | solution.py:26
  59.3 3.6 %collective-permute-start.27 = (bf16[4,64,256]{2,1,0:T(8,128)(2,1)S(1)}, bf16[4,64,256]{2,1,0:T(8,128)(2,1)S(1)}, u32[]{:S(2)}, u32[]{:S(2)}) collective-permute-start(bf16[4,64,256]{2,1,0:T(8,128)(2,1)S(1)} %pad_maximum_fusion.4), channel_id=1, source_target_pairs={{0,2},{2,0},{1,3},{3,1},{4,6},{6,4},{5,7},{7,5},{8,10},{10,8},{9,1... | collective-permute-start | bytes 393224 | tf_op jit(solution)/shard_map/ppermute | solution.py:26
  60.2 4.8 %collective-permute-start.23 = (bf16[5,32,256]{2,1,0:T(8,128)(2,1)S(1)}, bf16[5,32,256]{2,1,0:T(8,128)(2,1)S(1)}, u32[]{:S(2)}, u32[]{:S(2)}) collective-permute-start(bf16[5,32,256]{2,1,0:T(8,128)(2,1)S(1)} %fusion.6), channel_id=1, source_target_pairs={{0,4},{4,0},{8,12},{12,8},{1,5},{5,1},{9,13},{13,9},{2,6},{6,2},{1... | collective-permute-start | bytes 245768 | tf_op jit(solution)/shard_map/ppermute | solution.py:26
  62.9 3.6 %collective-permute-start.22 = (bf16[9,64,256]{2,1,0:T(8,128)(2,1)S(1)}, bf16[9,64,256]{2,1,0:T(8,128)(2,1)S(1)}, u32[]{:S(2)}, u32[]{:S(2)}) collective-permute-start(bf16[9,64,256]{2,1,0:T(8,128)(2,1)S(1)} %maximum_maximum_fusion.1), channel_id=1, source_target_pairs={{0,2},{2,0},{1,3},{3,1},{4,6},{6,4},{5,7},{7,5},{8,10},{10,8},{9,1... | collective-permute-start | bytes 884744 | tf_op jit(solution)/shard_map/ppermute | solution.py:26
  65.0 1.5 %collective-permute-start.25 = (bf16[5,64,256]{2,1,0:T(8,128)(2,1)S(1)}, bf16[5,64,256]{2,1,0:T(8,128)(2,1)S(1)}, u32[]{:S(2)}, u32[]{:S(2)}) collective-permute-start(bf16[5,64,256]{2,1,0:T(8,128)(2,1)S(1)} %pad_maximum_fusion.3), channel_id=1, source_target_pairs={{0,2},{2,0},{1,3},{3,1},{4,6},{6,4},{5,7},{7,5},{8,10},{10,8},{9,1... | collective-permute-start | bytes 491528 | tf_op jit(solution)/shard_map/ppermute | solution.py:26

commit v6 on v5

--- a/solution.py
+++ b/solution.py
@@ -10,7 +10,7 @@
 
 BLK = 8
 SLOT = 16
-CHUNKS = (5, 4, 5, 4)
+CHUNKS = (5, 4, 4, 5)
 F32 = jnp.float32
 BF16 = jnp.bfloat16
 VMEM = pl.BlockSpec(memory_space=pltpu.VMEM)

time: 69.8 us -> 70 us (level)
  starting transfers between devices: 29.1 us -> 30.2 us
  waiting for transfers between devices: 19.3 us -> 18.4 us
    ppermute x26, starting transfers between devices: 24 us -> 25 us  [swap(): return lax.ppermute(block, axis, [(i, i ^ distance) for i in range(count)])]
    ppermute x26, waiting for transfers between devices: 18.2 us -> 17.3 us  [swap(): return lax.ppermute(block, axis, [(i, i ^ distance) for i in range(count)])]
  transfers between devices with their start and end apart: 28 -> 28, of which waited for: 12 -> 13; matrix products, arithmetic and copies ran while one was open for 4% -> 4% of each run, Pallas kernels for 8% -> 8%
where the time goes in v6:
time: 70 us; the launch traced here: 69.8 us
  starting transfers between devices  30.2 us (43%)
  waiting for transfers between devices  18.4 us (26%)
  Pallas kernels  12.2 us (17%)
  other arithmetic  3.78 us (5%)
  between operations  2.88 us (4%)
  local copies, waits for them, and re-layouts  2.36 us (3%)
    ppermute x26, starting transfers between devices, swap(): return lax.ppermute(block, axis, [(i, i ^ distance) for i in range(count)])  25 us
    ppermute x26, waiting for transfers between devices, swap(): return lax.ppermute(block, axis, [(i, i ^ distance) for i in range(count)])  17.3 us
    pallas_call x1, Pallas kernels, local(): pl.pallas_call(functools.partial(last_layer, geom, scale), out_shape=kept...  6.79 us
    ppermute x2, starting transfers between devices, shift(): return lax.ppermute(block, axis, pairs)  5.15 us
    pallas_call x1, Pallas kernels, local(): pl.pallas_call(functools.partial(first_layer, geom), out_shape=(shape((ce...  3.11 us
    pallas_call x1, Pallas kernels, local(): pl.pallas_call(prepare, out_shape=(shape((height, 8, width), BF16),) + (s...  2.25 us
    unnamed x4, local copies, waits for them, and re-layouts  1.76 us
    convert_element_type x1, other arithmetic, local(): jnp.concatenate(taps_of, axis=0).astype(F32)  1.67 us
  transfers between devices with their start and end apart: 28, of which 13 were waited for; matrix products, arithmetic and copies ran while one was open for 4% of the time, Pallas kernels for 8%

profile of v6, /device:TPU:0, one launch (start us, length us, event | category | flops | bytes accessed | tf_op | source)
XLA Modules:
  0.0 69.8 jit_solution(5448468549139370451)
XLA Ops:
  0.6 1.2 %copy.11 = bf16[128,8,128]{0,2,1:T(8,128)(2,1)S(1)} copy(bf16[128,8,128]{2,1,0:T(8,128)(2,1)} %param.6) | data formatting | bytes 524288 | tf_op args[0]
  1.8 3.0 %collective-permute-start = (bf16[6,128,128]{2,1,0:T(8,128)(2,1)S(1)}, bf16[6,128,128]{2,1,0:T(8,128)(2,1)S(1)}, u32[]{:S(2)}, u32[]{:S(2)}) collective-permute-start(bf16[6,128,128]{2,1,0:T(8,128)(2,1)S(1)} %pad_maximum_fusion.2), channel_id=1, source_target_pairs={{0,1},{1,0},{2,3},{3,2},{4,5},{5,4},{6,7},{7,6},{8,9},{9,8},{10,11... | collective-permute-start | bytes 589832 | tf_op jit(solution)/shard_map/ppermute | solution.py:26
  4.8 0.1 pad_add_fusion.scal
  4.9 2.3 %prepare.1 = (bf16[8,8,128]{2,1,0:T(8,128)(2,1)S(1)}, bf16[9,256,128]{2,1,0:T(8,128)(2,1)S(1)}, bf16[9,256,128]{2,1,0:T(8,128)(2,1)S(1)}, bf16[9,128,128]{2,1,0:T(8,128)(2,1)S(1)}, bf16[9,128,128]{2,1,0:T(8,128)(2,1)S(1)}) custom-call(s32[4]{0:T(128)S(1)} %pad_add_fusion.scal, s32[8,128]{1,0:T(8,128)} %labels_in.1, f32[2,8,128]{2,1,0:T(8,128)} %flow_in.1, ...), custom_call_target="tpu_custom_call" | custom-call | tf_op jit(solution)/shard_map/prepare/pallas_call | solution.py:515
  7.2 0.1 collective-permute-start.5
  7.3 2.9 %collective-permute-done = bf16[6,128,128]{2,1,0:T(8,128)(2,1)S(1)} collective-permute-done((bf16[6,128,128]{2,1,0:T(8,128)(2,1)S(1)}, bf16[6,128,128]{2,1,0:T(8,128)(2,1)S(1)}, u32[]{:S(2)}, u32[]{:S(2)}) %collective-permute-start) | collective-permute-done | bytes 196640 | tf_op jit(solution)/shard_map/ppermute | solution.py:26
  10.2 0.7 %fusion.3 = (bf16[392,256]{1,0:T(8,128)(2,1)}, bf16[392,256]{1,0:T(8,128)(2,1)S(1)}) fusion(bf16[8,128]{1,0:T(8,128)(2,1)S(1)} %get-tuple-element.116, bf16[384,256]{1,0:T(8,128)(2,1)S(1)} %bitcast.53, bf16[8,128]{1,0:T(8,128)(2,1)S(1)} %get-tuple-element.115, bf16[384,256]{1,0:T(8,128)(2,1)S(1)} %bitcast.52), kind=kLoop, calls=%fused_computation.13 | loop fusion | flops 1103872 | bytes 798720 | tf_op jit(solution)/shard_map/concatenate | solution.py:556
  10.9 3.9 %collective-permute-start.1 = (bf16[392,256]{1,0:T(8,128)(2,1)}, bf16[392,256]{1,0:T(8,128)(2,1)S(1)}, u32[]{:S(2)}, u32[]{:S(2)}) collective-permute-start(bf16[392,256]{1,0:T(8,128)(2,1)} %get-tuple-element.42), channel_id=1, source_target_pairs={{0,4},{4,8},{8,12},{1,5},{5,9},{9,13},{2,6},{6,10},{10,14},{3,7},{... | collective-permute-start | bytes 602120 | tf_op jit(solution)/shard_map/ppermute | solution.py:32
  14.8 1.3 %collective-permute-start.2 = (bf16[392,256]{1,0:T(8,128)(2,1)S(1)}, bf16[392,256]{1,0:T(8,128)(2,1)S(1)}, u32[]{:S(2)}, u32[]{:S(2)}) collective-permute-start(bf16[392,256]{1,0:T(8,128)(2,1)S(1)} %get-tuple-element.43), channel_id=1, source_target_pairs={{4,0},{8,4},{12,8},{5,1},{9,5},{13,9},{6,2},{10,6},{14,10},{7,3},{... | collective-permute-start | bytes 602120 | tf_op jit(solution)/shard_map/ppermute | solution.py:32
  16.1 2.2 %collective-permute-start.3 = (bf16[2,128,128]{2,1,0:T(8,128)(2,1)S(1)}, bf16[2,128,128]{2,1,0:T(8,128)(2,1)S(1)}, u32[]{:S(2)}, u32[]{:S(2)}) collective-permute-start(bf16[2,128,128]{2,1,0:T(8,128)(2,1)S(1)} %slice.182), channel_id=1, source_target_pairs={{0,1},{1,0},{2,3},{3,2},{4,5},{5,4},{6,7},{7,6},{8,9},{9,8},{10,11... | collective-permute-start | bytes 196616 | tf_op jit(solution)/shard_map/ppermute | solution.py:26
  18.3 0.1 collective-permute-start.7
  18.4 0.0 collective-permute-done.5.refs_1_
  18.4 0.0 collective-permute-start.6
  18.4 2.9 %collective-permute-done.3 = bf16[2,128,128]{2,1,0:T(8,128)(2,1)S(1)} collective-permute-done((bf16[2,128,128]{2,1,0:T(8,128)(2,1)S(1)}, bf16[2,128,128]{2,1,0:T(8,128)(2,1)S(1)}, u32[]{:S(2)}, u32[]{:S(2)}) %collective-permute-start.3) | collective-permute-done | bytes 65568 | tf_op jit(solution)/shard_map/ppermute | solution.py:26
  21.3 0.0 collective-permute-done.1.top.above
  21.3 1.1 %collective-permute-done.2.bottom.below = bf16[392,256]{1,0:T(8,128)(2,1)S(1)} collective-permute-done((bf16[392,256]{1,0:T(8,128)(2,1)S(1)}, bf16[392,256]{1,0:T(8,128)(2,1)S(1)}, u32[]{:S(2)}, u32[]{:S(2)}) %collective-permute-start.2) | collective-permute-done | bytes 200736 | tf_op jit(solution)/shard_map/ppermute | solution.py:32
  22.4 0.0 copy-start
  22.6 0.1 fusion.9
  22.7 0.1 collective-permute-start.4
  22.8 1.4 %collective-permute-done.4.tiles.tile = bf16[304,256]{1,0:T(8,128)(2,1)S(1)} collective-permute-done((bf16[304,256]{1,0:T(8,128)(2,1)S(1)}, bf16[304,256]{1,0:T(8,128)(2,1)S(1)}, u32[]{:S(2)}, u32[]{:S(2)}) %collective-permute-start.4) | collective-permute-done | bytes 155680 | tf_op jit(solution)/shard_map/ppermute | solution.py:26
  24.2 0.0 collective-permute-done.6.refs_2_
  24.2 3.1 %first_layer.1 = (bf16[2032,256]{1,0:T(8,128)(2,1)S(1)}, bf16[1744,256]{1,0:T(8,128)(2,1)S(1)}, f32[1024,128]{1,0:T(8,128)S(1)}) custom-call(s32[4]{0:T(128)S(1)} %pad_add_fusion.scal, bf16[8,128,256]{2,1,0:T(8,128)(2,1)S(1)} %pad_maximum_fusion.mid, bf16[392,256]{1,0:T(8,128)(2,1)S(1)} %collective-permute-done.1.top.above, ...), custom_call_target="tpu_custom_call" | custom-call | tf_op jit(solution)/shard_map/first_layer/pallas_call | solution.py:590
  27.3 0.0 collective-permute-done.7.refs_1_
  27.3 0.2 collective-permute-start.8
  27.5 1.4 %collective-permute-done.8.refs_2_ = bf16[9,128,128]{2,1,0:T(8,128)(2,1)S(1)} collective-permute-done((bf16[9,128,128]{2,1,0:T(8,128)(2,1)S(1)}, bf16[9,128,128]{2,1,0:T(8,128)(2,1)S(1)}, u32[]{:S(2)}, u32[]{:S(2)}) %collective-permute-start.8) | collective-permute-done | bytes 294944 | tf_op jit(solution)/shard_map/ppermute | solution.py:26
  29.0 6.8 %last_layer.1 = (f32[320,256]{1,0:T(8,128)S(1)}, f32[256,256]{1,0:T(8,128)S(1)}, f32[256,256]{1,0:T(8,128)S(1)}, f32[320,256]{1,0:T(8,128)S(1)}, f32[336,256]{1,...) custom-call(s32[4]{0:T(128)S(1)} %pad_add_fusion.scal, ...), custom_call_target="tpu_custom_call" | custom-call | tf_op jit(solution)/shard_map/last_layer/pallas_call | solution.py:614
  35.7 0.2 collective-permute-start.14
  36.0 0.4 collective-permute-start.17
  36.3 0.1 collective-permute-start.9
  36.5 0.4 collective-permute-start.12
  36.8 0.5 collective-permute-done.14
  37.4 1.6 %collective-permute-start.16 = (bf16[4,32,256]{2,1,0:T(8,128)(2,1)S(1)}, bf16[4,32,256]{2,1,0:T(8,128)(2,1)S(1)}, u32[]{:S(2)}, u32[]{:S(2)}) collective-permute-start(bf16[4,32,256]{2,1,0:T(8,128)(2,1)S(1)} %reduce-precision_convert_fusion.3), channel_id=1, source_target_pairs={{0,4},{4,0},{8,12},{12,8},{1,5},{5,1},{9,13},{13,9},{2,6},{6,2},{1... | collective-permute-start | bytes 196616 | tf_op jit(solution)/shard_map/ppermute | solution.py:26
  39.0 0.0 collective-permute-done.17
  39.1 0.5 collective-permute-start.18
  39.7 1.6 %collective-permute-start.10 = (bf16[5,32,256]{2,1,0:T(8,128)(2,1)S(1)}, bf16[5,32,256]{2,1,0:T(8,128)(2,1)S(1)}, u32[]{:S(2)}, u32[]{:S(2)}) collective-permute-start(bf16[5,32,256]{2,1,0:T(8,128)(2,1)S(1)} %reduce-precision_convert_fusion.1), channel_id=1, source_target_pairs={{0,4},{4,0},{8,12},{12,8},{1,5},{5,1},{9,13},{13,9},{2,6},{6,2},{1... | collective-permute-start | bytes 245768 | tf_op jit(solution)/shard_map/ppermute | solution.py:26
  41.3 0.5 collective-permute-done.16
  41.9 2.7 %collective-permute-start.24 = (bf16[4,32,256]{2,1,0:T(8,128)(2,1)S(1)}, bf16[4,32,256]{2,1,0:T(8,128)(2,1)S(1)}, u32[]{:S(2)}, u32[]{:S(2)}) collective-permute-start(bf16[4,32,256]{2,1,0:T(8,128)(2,1)S(1)} %fusion.16), channel_id=1, source_target_pairs={{0,8},{4,12},{8,0},{12,4},{1,9},{5,13},{9,1},{13,5},{2,10},{6,14},... | collective-permute-start | bytes 196616 | tf_op jit(solution)/shard_map/ppermute | solution.py:26
  44.6 2.2 %collective-permute-start.19 = (bf16[4,32,256]{2,1,0:T(8,128)(2,1)S(1)}, bf16[4,32,256]{2,1,0:T(8,128)(2,1)S(1)}, u32[]{:S(2)}, u32[]{:S(2)}) collective-permute-start(bf16[4,32,256]{2,1,0:T(8,128)(2,1)S(1)} %fusion.17), channel_id=1, source_target_pairs={{0,8},{4,12},{8,0},{12,4},{1,9},{5,13},{9,1},{13,5},{2,10},{6,14},... | collective-permute-start | bytes 196616 | tf_op jit(solution)/shard_map/ppermute | solution.py:26
  46.8 0.0 collective-permute-done.12
  46.9 1.3 %collective-permute-start.13 = (bf16[208,256]{1,0:T(8,128)(2,1)S(1)}, bf16[208,256]{1,0:T(8,128)(2,1)S(1)}, u32[]{:S(2)}, u32[]{:S(2)}) collective-permute-start(bf16[208,256]{1,0:T(8,128)(2,1)S(1)} %pad_maximum_fusion.5), channel_id=1, source_target_pairs={{0,4},{4,0},{8,12},{12,8},{1,5},{5,1},{9,13},{13,9},{2,6},{6,2},{1... | collective-permute-start | bytes 319496 | tf_op jit(solution)/shard_map/ppermute | solution.py:26
  48.2 1.4 %collective-permute-done.24 = bf16[4,32,256]{2,1,0:T(8,128)(2,1)S(1)} collective-permute-done((bf16[4,32,256]{2,1,0:T(8,128)(2,1)S(1)}, bf16[4,32,256]{2,1,0:T(8,128)(2,1)S(1)}, u32[]{:S(2)}, u32[]{:S(2)}) %collective-permute-start.24) | collective-permute-done | bytes 65568 | tf_op jit(solution)/shard_map/ppermute | solution.py:26
  49.7 0.4 collective-permute-start.26
  50.1 0.0 collective-permute-done.10
  50.1 2.9 %collective-permute-start.11 = (bf16[5,32,256]{2,1,0:T(8,128)(2,1)S(1)}, bf16[5,32,256]{2,1,0:T(8,128)(2,1)S(1)}, u32[]{:S(2)}, u32[]{:S(2)}) collective-permute-start(bf16[5,32,256]{2,1,0:T(8,128)(2,1)S(1)} %fusion.18), channel_id=1, source_target_pairs={{0,8},{4,12},{8,0},{12,4},{1,9},{5,13},{9,1},{13,5},{2,10},{6,14},... | collective-permute-start | bytes 245768 | tf_op jit(solution)/shard_map/ppermute | solution.py:26
  53.0 0.0 collective-permute-done.19
  53.1 0.1 collective-permute-start.20
  53.3 1.8 %collective-permute-start.15 = (bf16[208,256]{1,0:T(8,128)(2,1)S(1)}, bf16[208,256]{1,0:T(8,128)(2,1)S(1)}, u32[]{:S(2)}, u32[]{:S(2)}) collective-permute-start(bf16[208,256]{1,0:T(8,128)(2,1)S(1)} %pad_maximum_fusion.6), channel_id=1, source_target_pairs={{0,8},{4,12},{8,0},{12,4},{1,9},{5,13},{9,1},{13,5},{2,10},{6,14},... | collective-permute-start | bytes 319496 | tf_op jit(solution)/shard_map/ppermute | solution.py:26
  55.1 1.0 %collective-permute-done.26 = bf16[4,32,256]{2,1,0:T(8,128)(2,1)S(1)} collective-permute-done((bf16[4,32,256]{2,1,0:T(8,128)(2,1)S(1)}, bf16[4,32,256]{2,1,0:T(8,128)(2,1)S(1)}, u32[]{:S(2)}, u32[]{:S(2)}) %collective-permute-start.26) | collective-permute-done | bytes 65568 | tf_op jit(solution)/shard_map/ppermute | solution.py:26
  56.1 0.1 collective-permute-start.27
  56.2 1.8 %collective-permute-done.11 = bf16[5,32,256]{2,1,0:T(8,128)(2,1)S(1)} collective-permute-done((bf16[5,32,256]{2,1,0:T(8,128)(2,1)S(1)}, bf16[5,32,256]{2,1,0:T(8,128)(2,1)S(1)}, u32[]{:S(2)}, u32[]{:S(2)}) %collective-permute-start.11) | collective-permute-done | bytes 81952 | tf_op jit(solution)/shard_map/ppermute | solution.py:26
  58.0 0.5 collective-permute-start.21
  58.5 0.6 collective-permute-done.20
  59.1 0.1 fusion.6
  59.2 0.5 slice.175
  59.7 0.6 copy.12
  60.3 2.4 %collective-permute-start.23 = (bf16[5,32,256]{2,1,0:T(8,128)(2,1)S(1)}, bf16[5,32,256]{2,1,0:T(8,128)(2,1)S(1)}, u32[]{:S(2)}, u32[]{:S(2)}) collective-permute-start(bf16[5,32,256]{2,1,0:T(8,128)(2,1)S(1)} %fusion.6), channel_id=1, source_target_pairs={{0,4},{4,0},{8,12},{12,8},{1,5},{5,1},{9,13},{13,9},{2,6},{6,2},{1... | collective-permute-start | bytes 245768 | tf_op jit(solution)/shard_map/ppermute | solution.py:26
  63.5 0.1 collective-permute-start.22
  63.6 1.6 %collective-permute-done.23 = bf16[5,32,256]{2,1,0:T(8,128)(2,1)S(1)} collective-permute-done((bf16[5,32,256]{2,1,0:T(8,128)(2,1)S(1)}, bf16[5,32,256]{2,1,0:T(8,128)(2,1)S(1)}, u32[]{:S(2)}, u32[]{:S(2)}) %collective-permute-start.23) | collective-permute-done | bytes 81952 | tf_op jit(solution)/shard_map/ppermute | solution.py:26
  65.2 0.1 collective-permute-start.25
  65.3 1.3 %collective-permute-done.25 = bf16[5,64,256]{2,1,0:T(8,128)(2,1)S(1)} collective-permute-done((bf16[5,64,256]{2,1,0:T(8,128)(2,1)S(1)}, bf16[5,64,256]{2,1,0:T(8,128)(2,1)S(1)}, u32[]{:S(2)}, u32[]{:S(2)}) %collective-permute-start.25) | collective-permute-done | bytes 163872 | tf_op jit(solution)/shard_map/ppermute | solution.py:26
  66.7 0.1 broadcast_select_fusion.5
  66.7 0.1 broadcast_select_fusion.1
  66.9 0.1 maximum_maximum_fusion
  67.0 1.7 %convert.5 = f32[2,9,128,256]{3,2,1,0:T(8,128)} convert(bf16[2,9,128,256]{3,2,1,0:T(8,128)(2,1)S(1)} %bitcast.45) | non-fusion elementwise | flops 589824 | bytes 3538944 | tf_op jit(solution)/shard_map/convert_element_type | solution.py:652
  (60 shorter events, 1.0 us)
Async XLA Ops:
  1.8 8.3 %collective-permute-start = (bf16[6,128,128]{2,1,0:T(8,128)(2,1)S(1)}, bf16[6,128,128]{2,1,0:T(8,128)(2,1)S(1)}, u32[]{:S(2)}, u32[]{:S(2)}) collective-permute-start(bf16[6,128,128]{2,1,0:T(8,128)(2,1)S(1)} %pad_maximum_fusion.2), channel_id=1, source_target_pairs={{0,1},{1,0},{2,3},{3,2},{4,5},{5,4},{6,7},{7,6},{8,9},{9,8},{10,11... | collective-permute-start | bytes 589832 | tf_op jit(solution)/shard_map/ppermute | solution.py:26
  7.2 11.2 %collective-permute-start.5 = (bf16[9,128,128]{2,1,0:T(8,128)(2,1)S(1)}, bf16[9,128,128]{2,1,0:T(8,128)(2,1)S(1)}, u32[]{:S(2)}, u32[]{:S(2)}) collective-permute-start(bf16[9,128,128]{2,1,0:T(8,128)(2,1)S(1)} %get-tuple-element.49), channel_id=1, source_target_pairs={{0,1},{1,0},{2,3},{3,2},{4,5},{5,4},{6,7},{7,6},{8,9},{9,8},{10,11... | collective-permute-start | bytes 884744 | tf_op jit(solution)/shard_map/ppermute | solution.py:26
  10.9 10.4 %collective-permute-start.1 = (bf16[392,256]{1,0:T(8,128)(2,1)}, bf16[392,256]{1,0:T(8,128)(2,1)S(1)}, u32[]{:S(2)}, u32[]{:S(2)}) collective-permute-start(bf16[392,256]{1,0:T(8,128)(2,1)} %get-tuple-element.42), channel_id=1, source_target_pairs={{0,4},{4,8},{8,12},{1,5},{5,9},{9,13},{2,6},{6,10},{10,14},{3,7},{... | collective-permute-start | bytes 602120 | tf_op jit(solution)/shard_map/ppermute | solution.py:32
  14.8 7.6 %collective-permute-start.2 = (bf16[392,256]{1,0:T(8,128)(2,1)S(1)}, bf16[392,256]{1,0:T(8,128)(2,1)S(1)}, u32[]{:S(2)}, u32[]{:S(2)}) collective-permute-start(bf16[392,256]{1,0:T(8,128)(2,1)S(1)} %get-tuple-element.43), channel_id=1, source_target_pairs={{4,0},{8,4},{12,8},{5,1},{9,5},{13,9},{6,2},{10,6},{14,10},{7,3},{... | collective-permute-start | bytes 602120 | tf_op jit(solution)/shard_map/ppermute | solution.py:32
  16.1 5.2 %collective-permute-start.3 = (bf16[2,128,128]{2,1,0:T(8,128)(2,1)S(1)}, bf16[2,128,128]{2,1,0:T(8,128)(2,1)S(1)}, u32[]{:S(2)}, u32[]{:S(2)}) collective-permute-start(bf16[2,128,128]{2,1,0:T(8,128)(2,1)S(1)} %slice.182), channel_id=1, source_target_pairs={{0,1},{1,0},{2,3},{3,2},{4,5},{5,4},{6,7},{7,6},{8,9},{9,8},{10,11... | collective-permute-start | bytes 196616 | tf_op jit(solution)/shard_map/ppermute | solution.py:26
  18.3 9.0 %collective-permute-start.7 = (bf16[9,128,128]{2,1,0:T(8,128)(2,1)S(1)}, bf16[9,128,128]{2,1,0:T(8,128)(2,1)S(1)}, u32[]{:S(2)}, u32[]{:S(2)}) collective-permute-start(bf16[9,128,128]{2,1,0:T(8,128)(2,1)S(1)} %get-tuple-element.55), channel_id=1, source_target_pairs={{0,1},{1,0},{2,3},{3,2},{4,5},{5,4},{6,7},{7,6},{8,9},{9,8},{10,11... | collective-permute-start | bytes 884744 | tf_op jit(solution)/shard_map/ppermute | solution.py:26
  18.4 5.8 %collective-permute-start.6 = (bf16[9,128,128]{2,1,0:T(8,128)(2,1)S(1)}, bf16[9,128,128]{2,1,0:T(8,128)(2,1)S(1)}, u32[]{:S(2)}, u32[]{:S(2)}) collective-permute-start(bf16[9,128,128]{2,1,0:T(8,128)(2,1)S(1)} %collective-permute-done.5.refs_1_), channel_id=1, source_target_pairs={{0,2},{2,0},{1,3},{3,1},{4,6},{6,4},{5,7},{7,5},{8,10},{10,8},{9,1... | collective-permute-start | bytes 884744 | tf_op jit(solution)/shard_map/ppermute | solution.py:26
  22.4 6.5 %copy-start = (bf16[8,3,256]{2,0,1:T(8,128)(2,1)S(1)}, bf16[8,3,256]{2,0,1:T(8,128)(2,1)}, u32[]{:S(2)}) copy-start(bf16[8,3,256]{2,0,1:T(8,128)(2,1)} %param.8) | copy-start | bytes 36868
  22.7 1.4 %collective-permute-start.4 = (bf16[304,256]{1,0:T(8,128)(2,1)S(1)}, bf16[304,256]{1,0:T(8,128)(2,1)S(1)}, u32[]{:S(2)}, u32[]{:S(2)}) collective-permute-start(bf16[304,256]{1,0:T(8,128)(2,1)S(1)} %fusion.8), channel_id=1, source_target_pairs={{0,2},{2,0},{1,3},{3,1},{4,6},{6,4},{5,7},{7,5},{8,10},{10,8},{9,1... | collective-permute-start | bytes 466952 | tf_op jit(solution)/shard_map/ppermute | solution.py:26
  27.3 1.6 %collective-permute-start.8 = (bf16[9,128,128]{2,1,0:T(8,128)(2,1)S(1)}, bf16[9,128,128]{2,1,0:T(8,128)(2,1)S(1)}, u32[]{:S(2)}, u32[]{:S(2)}) collective-permute-start(bf16[9,128,128]{2,1,0:T(8,128)(2,1)S(1)} %collective-permute-done.7.refs_1_), channel_id=1, source_target_pairs={{0,2},{2,0},{1,3},{3,1},{4,6},{6,4},{5,7},{7,5},{8,10},{10,8},{9,1... | collective-permute-start | bytes 884744 | tf_op jit(solution)/shard_map/ppermute | solution.py:26
  35.7 1.6 %collective-permute-start.14 = (f32[256,256]{1,0:T(8,128)S(1)}, f32[256,256]{1,0:T(8,128)S(1)}, u32[]{:S(2)}, u32[]{:S(2)}) collective-permute-start(f32[256,256]{1,0:T(8,128)S(1)} %get-tuple-element.63), channel_id=1, source_target_pairs={{0,2},{2,0},{1,3},{3,1},{4,6},{6,4},{5,7},{7,5},{8,10},{10,8},{9,1... | collective-permute-start | bytes 786440 | tf_op jit(solution)/shard_map/ppermute | solution.py:26
  36.0 3.1 %collective-permute-start.17 = (f32[256,256]{1,0:T(8,128)S(1)}, f32[256,256]{1,0:T(8,128)S(1)}, u32[]{:S(2)}, u32[]{:S(2)}) collective-permute-start(f32[256,256]{1,0:T(8,128)S(1)} %get-tuple-element.66), channel_id=1, source_target_pairs={{0,2},{2,0},{1,3},{3,1},{4,6},{6,4},{5,7},{7,5},{8,10},{10,8},{9,1... | collective-permute-start | bytes 786440 | tf_op jit(solution)/shard_map/ppermute | solution.py:26
  36.3 3.3 %collective-permute-start.9 = (f32[320,256]{1,0:T(8,128)S(1)}, f32[320,256]{1,0:T(8,128)S(1)}, u32[]{:S(2)}, u32[]{:S(2)}) collective-permute-start(f32[320,256]{1,0:T(8,128)S(1)} %get-tuple-element.58), channel_id=1, source_target_pairs={{0,2},{2,0},{1,3},{3,1},{4,6},{6,4},{5,7},{7,5},{8,10},{10,8},{9,1... | collective-permute-start | bytes 983048 | tf_op jit(solution)/shard_map/ppermute | solution.py:26
  36.5 10.4 %collective-permute-start.12 = (f32[336,256]{1,0:T(8,128)S(1)}, f32[336,256]{1,0:T(8,128)S(1)}, u32[]{:S(2)}, u32[]{:S(2)}) collective-permute-start(f32[336,256]{1,0:T(8,128)S(1)} %get-tuple-element.60), channel_id=1, source_target_pairs={{0,2},{2,0},{1,3},{3,1},{4,6},{6,4},{5,7},{7,5},{8,10},{10,8},{9,1... | collective-permute-start | bytes 1032200 | tf_op jit(solution)/shard_map/ppermute | solution.py:26
  37.4 4.5 %collective-permute-start.16 = (bf16[4,32,256]{2,1,0:T(8,128)(2,1)S(1)}, bf16[4,32,256]{2,1,0:T(8,128)(2,1)S(1)}, u32[]{:S(2)}, u32[]{:S(2)}) collective-permute-start(bf16[4,32,256]{2,1,0:T(8,128)(2,1)S(1)} %reduce-precision_convert_fusion.3), channel_id=1, source_target_pairs={{0,4},{4,0},{8,12},{12,8},{1,5},{5,1},{9,13},{13,9},{2,6},{6,2},{1... | collective-permute-start | bytes 196616 | tf_op jit(solution)/shard_map/ppermute | solution.py:26
  39.1 5.5 %collective-permute-start.18 = (bf16[4,32,256]{2,1,0:T(8,128)(2,1)S(1)}, bf16[4,32,256]{2,1,0:T(8,128)(2,1)S(1)}, u32[]{:S(2)}, u32[]{:S(2)}) collective-permute-start(bf16[4,32,256]{2,1,0:T(8,128)(2,1)S(1)} %reduce-precision_convert_fusion.2), channel_id=1, source_target_pairs={{0,4},{4,0},{8,12},{12,8},{1,5},{5,1},{9,13},{13,9},{2,6},{6,2},{1... | collective-permute-start | bytes 196616 | tf_op jit(solution)/shard_map/ppermute | solution.py:26
  39.7 10.4 %collective-permute-start.10 = (bf16[5,32,256]{2,1,0:T(8,128)(2,1)S(1)}, bf16[5,32,256]{2,1,0:T(8,128)(2,1)S(1)}, u32[]{:S(2)}, u32[]{:S(2)}) collective-permute-start(bf16[5,32,256]{2,1,0:T(8,128)(2,1)S(1)} %reduce-precision_convert_fusion.1), channel_id=1, source_target_pairs={{0,4},{4,0},{8,12},{12,8},{1,5},{5,1},{9,13},{13,9},{2,6},{6,2},{1... | collective-permute-start | bytes 245768 | tf_op jit(solution)/shard_map/ppermute | solution.py:26
  41.9 7.7 %collective-permute-start.24 = (bf16[4,32,256]{2,1,0:T(8,128)(2,1)S(1)}, bf16[4,32,256]{2,1,0:T(8,128)(2,1)S(1)}, u32[]{:S(2)}, u32[]{:S(2)}) collective-permute-start(bf16[4,32,256]{2,1,0:T(8,128)(2,1)S(1)} %fusion.16), channel_id=1, source_target_pairs={{0,8},{4,12},{8,0},{12,4},{1,9},{5,13},{9,1},{13,5},{2,10},{6,14},... | collective-permute-start | bytes 196616 | tf_op jit(solution)/shard_map/ppermute | solution.py:26
  44.6 8.4 %collective-permute-start.19 = (bf16[4,32,256]{2,1,0:T(8,128)(2,1)S(1)}, bf16[4,32,256]{2,1,0:T(8,128)(2,1)S(1)}, u32[]{:S(2)}, u32[]{:S(2)}) collective-permute-start(bf16[4,32,256]{2,1,0:T(8,128)(2,1)S(1)} %fusion.17), channel_id=1, source_target_pairs={{0,8},{4,12},{8,0},{12,4},{1,9},{5,13},{9,1},{13,5},{2,10},{6,14},... | collective-permute-start | bytes 196616 | tf_op jit(solution)/shard_map/ppermute | solution.py:26
  46.9 6.2 %collective-permute-start.13 = (bf16[208,256]{1,0:T(8,128)(2,1)S(1)}, bf16[208,256]{1,0:T(8,128)(2,1)S(1)}, u32[]{:S(2)}, u32[]{:S(2)}) collective-permute-start(bf16[208,256]{1,0:T(8,128)(2,1)S(1)} %pad_maximum_fusion.5), channel_id=1, source_target_pairs={{0,4},{4,0},{8,12},{12,8},{1,5},{5,1},{9,13},{13,9},{2,6},{6,2},{1... | collective-permute-start | bytes 319496 | tf_op jit(solution)/shard_map/ppermute | solution.py:26
  49.7 6.4 %collective-permute-start.26 = (bf16[4,32,256]{2,1,0:T(8,128)(2,1)S(1)}, bf16[4,32,256]{2,1,0:T(8,128)(2,1)S(1)}, u32[]{:S(2)}, u32[]{:S(2)}) collective-permute-start(bf16[4,32,256]{2,1,0:T(8,128)(2,1)S(1)} %add_convert_fusion.1), channel_id=1, source_target_pairs={{0,4},{4,0},{8,12},{12,8},{1,5},{5,1},{9,13},{13,9},{2,6},{6,2},{1... | collective-permute-start | bytes 196616 | tf_op jit(solution)/shard_map/ppermute | solution.py:26
  50.1 7.8 %collective-permute-start.11 = (bf16[5,32,256]{2,1,0:T(8,128)(2,1)S(1)}, bf16[5,32,256]{2,1,0:T(8,128)(2,1)S(1)}, u32[]{:S(2)}, u32[]{:S(2)}) collective-permute-start(bf16[5,32,256]{2,1,0:T(8,128)(2,1)S(1)} %fusion.18), channel_id=1, source_target_pairs={{0,8},{4,12},{8,0},{12,4},{1,9},{5,13},{9,1},{13,5},{2,10},{6,14},... | collective-permute-start | bytes 245768 | tf_op jit(solution)/shard_map/ppermute | solution.py:26
  53.1 6.0 %collective-permute-start.20 = (bf16[4,32,256]{2,1,0:T(8,128)(2,1)S(1)}, bf16[4,32,256]{2,1,0:T(8,128)(2,1)S(1)}, u32[]{:S(2)}, u32[]{:S(2)}) collective-permute-start(bf16[4,32,256]{2,1,0:T(8,128)(2,1)S(1)} %add_convert_fusion.2), channel_id=1, source_target_pairs={{0,4},{4,0},{8,12},{12,8},{1,5},{5,1},{9,13},{13,9},{2,6},{6,2},{1... | collective-permute-start | bytes 196616 | tf_op jit(solution)/shard_map/ppermute | solution.py:26
  53.3 5.8 %collective-permute-start.15 = (bf16[208,256]{1,0:T(8,128)(2,1)S(1)}, bf16[208,256]{1,0:T(8,128)(2,1)S(1)}, u32[]{:S(2)}, u32[]{:S(2)}) collective-permute-start(bf16[208,256]{1,0:T(8,128)(2,1)S(1)} %pad_maximum_fusion.6), channel_id=1, source_target_pairs={{0,8},{4,12},{8,0},{12,4},{1,9},{5,13},{9,1},{13,5},{2,10},{6,14},... | collective-permute-start | bytes 319496 | tf_op jit(solution)/shard_map/ppermute | solution.py:26
  56.1 7.5 %collective-permute-start.27 = (bf16[4,64,256]{2,1,0:T(8,128)(2,1)S(1)}, bf16[4,64,256]{2,1,0:T(8,128)(2,1)S(1)}, u32[]{:S(2)}, u32[]{:S(2)}) collective-permute-start(bf16[4,64,256]{2,1,0:T(8,128)(2,1)S(1)} %pad_maximum_fusion.4), channel_id=1, source_target_pairs={{0,2},{2,0},{1,3},{3,1},{4,6},{6,4},{5,7},{7,5},{8,10},{10,8},{9,1... | collective-permute-start | bytes 393224 | tf_op jit(solution)/shard_map/ppermute | solution.py:26
  58.0 5.4 %collective-permute-start.21 = (bf16[5,32,256]{2,1,0:T(8,128)(2,1)S(1)}, bf16[5,32,256]{2,1,0:T(8,128)(2,1)S(1)}, u32[]{:S(2)}, u32[]{:S(2)}) collective-permute-start(bf16[5,32,256]{2,1,0:T(8,128)(2,1)S(1)} %add_convert_fusion), channel_id=1, source_target_pairs={{0,4},{4,0},{8,12},{12,8},{1,5},{5,1},{9,13},{13,9},{2,6},{6,2},{1... | collective-permute-start | bytes 245768 | tf_op jit(solution)/shard_map/ppermute | solution.py:26
  60.3 4.8 %collective-permute-start.23 = (bf16[5,32,256]{2,1,0:T(8,128)(2,1)S(1)}, bf16[5,32,256]{2,1,0:T(8,128)(2,1)S(1)}, u32[]{:S(2)}, u32[]{:S(2)}) collective-permute-start(bf16[5,32,256]{2,1,0:T(8,128)(2,1)S(1)} %fusion.6), channel_id=1, source_target_pairs={{0,4},{4,0},{8,12},{12,8},{1,5},{5,1},{9,13},{13,9},{2,6},{6,2},{1... | collective-permute-start | bytes 245768 | tf_op jit(solution)/shard_map/ppermute | solution.py:26
  63.5 3.3 %collective-permute-start.22 = (bf16[9,64,256]{2,1,0:T(8,128)(2,1)S(1)}, bf16[9,64,256]{2,1,0:T(8,128)(2,1)S(1)}, u32[]{:S(2)}, u32[]{:S(2)}) collective-permute-start(bf16[9,64,256]{2,1,0:T(8,128)(2,1)S(1)} %maximum_maximum_fusion.1), channel_id=1, source_target_pairs={{0,2},{2,0},{1,3},{3,1},{4,6},{6,4},{5,7},{7,5},{8,10},{10,8},{9,1... | collective-permute-start | bytes 884744 | tf_op jit(solution)/shard_map/ppermute | solution.py:26
  65.2 1.5 %collective-permute-start.25 = (bf16[5,64,256]{2,1,0:T(8,128)(2,1)S(1)}, bf16[5,64,256]{2,1,0:T(8,128)(2,1)S(1)}, u32[]{:S(2)}, u32[]{:S(2)}) collective-permute-start(bf16[5,64,256]{2,1,0:T(8,128)(2,1)S(1)} %pad_maximum_fusion.3), channel_id=1, source_target_pairs={{0,2},{2,0},{1,3},{3,1},{4,6},{6,4},{5,7},{7,5},{8,10},{10,8},{9,1... | collective-permute-start | bytes 491528 | tf_op jit(solution)/shard_map/ppermute | solution.py:26
